TPU v7x, 32 devices: a whole 2x2x4 slice. The times are simulated.
32 devices in a mesh: groups: 2 (over x), space: 8 (over z, y), chan: 2 (over core).
Axes of the slice: x: 2, y: 2, z: 4, core: 2. Of those that a mesh axis runs over, the one named last changes fastest.
Arguments:
- inputs: float32 [128, 32, 2, 256], P('chan', ('groups', 'space')), parts along dimension 1, may hold values from -6 to 6
- weights: float32 [128, 27, 128], replicated, may hold values from -0.109375 to 0.109375
- out_grad: float32 [128, 32, 2, 256], P('chan', ('groups', 'space')), parts along dimension 1, may hold values from -6 to 6
Outputs:
- outputs: float32 [128, 32, 2, 256], P('chan', ('groups', 'space')), parts along dimension 1
- in_grad: float32 [128, 32, 2, 256], P('chan', ('groups', 'space')), parts along dimension 1
- filter_grad: float32 [128, 54, 128], P('chan', 'groups'), parts along dimension 1
There are 2 independent parts, one for each index of `groups`. A program takes and returns all parts, laid end to end along the dimension named above; an argument that names none is the same for every part. Nothing has to cross between parts.
All inputs are finite; a program needn't handle non-finite values.
Results may differ from a plain program's by a relative error of at most 0.0001.
Values sent between devices are 32-bit elements; how exact they have to be, the bound alone decides.
No kernel may reach another device: no remote copies, remote signals or barrier semaphores. Data moves between devices by JAX's collectives and lax.ppermute only.
A program may use at most 128 MiB of HBM per device.

v0:
```python
import jax
import jax.numpy as jnp
from jax import lax
from jax.experimental import pallas as pl
from jax.experimental.pallas import tpu as pltpu
from jax.sharding import PartitionSpec as P

F32 = jnp.float32
BF16 = jnp.bfloat16
VMEM = pl.BlockSpec(memory_space=pltpu.VMEM)
SMEM = pl.BlockSpec(memory_space=pltpu.SMEM)
NN = (((1,), (0,)), ((), ()))
NT = (((1,), (1,)), ((), ()))


def call(body, out_shape, n_in, scratch=()):
    return pl.pallas_call(
        body,
        out_shape=out_shape,
        in_specs=[SMEM] + [VMEM] * n_in,
        out_specs=jax.tree.map(lambda _: VMEM, out_shape),
        scratch_shapes=scratch,
        compiler_params=pltpu.CompilerParams(vmem_limit_bytes=40 << 20),
    )


def halves(value):
    high = value.astype(BF16)
    return high, (value - high.astype(F32)).astype(BF16)


def dot3(a_hi, a_lo, b_hi, b_lo, dims):
    def dot(a, b):
        return lax.dot_general(a, b, dims, preferred_element_type=F32)

    return dot(a_hi, b_hi) + (dot(a_hi, b_lo) + dot(a_lo, b_hi))


def moved(value, step):
    width = value.shape[-1]
    lane = lax.broadcasted_iota(jnp.int32, value.shape, value.ndim - 1)
    edge = 0 if step > 0 else width - 1
    return jnp.where(lane == edge, 0.0, pltpu.roll(value, step % width, value.ndim - 1))


def weight_kernel(at, w, a_hi, a_lo, b_hi, b_lo, turned):
    side, chan = at[1], at[2]
    sign = 1 - 2 * side
    half = a_hi.shape[1] // 6
    full = 2 * half
    own = pl.ds(pl.multiple_of(chan * half, half), half)
    for first in range(3):
        for second in range(3):
            for third in range(3):
                tap = 9 * first + 3 * second + third
                turned[...] = w[tap].T
                fwd = halves(w[tap, own, :])
                back = halves(turned[own, :])
                fwd_at = 1 + (first - 1) * sign
                back_at = 1 - (first - 1) * sign
                for low in range(2):
                    up = low + second - 1
                    if up < 0 or up > 1:
                        continue
                    row = (low * 3 + third) * half
                    a_hi[fwd_at, row : row + half, up * full : up * full + full] = fwd[0]
                    a_lo[fwd_at, row : row + half, up * full : up * full + full] = fwd[1]
                    row = (up * 3 + 2 - third) * half
                    b_hi[back_at, row : row + half, low * full : low * full + full] = back[0]
                    b_lo[back_at, row : row + half, low * full : low * full + full] = back[1]


def put_slab(hi, lo, chan, own, other):
    half = own.shape[1]
    for z in range(2):
        for piece, place in ((own, chan), (other, 1 - chan)):
            rows = pl.ds(pl.multiple_of((2 * z + place) * half, half), half)
            hi[rows, :], lo[rows, :] = halves(piece[z])


def conv_kernel(at, halo, halo2, own, own2, pair, pair2, w_hi, w_lo, out, x_hi, x_lo):
    side, chan = at[1], at[2]
    half = own.shape[2]
    put_slab(x_hi.at[0], x_lo.at[0], chan, halo, halo2)
    put_slab(x_hi.at[1], x_lo.at[1], chan, own.at[side], own2.at[side])
    put_slab(x_hi.at[2], x_lo.at[2], chan, own.at[1 - side], own2.at[1 - side])
    put_slab(x_hi.at[3], x_lo.at[3], chan, pair.at[side], pair2.at[side])
    for t in range(2):
        total = jnp.zeros((6 * half, own.shape[3]), F32)
        for d in range(3):
            total = total + dot3(w_hi[d], w_lo[d], x_hi[t + d], x_lo[t + d], NN)
        slab = side if t == 0 else 1 - side
        for z in range(2):
            low, mid, high = (
                total[(3 * z + c) * half : (3 * z + c + 1) * half, :] for c in range(3)
            )
            out[slab, z] = mid + moved(low, 1) + moved(high, -1)


def filter_kernel(at, own, own2, pair, pair2, edge, edge2, g_own, g_pair, *rest):
    count = len(rest) - 7
    outs = rest[:count]
    x_hi, x_lo, g_hi, g_lo, acc1, acc0, flat = rest[count:]
    z_at, side, chan = at[0], at[1], at[2]
    half = own.shape[2]
    part = half // 2
    slabs = (
        (own.at[side], own2.at[side]),
        (own.at[1 - side], own2.at[1 - side]),
        (pair.at[side], pair2.at[side]),
        (pair.at[1 - side], pair2.at[1 - side]),
        (edge, edge2),
    )
    grads = (g_own.at[side], g_own.at[1 - side], g_pair.at[side], g_pair.at[1 - side])
    for t in range(5):
        put_slab(x_hi.at[t], x_lo.at[t], chan, *slabs[t])
    for t in range(4):
        for z in range(2):
            value = grads[t][z]
            for c, shifted in enumerate((moved(value, -1), value, moved(value, 1))):
                row = (3 * z + c) * half
                g_hi[t, row : row + half, :], g_lo[t, row : row + half, :] = halves(shifted)
    total = None
    for t in range(4):
        term = dot3(g_hi[t], g_lo[t], x_hi[t + 1], x_lo[t + 1], NT)
        total = term if total is None else total + term
    acc1[...] = total

    def some(ref, t):
        pieces = [
            ref[t, pl.ds(pl.multiple_of(k * half + side * part, part), part), :] for k in range(6)
        ]
        return jnp.concatenate(pieces, axis=0)

    total = None
    for t in range(4):
        term = dot3(some(g_hi, t), some(g_lo, t), x_hi[t], x_lo[t], NT)
        total = term if total is None else total + term
    acc0[...] = total

    tiles = flat.shape[0]
    place = 0
    for acc, size in ((acc1, half), (acc0, part)):
        full = 2 * half
        for b in range(3):
            for c in range(3):
                lower = acc[c * size : (c + 1) * size, :]
                upper = acc[(3 + c) * size : (4 + c) * size, :]
                if b == 0:
                    value = upper[:, :full]
                elif b == 1:
                    value = lower[:, :full] + upper[:, full:]
                else:
                    value = lower[:, full:]
                flat[place : place + size // 8] = value.reshape(size // 8, 8, full)
                place += size // 8
    if place < tiles:
        flat[place:] = jnp.zeros((tiles - place, 8, 2 * half), F32)
    each = tiles // count
    for k in range(count):
        outs[k][...] = flat[pl.ds(lax.rem(z_at + k, count) * each, each)]


def sum_kernel(scale, at, *refs):
    total = refs[0][...]
    for ref in refs[1:-1]:
        total = total + ref[...]
    refs[-1][...] = total * scale


def join_kernel(at, *refs):
    count = (len(refs) - 3) // 2
    mine, theirs = refs[:count], refs[count : 2 * count]
    out, flat, flat2 = refs[2 * count :]
    z_at, side = at[0], at[1]
    each = mine[0].shape[0]
    for k in range(count):
        here = pl.ds(lax.rem(z_at + count - k, count) * each, each)
        flat[here] = mine[k][...]
        flat2[here] = theirs[k][...]
    rows = out.shape[1]
    for source, which in ((flat, side), (flat2, 1 - side)):
        first = source[: 9 * rows].reshape(9, rows, 8, out.shape[3])
        out[pl.ds((1 - which) * 18, 9)] = first
        rest = source[9 * rows : 9 * rows + 9 * rows // 2]
        out[9:18, pl.ds(which * (rows // 2), rows // 2)] = rest.reshape(
            9, rows // 2, 8, out.shape[3]
        )


def local(inputs, weights, out_grad):
    half, _, _, width = inputs.shape
    full = 2 * half
    ring = lax.axis_size("space")
    count = ring // 2
    here = lax.axis_index("space")
    z_at, side, chan = here // 2, here % 2, lax.axis_index("chan")
    at = jnp.stack([z_at, side, chan]).astype(jnp.int32)

    def swap_chan(value):
        return lax.ppermute(value, "chan", [(0, 1), (1, 0)])

    def swap_side(value):
        return lax.ppermute(value, "space", [(i, i ^ 1) for i in range(ring)])

    def shift(value, step):
        pairs = [(2 * z + y, 2 * ((z + step) % count) + y) for z in range(count) for y in range(2)]
        return lax.ppermute(value, "space", pairs)

    def outward(value):
        pairs = []
        for z in range(count):
            if z > 0:
                pairs.append((2 * z, 2 * z - 2))
            if z + 1 < count:
                pairs.append((2 * z + 1, 2 * z + 3))
        return lax.ppermute(value, "space", pairs)

    x_own = inputs.transpose(1, 2, 0, 3)
    x_pair = swap_side(x_own)
    g_own = out_grad.transpose(1, 2, 0, 3)
    g_pair = swap_side(g_own)
    x_edge = outward(lax.dynamic_index_in_dim(x_own, side, 0, keepdims=False))
    g_edge = outward(lax.dynamic_index_in_dim(g_own, side, 0, keepdims=False))
    x_own2 = swap_chan(x_own)
    x_pair2 = swap_chan(x_pair)
    x_edge2 = swap_chan(x_edge)

    w_taps = weights.transpose(1, 0, 2)
    block = jax.ShapeDtypeStruct((3, 6 * half, 2 * full), BF16)
    a_hi, a_lo, b_hi, b_lo = call(
        weight_kernel, [block] * 4, 1, [pltpu.VMEM((full, full), F32)]
    )(at, w_taps)

    tiles = 9 * (half + half // 2) // 8
    each = -(-tiles // count)
    chunk = jax.ShapeDtypeStruct((each, 8, full), F32)
    parts = call(
        filter_kernel,
        [chunk] * count,
        8,
        [
            pltpu.VMEM((5, 2 * full, width), BF16),
            pltpu.VMEM((5, 2 * full, width), BF16),
            pltpu.VMEM((4, 6 * half, width), BF16),
            pltpu.VMEM((4, 6 * half, width), BF16),
            pltpu.VMEM((6 * half, 2 * full), F32),
            pltpu.VMEM((3 * half, 2 * full), F32),
            pltpu.VMEM((each * count, 8, full), F32),
        ],
    )(at, x_own, x_own2, x_pair, x_pair2, x_edge, x_edge2, g_own, g_pair)

    got = [parts[0]] + [shift(parts[k], k) for k in range(1, count)]

    x_halo = swap_side(x_edge)
    g_halo = swap_side(g_edge)
    x_halo2 = swap_chan(x_halo)
    g_halo2 = swap_chan(g_halo)
    g_own2 = swap_chan(g_own)
    g_pair2 = swap_chan(g_pair)
    conv = call(
        conv_kernel,
        jax.ShapeDtypeStruct((2, 2, half, width), F32),
        8,
        [pltpu.VMEM((4, 2 * full, width), BF16)] * 2,
    )
    outputs = conv(at, x_halo, x_halo2, x_own, x_own2, x_pair, x_pair2, a_hi, a_lo)
    in_grad = conv(at, g_halo, g_halo2, g_own, g_own2, g_pair, g_pair2, b_hi, b_lo)

    cells = inputs.shape[1] * ring * inputs.shape[2] * width
    scale = float(1.0 / cells**0.5)
    shard = call(lambda *refs: sum_kernel(scale, *refs), chunk, count)(at, *got)
    mine = [shard] + [shift(shard, k) for k in range(1, count)]
    theirs = [swap_side(value) for value in mine]
    joined = call(
        join_kernel,
        jax.ShapeDtypeStruct((27, half // 8, 8, full), F32),
        2 * count,
        [pltpu.VMEM((each * count, 8, full), F32)] * 2,
    )(at, *mine, *theirs)
    filter_grad = joined.reshape(27, half, full).transpose(1, 0, 2)
    return (
        outputs.transpose(2, 0, 1, 3),
        in_grad.transpose(2, 0, 1, 3),
        filter_grad,
    )


def solution(mesh):
    in_specs = (
        P("chan", ("groups", "space"), None, None),
        P(),
        P("chan", ("groups", "space"), None, None),
    )
    out_specs = (
        P("chan", ("groups", "space"), None, None),
        P("chan", ("groups", "space"), None, None),
        P("chan", "groups", None),
    )
    return jax.shard_map(local, mesh=mesh, in_specs=in_specs, out_specs=out_specs, check_vma=False)
```

profile of v0, /device:TPU:0, one launch (start us, length us, event | category | flops | bytes accessed | tf_op | source)
XLA Modules:
  0.0 60.8 jit_solution(11724682262565761149)
XLA Ops:
  0.6 1.0 %copy.17 = f32[64,2,2,256]{3,0,2,1:T(8,128)S(1)} copy(f32[64,2,2,256]{3,2,1,0:T(2,128)} %param.3) | data formatting | bytes 524288 | tf_op args[0]
  1.6 3.0 %collective-permute-start.4 = (f32[2,2,64,256]{3,2,1,0:T(8,128)S(1)}, f32[2,2,64,256]{3,2,1,0:T(8,128)S(1)}, u32[]{:S(2)}, u32[]{:S(2)}) collective-permute-start(f32[2,2,64,256]{3,2,1,0:T(8,128)S(1)} %bitcast.27), channel_id=1, source_target_pairs={{0,2},{2,0},{4,6},{6,4},{8,10},{10,8},{12,14},{14,12},{1,3},{3,1},... | collective-permute-start | bytes 786440 | tf_op jit(solution)/shard_map/ppermute | solution.py:204
  4.7 1.0 %copy.16 = f32[64,2,2,256]{3,0,2,1:T(8,128)S(1)} copy(f32[64,2,2,256]{3,2,1,0:T(2,128)} %param.5) | data formatting | bytes 524288 | tf_op args[2]
  6.0 1.3 %collective-permute-start = (f32[2,64,256]{2,1,0:T(8,128)S(1)}, f32[2,64,256]{2,1,0:T(8,128)S(1)}, u32[]{:S(2)}, u32[]{:S(2)}) collective-permute-start(f32[2,64,256]{2,1,0:T(8,128)S(1)} %dynamic-slice_bitcast_fusion.1), channel_id=1, source_target_pairs={{2,6},{4,0},{6,10},{8,4},{10,14},{12,8},{3,7},{5,1},{7,11},{9,5},{... | collective-permute-start | bytes 393224 | tf_op jit(solution)/shard_map/ppermute | solution.py:217
  7.3 4.6 %collective-permute-done.4.pair = f32[2,2,64,256]{3,2,1,0:T(8,128)S(1)} collective-permute-done((f32[2,2,64,256]{3,2,1,0:T(8,128)S(1)}, f32[2,2,64,256]{3,2,1,0:T(8,128)S(1)}, u32[]{:S(2)}, u32[]{:S(2)}) %collective-permute-start.4) | collective-permute-done | bytes 262176 | tf_op jit(solution)/shard_map/ppermute | solution.py:204
  12.5 1.3 %collective-permute-start.6 = (f32[2,64,256]{2,1,0:T(8,128)}, f32[2,64,256]{2,1,0:T(8,128)}, u32[]{:S(2)}, u32[]{:S(2)}) collective-permute-start(f32[2,64,256]{2,1,0:T(8,128)} %dynamic-slice_bitcast_fusion), channel_id=1, source_target_pairs={{2,6},{4,0},{6,10},{8,4},{10,14},{12,8},{3,7},{5,1},{7,11},{9,5},{... | collective-permute-start | bytes 393224 | tf_op jit(solution)/shard_map/ppermute | solution.py:217
  14.4 6.6 %collective-permute-done.6 = f32[2,64,256]{2,1,0:T(8,128)} collective-permute-done((f32[2,64,256]{2,1,0:T(8,128)}, f32[2,64,256]{2,1,0:T(8,128)}, u32[]{:S(2)}, u32[]{:S(2)}) %collective-permute-start.6) | collective-permute-done | bytes 131104 | tf_op jit(solution)/shard_map/ppermute | solution.py:217
  21.8 1.3 %collective-permute-start.7 = (f32[2,64,256]{2,1,0:T(8,128)}, f32[2,64,256]{2,1,0:T(8,128)S(1)}, u32[]{:S(2)}, u32[]{:S(2)}) collective-permute-start(f32[2,64,256]{2,1,0:T(8,128)} %collective-permute-done.6), channel_id=1, source_target_pairs={{0,2},{2,0},{4,6},{6,4},{8,10},{10,8},{12,14},{14,12},{1,3},{3,1},... | collective-permute-start | bytes 393224 | tf_op jit(solution)/shard_map/ppermute | solution.py:204
  23.1 2.5 %shard_map.61 = (f32[27,8,128]{2,1,0:T(8,128)S(1)}, f32[27,8,128]{2,1,0:T(8,128)S(1)}, f32[27,8,128]{2,1,0:T(8,128)S(1)}, f32[27,8,128]{2,1,0:T(8,128)S(1)}) custom-call(s32[3]{0:T(128)S(1)} %pad_add_fusion.at.refs_0_, f32[2,2,64,256]{3,2,1,0:T(8,128)S(1)} %bitcast.29, f32[2,2,64,256]{3,2,1,0:T(8,128)S(1)} %collective-permute-done.3.own2, ...), custom_call_target="tpu_custom_call" | custom-call | tf_op jit(solution)/shard_map/pallas_call | solution.py:238
  25.6 1.8 %collective-permute-start.13 = (f32[27,8,128]{2,1,0:T(8,128)S(1)}, f32[27,8,128]{2,1,0:T(8,128)S(1)}, u32[]{:S(2)}, u32[]{:S(2)}) collective-permute-start(f32[27,8,128]{2,1,0:T(8,128)S(1)} %get-tuple-element.16), channel_id=1, source_target_pairs={{0,4},{2,6},{4,8},{6,10},{8,12},{10,14},{12,0},{14,2},{1,5},{3,7},... | collective-permute-start | bytes 331784 | tf_op jit(solution)/shard_map/ppermute | solution.py:208
  27.3 2.2 %collective-permute-start.14 = (f32[27,8,128]{2,1,0:T(8,128)S(1)}, f32[27,8,128]{2,1,0:T(8,128)S(1)}, u32[]{:S(2)}, u32[]{:S(2)}) collective-permute-start(f32[27,8,128]{2,1,0:T(8,128)S(1)} %get-tuple-element.17), channel_id=1, source_target_pairs={{0,8},{2,10},{4,12},{6,14},{8,0},{10,2},{12,4},{14,6},{1,9},{3,11}... | collective-permute-start | bytes 331784 | tf_op jit(solution)/shard_map/ppermute | solution.py:208
  29.7 3.5 %collective-permute-start.15 = (f32[27,8,128]{2,1,0:T(8,128)S(1)}, f32[27,8,128]{2,1,0:T(8,128)S(1)}, u32[]{:S(2)}, u32[]{:S(2)}) collective-permute-start(f32[27,8,128]{2,1,0:T(8,128)S(1)} %get-tuple-element.18), channel_id=1, source_target_pairs={{0,12},{2,14},{4,0},{6,2},{8,4},{10,6},{12,8},{14,10},{1,13},{3,15... | collective-permute-start | bytes 331784 | tf_op jit(solution)/shard_map/ppermute | solution.py:208
  33.4 3.9 %collective-permute-done.14.refs_3_ = f32[27,8,128]{2,1,0:T(8,128)S(1)} collective-permute-done((f32[27,8,128]{2,1,0:T(8,128)S(1)}, f32[27,8,128]{2,1,0:T(8,128)S(1)}, u32[]{:S(2)}, u32[]{:S(2)}) %collective-permute-start.14) | collective-permute-done | bytes 110624 | tf_op jit(solution)/shard_map/ppermute | solution.py:208
  38.2 2.5 %collective-permute-start.16 = (f32[27,8,128]{2,1,0:T(8,128)S(1)}, f32[27,8,128]{2,1,0:T(8,128)S(1)}, u32[]{:S(2)}, u32[]{:S(2)}) collective-permute-start(f32[27,8,128]{2,1,0:T(8,128)S(1)} %shard_map.62.refs_0_), channel_id=1, source_target_pairs={{0,4},{2,6},{4,8},{6,10},{8,12},{10,14},{12,0},{14,2},{1,5},{3,7},... | collective-permute-start | bytes 331784 | tf_op jit(solution)/shard_map/ppermute | solution.py:208
  40.7 1.7 %collective-permute-start.17 = (f32[27,8,128]{2,1,0:T(8,128)S(1)}, f32[27,8,128]{2,1,0:T(8,128)S(1)}, u32[]{:S(2)}, u32[]{:S(2)}) collective-permute-start(f32[27,8,128]{2,1,0:T(8,128)S(1)} %shard_map.62.refs_0_), channel_id=1, source_target_pairs={{0,8},{2,10},{4,12},{6,14},{8,0},{10,2},{12,4},{14,6},{1,9},{3,11}... | collective-permute-start | bytes 331784 | tf_op jit(solution)/shard_map/ppermute | solution.py:208
  43.2 1.7 %collective-permute-start.19 = (f32[27,8,128]{2,1,0:T(8,128)S(1)}, f32[27,8,128]{2,1,0:T(8,128)S(1)}, u32[]{:S(2)}, u32[]{:S(2)}) collective-permute-start(f32[27,8,128]{2,1,0:T(8,128)S(1)} %shard_map.62.refs_0_), channel_id=1, source_target_pairs={{0,2},{2,0},{4,6},{6,4},{8,10},{10,8},{12,14},{14,12},{1,3},{3,1},... | collective-permute-start | bytes 331784 | tf_op jit(solution)/shard_map/ppermute | solution.py:204
  44.9 1.1 %collective-permute-done.16.refs_1_ = f32[27,8,128]{2,1,0:T(8,128)S(1)} collective-permute-done((f32[27,8,128]{2,1,0:T(8,128)S(1)}, f32[27,8,128]{2,1,0:T(8,128)S(1)}, u32[]{:S(2)}, u32[]{:S(2)}) %collective-permute-start.16) | collective-permute-done | bytes 110624 | tf_op jit(solution)/shard_map/ppermute | solution.py:208
  46.0 1.7 %collective-permute-start.20 = (f32[27,8,128]{2,1,0:T(8,128)S(1)}, f32[27,8,128]{2,1,0:T(8,128)S(1)}, u32[]{:S(2)}, u32[]{:S(2)}) collective-permute-start(f32[27,8,128]{2,1,0:T(8,128)S(1)} %collective-permute-done.16.refs_1_), channel_id=1, source_target_pairs={{0,2},{2,0},{4,6},{6,4},{8,10},{10,8},{12,14},{14,12},{1,3},{3,1},... | collective-permute-start | bytes 331784 | tf_op jit(solution)/shard_map/ppermute | solution.py:204
  47.7 2.7 %collective-permute-done.17.refs_2_ = f32[27,8,128]{2,1,0:T(8,128)S(1)} collective-permute-done((f32[27,8,128]{2,1,0:T(8,128)S(1)}, f32[27,8,128]{2,1,0:T(8,128)S(1)}, u32[]{:S(2)}, u32[]{:S(2)}) %collective-permute-start.17) | collective-permute-done | bytes 110624 | tf_op jit(solution)/shard_map/ppermute | solution.py:208
  50.5 1.5 %collective-permute-start.21 = (f32[27,8,128]{2,1,0:T(8,128)S(1)}, f32[27,8,128]{2,1,0:T(8,128)S(1)}, u32[]{:S(2)}, u32[]{:S(2)}) collective-permute-start(f32[27,8,128]{2,1,0:T(8,128)S(1)} %collective-permute-done.17.refs_2_), channel_id=1, source_target_pairs={{0,2},{2,0},{4,6},{6,4},{8,10},{10,8},{12,14},{14,12},{1,3},{3,1},... | collective-permute-start | bytes 331784 | tf_op jit(solution)/shard_map/ppermute | solution.py:204
  52.5 1.2 %shard_map.58 = (bf16[3,384,256]{2,1,0:T(8,128)(2,1)S(1)}, bf16[3,384,256]{2,1,0:T(8,128)(2,1)S(1)}, bf16[3,384,256]{2,1,0:T(8,128)(2,1)S(1)}, bf16[3,384,256]{2,1,0:T(8,128)(2,1)S(1)}) custom-call(s32[3]{0:T(128)S(1)} %pad_add_fusion.at.refs_0_, f32[27,128,128]{2,1,0:T(8,128)S(1)} %bitcast.31), custom_call_target="tpu_custom_call" | custom-call | tf_op jit(solution)/shard_map/pallas_call | solution.py:231
  53.7 1.8 %shard_map.59 = f32[2,2,64,256]{3,2,1,0:T(8,128)S(1)} custom-call(s32[3]{0:T(128)S(1)} %pad_add_fusion.at.refs_0_, f32[2,64,256]{2,1,0:T(8,128)S(1)} %collective-permute-done.1.halo, f32[2,64,256]{2,1,0:T(8,128)S(1)} %collective-permute-done.2.halo2, f32[2,2,64,256]{3,2,1,0:T(8,128)S(1)} %bitcast.30, f32[2,2,64,256]{3,2,1,0:T(8,128)S(1)} %collective-permute-done.3.own2, ...), custom_call_target="tpu_custom_call" | custom-call | tf_op jit(solution)/shard_map/pallas_call | solution.py:267
  56.4 1.8 %shard_map.60 = f32[2,2,64,256]{3,2,1,0:T(8,128)S(1)} custom-call(s32[3]{0:T(128)S(1)} %pad_add_fusion.at.refs_0_, f32[2,64,256]{2,1,0:T(8,128)S(1)} %collective-permute-done.7.halo, f32[2,64,256]{2,1,0:T(8,128)S(1)} %collective-permute-done.8.halo2, f32[2,2,64,256]{3,2,1,0:T(8,128)S(1)} %bitcast.26, f32[2,2,64,256]{3,2,1,0:T(8,128)S(1)} %collective-permute-done.9.own2, ...), custom_call_target="tpu_custom_call" | custom-call | tf_op jit(solution)/shard_map/pallas_call | solution.py:268
  59.2 1.6 %shard_map.63 = f32[27,8,8,128]{3,2,1,0:T(8,128)} custom-call(s32[3]{0:T(128)S(1)} %pad_add_fusion.at.refs_0_, f32[27,8,128]{2,1,0:T(8,128)S(1)} %shard_map.62.refs_0_, f32[27,8,128]{2,1,0:T(8,128)S(1)} %collective-permute-done.16.refs_1_, f32[27,8,128]{2,1,0:T(8,128)S(1)} %collective-permute-done.17.refs_2_, ...), custom_call_target="tpu_custom_call" | custom-call | tf_op jit(solution)/shard_map/pallas_call | solution.py:275
  (37 shorter events, 6.7 us)
Async XLA Ops:
  1.6 50.9 %copy-start = (f32[128,27,128]{2,0,1:T(8,128)S(1)}, f32[128,27,128]{2,0,1:T(8,128)}, u32[]{:S(2)}) copy-start(f32[128,27,128]{2,0,1:T(8,128)} %param.4) | copy-start | bytes 5308420
  1.6 10.2 %collective-permute-start.4 = (f32[2,2,64,256]{3,2,1,0:T(8,128)S(1)}, f32[2,2,64,256]{3,2,1,0:T(8,128)S(1)}, u32[]{:S(2)}, u32[]{:S(2)}) collective-permute-start(f32[2,2,64,256]{3,2,1,0:T(8,128)S(1)} %bitcast.27), channel_id=1, source_target_pairs={{0,2},{2,0},{4,6},{6,4},{8,10},{10,8},{12,14},{14,12},{1,3},{3,1},... | collective-permute-start | bytes 786440 | tf_op jit(solution)/shard_map/ppermute | solution.py:204
  4.7 16.3 %collective-permute-start.3 = (f32[2,2,64,256]{3,2,1,0:T(8,128)S(1)}, f32[2,2,64,256]{3,2,1,0:T(8,128)S(1)}, u32[]{:S(2)}, u32[]{:S(2)}) collective-permute-start(f32[2,2,64,256]{3,2,1,0:T(8,128)S(1)} %bitcast.28), channel_id=1, source_target_pairs={{0,1},{1,0},{2,3},{3,2},{4,5},{5,4},{6,7},{7,6},{8,9},{9,8},{10,11... | collective-permute-start | bytes 786440 | tf_op jit(solution)/shard_map/ppermute | solution.py:201
  5.7 16.1 %collective-permute-start.10 = (f32[2,2,64,256]{3,2,1,0:T(8,128)S(1)}, f32[2,2,64,256]{3,2,1,0:T(8,128)S(1)}, u32[]{:S(2)}, u32[]{:S(2)}) collective-permute-start(f32[2,2,64,256]{3,2,1,0:T(8,128)S(1)} %bitcast.23), channel_id=1, source_target_pairs={{0,2},{2,0},{4,6},{6,4},{8,10},{10,8},{12,14},{14,12},{1,3},{3,1},... | collective-permute-start | bytes 786440 | tf_op jit(solution)/shard_map/ppermute | solution.py:204
  6.0 7.8 %collective-permute-start = (f32[2,64,256]{2,1,0:T(8,128)S(1)}, f32[2,64,256]{2,1,0:T(8,128)S(1)}, u32[]{:S(2)}, u32[]{:S(2)}) collective-permute-start(f32[2,64,256]{2,1,0:T(8,128)S(1)} %dynamic-slice_bitcast_fusion.1), channel_id=1, source_target_pairs={{2,6},{4,0},{6,10},{8,4},{10,14},{12,8},{3,7},{5,1},{7,11},{9,5},{... | collective-permute-start | bytes 393224 | tf_op jit(solution)/shard_map/ppermute | solution.py:217
  11.8 11.3 %collective-permute-start.5 = (f32[2,2,64,256]{3,2,1,0:T(8,128)S(1)}, f32[2,2,64,256]{3,2,1,0:T(8,128)S(1)}, u32[]{:S(2)}, u32[]{:S(2)}) collective-permute-start(f32[2,2,64,256]{3,2,1,0:T(8,128)S(1)} %collective-permute-done.4.pair), channel_id=1, source_target_pairs={{0,1},{1,0},{2,3},{3,2},{4,5},{5,4},{6,7},{7,6},{8,9},{9,8},{10,11... | collective-permute-start | bytes 786440 | tf_op jit(solution)/shard_map/ppermute | solution.py:201
  12.5 8.5 %collective-permute-start.6 = (f32[2,64,256]{2,1,0:T(8,128)}, f32[2,64,256]{2,1,0:T(8,128)}, u32[]{:S(2)}, u32[]{:S(2)}) collective-permute-start(f32[2,64,256]{2,1,0:T(8,128)} %dynamic-slice_bitcast_fusion), channel_id=1, source_target_pairs={{2,6},{4,0},{6,10},{8,4},{10,14},{12,8},{3,7},{5,1},{7,11},{9,5},{... | collective-permute-start | bytes 393224 | tf_op jit(solution)/shard_map/ppermute | solution.py:217
  13.8 9.3 %collective-permute-start.12 = (f32[2,64,256]{2,1,0:T(8,128)S(1)}, f32[2,64,256]{2,1,0:T(8,128)}, u32[]{:S(2)}, u32[]{:S(2)}) collective-permute-start(f32[2,64,256]{2,1,0:T(8,128)S(1)} %collective-permute-done.edge), channel_id=1, source_target_pairs={{0,1},{1,0},{2,3},{3,2},{4,5},{5,4},{6,7},{7,6},{8,9},{9,8},{10,11... | collective-permute-start | bytes 393224 | tf_op jit(solution)/shard_map/ppermute | solution.py:201
  21.0 19.8 %collective-permute-start.9 = (f32[2,2,64,256]{3,2,1,0:T(8,128)S(1)}, f32[2,2,64,256]{3,2,1,0:T(8,128)S(1)}, u32[]{:S(2)}, u32[]{:S(2)}) collective-permute-start(f32[2,2,64,256]{3,2,1,0:T(8,128)S(1)} %bitcast.24), channel_id=1, source_target_pairs={{0,1},{1,0},{2,3},{3,2},{4,5},{5,4},{6,7},{7,6},{8,9},{9,8},{10,11... | collective-permute-start | bytes 786440 | tf_op jit(solution)/shard_map/ppermute | solution.py:201
  21.0 8.5 %collective-permute-start.1 = (f32[2,64,256]{2,1,0:T(8,128)S(1)}, f32[2,64,256]{2,1,0:T(8,128)S(1)}, u32[]{:S(2)}, u32[]{:S(2)}) collective-permute-start(f32[2,64,256]{2,1,0:T(8,128)S(1)} %collective-permute-done.edge), channel_id=1, source_target_pairs={{0,2},{2,0},{4,6},{6,4},{8,10},{10,8},{12,14},{14,12},{1,3},{3,1},... | collective-permute-start | bytes 393224 | tf_op jit(solution)/shard_map/ppermute | solution.py:204
  21.8 7.9 %collective-permute-start.7 = (f32[2,64,256]{2,1,0:T(8,128)}, f32[2,64,256]{2,1,0:T(8,128)S(1)}, u32[]{:S(2)}, u32[]{:S(2)}) collective-permute-start(f32[2,64,256]{2,1,0:T(8,128)} %collective-permute-done.6), channel_id=1, source_target_pairs={{0,2},{2,0},{4,6},{6,4},{8,10},{10,8},{12,14},{14,12},{1,3},{3,1},... | collective-permute-start | bytes 393224 | tf_op jit(solution)/shard_map/ppermute | solution.py:204
  25.6 7.8 %collective-permute-start.13 = (f32[27,8,128]{2,1,0:T(8,128)S(1)}, f32[27,8,128]{2,1,0:T(8,128)S(1)}, u32[]{:S(2)}, u32[]{:S(2)}) collective-permute-start(f32[27,8,128]{2,1,0:T(8,128)S(1)} %get-tuple-element.16), channel_id=1, source_target_pairs={{0,4},{2,6},{4,8},{6,10},{8,12},{10,14},{12,0},{14,2},{1,5},{3,7},... | collective-permute-start | bytes 331784 | tf_op jit(solution)/shard_map/ppermute | solution.py:208
  27.3 9.9 %collective-permute-start.14 = (f32[27,8,128]{2,1,0:T(8,128)S(1)}, f32[27,8,128]{2,1,0:T(8,128)S(1)}, u32[]{:S(2)}, u32[]{:S(2)}) collective-permute-start(f32[27,8,128]{2,1,0:T(8,128)S(1)} %get-tuple-element.17), channel_id=1, source_target_pairs={{0,8},{2,10},{4,12},{6,14},{8,0},{10,2},{12,4},{14,6},{1,9},{3,11}... | collective-permute-start | bytes 331784 | tf_op jit(solution)/shard_map/ppermute | solution.py:208
  29.5 13.0 %collective-permute-start.2 = (f32[2,64,256]{2,1,0:T(8,128)S(1)}, f32[2,64,256]{2,1,0:T(8,128)S(1)}, u32[]{:S(2)}, u32[]{:S(2)}) collective-permute-start(f32[2,64,256]{2,1,0:T(8,128)S(1)} %collective-permute-done.1.halo), channel_id=1, source_target_pairs={{0,1},{1,0},{2,3},{3,2},{4,5},{5,4},{6,7},{7,6},{8,9},{9,8},{10,11... | collective-permute-start | bytes 393224 | tf_op jit(solution)/shard_map/ppermute | solution.py:201
  29.7 7.9 %collective-permute-start.15 = (f32[27,8,128]{2,1,0:T(8,128)S(1)}, f32[27,8,128]{2,1,0:T(8,128)S(1)}, u32[]{:S(2)}, u32[]{:S(2)}) collective-permute-start(f32[27,8,128]{2,1,0:T(8,128)S(1)} %get-tuple-element.18), channel_id=1, source_target_pairs={{0,12},{2,14},{4,0},{6,2},{8,4},{10,6},{12,8},{14,10},{1,13},{3,15... | collective-permute-start | bytes 331784 | tf_op jit(solution)/shard_map/ppermute | solution.py:208
  33.4 23.1 %collective-permute-start.11 = (f32[2,2,64,256]{3,2,1,0:T(8,128)S(1)}, f32[2,2,64,256]{3,2,1,0:T(8,128)S(1)}, u32[]{:S(2)}, u32[]{:S(2)}) collective-permute-start(f32[2,2,64,256]{3,2,1,0:T(8,128)S(1)} %collective-permute-done.10.pair.g_pair), channel_id=1, source_target_pairs={{0,1},{1,0},{2,3},{3,2},{4,5},{5,4},{6,7},{7,6},{8,9},{9,8},{10,11... | collective-permute-start | bytes 786440 | tf_op jit(solution)/shard_map/ppermute | solution.py:201
  37.3 5.9 %collective-permute-start.8 = (f32[2,64,256]{2,1,0:T(8,128)S(1)}, f32[2,64,256]{2,1,0:T(8,128)S(1)}, u32[]{:S(2)}, u32[]{:S(2)}) collective-permute-start(f32[2,64,256]{2,1,0:T(8,128)S(1)} %collective-permute-done.7.halo), channel_id=1, source_target_pairs={{0,1},{1,0},{2,3},{3,2},{4,5},{5,4},{6,7},{7,6},{8,9},{9,8},{10,11... | collective-permute-start | bytes 393224 | tf_op jit(solution)/shard_map/ppermute | solution.py:201
  38.2 7.8 %collective-permute-start.16 = (f32[27,8,128]{2,1,0:T(8,128)S(1)}, f32[27,8,128]{2,1,0:T(8,128)S(1)}, u32[]{:S(2)}, u32[]{:S(2)}) collective-permute-start(f32[27,8,128]{2,1,0:T(8,128)S(1)} %shard_map.62.refs_0_), channel_id=1, source_target_pairs={{0,4},{2,6},{4,8},{6,10},{8,12},{10,14},{12,0},{14,2},{1,5},{3,7},... | collective-permute-start | bytes 331784 | tf_op jit(solution)/shard_map/ppermute | solution.py:208
  40.7 9.7 %collective-permute-start.17 = (f32[27,8,128]{2,1,0:T(8,128)S(1)}, f32[27,8,128]{2,1,0:T(8,128)S(1)}, u32[]{:S(2)}, u32[]{:S(2)}) collective-permute-start(f32[27,8,128]{2,1,0:T(8,128)S(1)} %shard_map.62.refs_0_), channel_id=1, source_target_pairs={{0,8},{2,10},{4,12},{6,14},{8,0},{10,2},{12,4},{14,6},{1,9},{3,11}... | collective-permute-start | bytes 331784 | tf_op jit(solution)/shard_map/ppermute | solution.py:208
  42.5 9.5 %collective-permute-start.18 = (f32[27,8,128]{2,1,0:T(8,128)S(1)}, f32[27,8,128]{2,1,0:T(8,128)S(1)}, u32[]{:S(2)}, u32[]{:S(2)}) collective-permute-start(f32[27,8,128]{2,1,0:T(8,128)S(1)} %shard_map.62.refs_0_), channel_id=1, source_target_pairs={{0,12},{2,14},{4,0},{6,2},{8,4},{10,6},{12,8},{14,10},{1,13},{3,15... | collective-permute-start | bytes 331784 | tf_op jit(solution)/shard_map/ppermute | solution.py:208
  43.2 16.0 %collective-permute-start.19 = (f32[27,8,128]{2,1,0:T(8,128)S(1)}, f32[27,8,128]{2,1,0:T(8,128)S(1)}, u32[]{:S(2)}, u32[]{:S(2)}) collective-permute-start(f32[27,8,128]{2,1,0:T(8,128)S(1)} %shard_map.62.refs_0_), channel_id=1, source_target_pairs={{0,2},{2,0},{4,6},{6,4},{8,10},{10,8},{12,14},{14,12},{1,3},{3,1},... | collective-permute-start | bytes 331784 | tf_op jit(solution)/shard_map/ppermute | solution.py:204
  46.0 13.2 %collective-permute-start.20 = (f32[27,8,128]{2,1,0:T(8,128)S(1)}, f32[27,8,128]{2,1,0:T(8,128)S(1)}, u32[]{:S(2)}, u32[]{:S(2)}) collective-permute-start(f32[27,8,128]{2,1,0:T(8,128)S(1)} %collective-permute-done.16.refs_1_), channel_id=1, source_target_pairs={{0,2},{2,0},{4,6},{6,4},{8,10},{10,8},{12,14},{14,12},{1,3},{3,1},... | collective-permute-start | bytes 331784 | tf_op jit(solution)/shard_map/ppermute | solution.py:204
  50.5 8.7 %collective-permute-start.21 = (f32[27,8,128]{2,1,0:T(8,128)S(1)}, f32[27,8,128]{2,1,0:T(8,128)S(1)}, u32[]{:S(2)}, u32[]{:S(2)}) collective-permute-start(f32[27,8,128]{2,1,0:T(8,128)S(1)} %collective-permute-done.17.refs_2_), channel_id=1, source_target_pairs={{0,2},{2,0},{4,6},{6,4},{8,10},{10,8},{12,14},{14,12},{1,3},{3,1},... | collective-permute-start | bytes 331784 | tf_op jit(solution)/shard_map/ppermute | solution.py:204
  52.0 7.2 %collective-permute-start.22 = (f32[27,8,128]{2,1,0:T(8,128)S(1)}, f32[27,8,128]{2,1,0:T(8,128)S(1)}, u32[]{:S(2)}, u32[]{:S(2)}) collective-permute-start(f32[27,8,128]{2,1,0:T(8,128)S(1)} %collective-permute-done.18.refs_3_), channel_id=1, source_target_pairs={{0,2},{2,0},{4,6},{6,4},{8,10},{10,8},{12,14},{14,12},{1,3},{3,1},... | collective-permute-start | bytes 331784 | tf_op jit(solution)/shard_map/ppermute | solution.py:204
where the time goes:
time: 61 us; the launch traced here: 60.8 us
  starting transfers between devices  26.4 us (43%)
  waiting for transfers between devices  19.6 us (32%)
  Pallas kernels  9.42 us (15%)
  local copies, waits for them, and re-layouts  4.5 us (7%)
  between operations  0.74 us (1%)
    ppermute x6, starting transfers between devices, shift(): return lax.ppermute(value, 'space', pairs)  12.5 us
    ppermute x8, starting transfers between devices, swap_side(): return lax.ppermute(value, 'space', [(i, i ^ 1) for i in range(ring)])  10.8 us
    ppermute x6, waiting for transfers between devices, shift(): return lax.ppermute(value, 'space', pairs)  8.23 us
    ppermute x2, waiting for transfers between devices, outward(): return lax.ppermute(value, 'space', pairs)  6.62 us
    ppermute x8, waiting for transfers between devices, swap_side(): return lax.ppermute(value, 'space', [(i, i ^ 1) for i in range(ring)])  4.76 us
    unnamed x6, local copies, waits for them, and re-layouts  3.82 us
    ppermute x2, starting transfers between devices, outward(): return lax.ppermute(value, 'space', pairs)  2.57 us
    pallas_call x1, Pallas kernels, local(): call(filter_kernel, [chunk] * count, 8, [pltpu.VMEM((5, 2 * full, width),...  2.46 us
  transfers between devices with their start and end apart: 23, of which 8 were waited for; matrix products, arithmetic and copies ran while one was open for 6% of the time, Pallas kernels for 13%

commit v1 on v0

v1 whole, which is shorter than its diff:
```python
import jax
import jax.numpy as jnp
from jax import lax
from jax.experimental import pallas as pl
from jax.experimental.pallas import tpu as pltpu
from jax.sharding import PartitionSpec as P

F32 = jnp.float32
BF16 = jnp.bfloat16
VMEM = pl.BlockSpec(memory_space=pltpu.VMEM)
SMEM = pl.BlockSpec(memory_space=pltpu.SMEM)
NN = (((1,), (0,)), ((), ()))
NT = (((1,), (1,)), ((), ()))


def call(body, out_shape, n_in, scratch=(), cost=None):
    return pl.pallas_call(
        body,
        out_shape=out_shape,
        in_specs=[SMEM] + [VMEM] * n_in,
        out_specs=jax.tree.map(lambda _: VMEM, out_shape),
        scratch_shapes=scratch,
        cost_estimate=cost,
        compiler_params=pltpu.CompilerParams(vmem_limit_bytes=40 << 20),
    )


def halves(value):
    high = value.astype(BF16)
    return high, (value - high.astype(F32)).astype(BF16)


def dot3(a_hi, a_lo, b_hi, b_lo, dims):
    def dot(a, b):
        return lax.dot_general(a, b, dims, preferred_element_type=F32)

    return dot(a_hi, b_hi) + (dot(a_hi, b_lo) + dot(a_lo, b_hi))


def moved(value, step):
    width = value.shape[-1]
    lane = lax.broadcasted_iota(jnp.int32, value.shape, value.ndim - 1)
    edge = 0 if step > 0 else width - 1
    return jnp.where(lane == edge, 0.0, pltpu.roll(value, step % width, value.ndim - 1))


def weight_kernel(at, w, a_hi, a_lo, b_hi, b_lo, token, turned):
    token[...] = jnp.zeros(token.shape, F32)
    side, chan = at[1], at[2]
    sign = 1 - 2 * side
    half = a_hi.shape[1] // 6
    full = 2 * half
    own = pl.ds(pl.multiple_of(chan * half, half), half)
    for first in range(3):
        for second in range(3):
            for third in range(3):
                tap = 9 * first + 3 * second + third
                turned[...] = w[tap].T
                fwd = halves(w[tap, own, :])
                back = halves(turned[own, :])
                fwd_at = 1 + (first - 1) * sign
                back_at = 1 - (first - 1) * sign
                for low in range(2):
                    up = low + second - 1
                    if up < 0 or up > 1:
                        continue
                    row = (low * 3 + third) * half
                    a_hi[fwd_at, row : row + half, up * full : up * full + full] = fwd[0]
                    a_lo[fwd_at, row : row + half, up * full : up * full + full] = fwd[1]
                    row = (up * 3 + 2 - third) * half
                    b_hi[back_at, row : row + half, low * full : low * full + full] = back[0]
                    b_lo[back_at, row : row + half, low * full : low * full + full] = back[1]


def put_slab(hi, lo, chan, own, other):
    half = own.shape[1]
    for z in range(2):
        for piece, place in ((own, chan), (other, 1 - chan)):
            rows = pl.ds(pl.multiple_of((2 * z + place) * half, half), half)
            hi[rows, :], lo[rows, :] = halves(piece[z])


def conv_kernel(places, at, *refs):
    *blocks, w_hi, w_lo, out, x_hi, x_lo = refs
    side, chan = at[1], at[2]
    half, width = out.shape[2:]
    for t in range(4):
        put_slab(
            x_hi.at[t],
            x_lo.at[t],
            chan,
            places[t](blocks, 0, side),
            places[t](blocks, 1, side),
        )
    for t in range(2):
        total = jnp.zeros((6 * half, width), F32)
        for d in range(3):
            total = total + dot3(w_hi[d], w_lo[d], x_hi[t + d], x_lo[t + d], NN)
        slab = side if t == 0 else 1 - side
        for z in range(2):
            low, mid, high = (
                total[(3 * z + c) * half : (3 * z + c + 1) * half, :] for c in range(3)
            )
            out[slab, z] = mid + moved(low, 1) + moved(high, -1)


def filter_kernel(at, own, own2, pair, pair2, edge, edge2, g_own, g_pair, _, *rest):
    count = len(rest) - 6
    outs = rest[:count]
    x_hi, x_lo, g_hi, g_lo, acc, flat = rest[count:]
    z_at, side, chan = at[0], at[1], at[2]
    half = own.shape[2]
    part = half // 2
    group = 6 * part
    slabs = (
        (own.at[side], own2.at[side]),
        (own.at[1 - side], own2.at[1 - side]),
        (pair.at[side], pair2.at[side]),
        (pair.at[1 - side], pair2.at[1 - side]),
        (edge.at[0], edge2.at[0]),
    )
    mine = pl.ds(pl.multiple_of(side * part, part), part)
    grads = (
        lambda z: g_own[side, z, mine, :],
        lambda z: g_own[1 - side, z, mine, :],
        lambda z: g_pair[side, z],
        lambda z: g_pair[1 - side, z],
        lambda z: edge[1, z, mine, :],
    )
    for t in range(5):
        put_slab(x_hi.at[t], x_lo.at[t], chan, *slabs[t])
        for z in range(2):
            value = grads[t](z)
            for c, shifted in enumerate((moved(value, -1), value, moved(value, 1))):
                row = t * group + (3 * z + c) * part
                g_hi[row : row + part, :], g_lo[row : row + part, :] = halves(shifted)

    def term(first, last, t):
        rows = slice(first * group, last * group)
        return dot3(g_hi[rows, :], g_lo[rows, :], x_hi[t], x_lo[t], NT)

    acc[...] = term(0, 3, 1) + term(1, 4, 2) + term(2, 5, 3)
    acc[group:, :] += term(0, 2, 0)
    acc[:group, :] += term(3, 4, 4)

    full = 2 * half
    tiles = flat.shape[0]
    place = 0
    for d in range(3):
        for b in range(3):
            for c in range(3):
                row = d * group + c * part
                lower = acc[row : row + part, :]
                upper = acc[row + 3 * part : row + 4 * part, :]
                if b == 0:
                    value = upper[:, :full]
                elif b == 1:
                    value = lower[:, :full] + upper[:, full:]
                else:
                    value = lower[:, full:]
                flat[place : place + part // 8] = value.reshape(part // 8, 8, full)
                place += part // 8
    if place < tiles:
        flat[place:] = jnp.zeros((tiles - place, 8, full), F32)
    each = tiles // count
    for k in range(count):
        outs[k][...] = flat[pl.ds(lax.rem(z_at + k, count) * each, each)]


def sum_kernel(scale, at, *refs):
    total = refs[0][...]
    for ref in refs[1:-1]:
        total = total + ref[...]
    refs[-1][...] = total * scale


def join_kernel(at, *refs):
    count = (len(refs) - 3) // 2
    mine, theirs = refs[:count], refs[count : 2 * count]
    out, flat, flat2 = refs[2 * count :]
    z_at, side = at[0], at[1]
    each = mine[0].shape[0]
    for k in range(count):
        here = pl.ds(lax.rem(z_at + count - k, count) * each, each)
        flat[here] = mine[k][...]
        flat2[here] = theirs[k][...]
    rows = out.shape[1] // 2
    for source, which in ((flat, side), (flat2, 1 - side)):
        for d, base in enumerate(((1 - which) * 18, 9, which * 18)):
            block = source[d * 9 * rows : (d + 1) * 9 * rows]
            out[pl.ds(base, 9), pl.ds(which * rows, rows)] = block.reshape(
                9, rows, 8, out.shape[3]
            )


def local(inputs, weights, out_grad):
    half, _, _, width = inputs.shape
    full = 2 * half
    ring = lax.axis_size("space")
    count = ring // 2
    here = lax.axis_index("space")
    z_at, side, chan = here // 2, here % 2, lax.axis_index("chan")
    at = jnp.stack([z_at, side, chan]).astype(jnp.int32)

    def swap_chan(value):
        return lax.ppermute(value, "chan", [(0, 1), (1, 0)])

    def swap_side(value):
        return lax.ppermute(value, "space", [(i, i ^ 1) for i in range(ring)])

    def shift(value, step):
        pairs = [(2 * z + y, 2 * ((z + step) % count) + y) for z in range(count) for y in range(2)]
        return lax.ppermute(value, "space", pairs)

    def outward(value):
        pairs = []
        for z in range(count):
            if z > 0:
                pairs.append((2 * z, 2 * z - 2))
            if z + 1 < count:
                pairs.append((2 * z + 1, 2 * z + 3))
        return lax.ppermute(value, "space", pairs)

    def slab(field, index):
        return lax.dynamic_index_in_dim(field, index, 0, keepdims=False)

    x_own = inputs.transpose(1, 2, 0, 3)
    x_pair = swap_side(x_own)
    x_own2 = swap_chan(x_own)
    g_own = out_grad.transpose(1, 2, 0, 3)
    g_pair = swap_side(lax.dynamic_slice_in_dim(g_own, (1 - side) * (half // 2), half // 2, 2))
    edge = outward(jnp.stack([slab(x_own, side), slab(g_own, side)]))
    g_own2 = swap_chan(g_own)

    w_taps = weights.transpose(1, 0, 2)
    block = jax.ShapeDtypeStruct((3, 6 * half, 2 * full), BF16)
    a_hi, a_lo, b_hi, b_lo, token = call(
        weight_kernel,
        [block] * 4 + [jax.ShapeDtypeStruct((8, full), F32)],
        1,
        [pltpu.VMEM((full, full), F32)],
    )(at, w_taps)
    x_pair, edge, token, _ = lax.optimization_barrier((x_pair, edge, token, g_pair))
    x_pair2 = swap_chan(x_pair)
    edge2 = swap_chan(edge)

    tiles = 27 * (half // 2) // 8
    each = -(-tiles // count)
    chunk = jax.ShapeDtypeStruct((each, 8, full), F32)
    group = 3 * half
    parts = call(
        filter_kernel,
        [chunk] * count,
        9,
        [
            pltpu.VMEM((5, 2 * full, width), BF16),
            pltpu.VMEM((5, 2 * full, width), BF16),
            pltpu.VMEM((5 * group, width), BF16),
            pltpu.VMEM((5 * group, width), BF16),
            pltpu.VMEM((3 * group, 2 * full), F32),
            pltpu.VMEM((each * count, 8, full), F32),
        ],
    )(at, x_own, x_own2, x_pair, x_pair2, edge, edge2, g_own, g_pair, token)

    late = swap_side(edge)
    next_g = swap_side(slab(g_own, 1 - side))
    got = [parts[0]] + [shift(parts[k], k) for k in range(1, count)]
    *got, late, next_g = lax.optimization_barrier((*got, late, next_g))
    late2 = swap_chan(late)
    next_g2 = swap_chan(next_g)

    def conv(places, *operands):
        return call(
            lambda *refs: conv_kernel(places, *refs),
            jax.ShapeDtypeStruct((2, 2, half, width), F32),
            len(operands),
            [pltpu.VMEM((4, 2 * full, width), BF16)] * 2,
        )(at, *operands)

    x_places = (
        lambda r, k, side: r[4 + k].at[0],
        lambda r, k, side: r[k].at[side],
        lambda r, k, side: r[k].at[1 - side],
        lambda r, k, side: r[2 + k].at[side],
    )
    g_places = (
        lambda r, k, side: r[2 + k].at[1],
        lambda r, k, side: r[k].at[side],
        lambda r, k, side: r[k].at[1 - side],
        lambda r, k, side: r[4 + k],
    )
    outputs = conv(x_places, x_own, x_own2, x_pair, x_pair2, late, late2, a_hi, a_lo)
    in_grad = conv(g_places, g_own, g_own2, late, late2, next_g, next_g2, b_hi, b_lo)
    outputs = outputs.transpose(2, 0, 1, 3)
    in_grad = in_grad.transpose(2, 0, 1, 3)
    cells = inputs.shape[1] * ring * inputs.shape[2] * width
    scale = float(1.0 / cells**0.5)
    shard = call(lambda *refs: sum_kernel(scale, *refs), chunk, count)(at, *got)
    mine = [shard] + [shift(shard, k) for k in range(1, count)]
    theirs = [swap_side(value) for value in mine]
    theirs[-1], outputs, in_grad = lax.optimization_barrier((theirs[-1], outputs, in_grad))
    joined = call(
        join_kernel,
        jax.ShapeDtypeStruct((27, half // 8, 8, full), F32),
        2 * count,
        [pltpu.VMEM((each * count, 8, full), F32)] * 2,
    )(at, *mine, *theirs)
    filter_grad = joined.reshape(27, half, full).transpose(1, 0, 2)
    return outputs, in_grad, filter_grad


def solution(mesh):
    in_specs = (
        P("chan", ("groups", "space"), None, None),
        P(),
        P("chan", ("groups", "space"), None, None),
    )
    out_specs = (
        P("chan", ("groups", "space"), None, None),
        P("chan", ("groups", "space"), None, None),
        P("chan", "groups", None),
    )
    return jax.shard_map(local, mesh=mesh, in_specs=in_specs, out_specs=out_specs, check_vma=False)
```

time: 61 us -> 56.7 us (0.930)
  starting transfers between devices: 26.4 us -> 22.7 us
  waiting for transfers between devices: 19.6 us -> 18.7 us
  local copies, waits for them, and re-layouts: 4.5 us -> 5.32 us
    ppermute x6, waiting for transfers between devices: 8.23 us -> 13.5 us  [shift(): return lax.ppermute(value, 'space', pairs)]
    ppermute x2 -> x1, waiting for transfers between devices: 6.62 us -> 1.81 us  [outward(): return lax.ppermute(value, 'space', pairs)]
    ppermute x6, starting transfers between devices: 12.5 us -> 10.1 us  [shift(): return lax.ppermute(value, 'space', pairs)]
    ppermute x8, waiting for transfers between devices: 4.76 us -> 3.35 us  [swap_side(): return lax.ppermute(value, 'space', [(i, i ^ 1) for i in range(ring)])]
    ppermute x2 -> x1, starting transfers between devices: 2.57 us -> 1.29 us  [outward(): return lax.ppermute(value, 'space', pairs)]
    dynamic_slice x0 -> x2, local copies, waits for them, and re-layouts: none -> 0.69 us  [the longest x1 0.67 us: local(): lax.dynamic_slice_in_dim(g_own, (1 - side) * (half // 2), half // 2, 2)]
    unnamed x6 -> x8, local copies, waits for them, and re-layouts: 3.82 us -> 3.95 us
  transfers between devices with their start and end apart: 23 -> 21, of which waited for: 8 -> 8; matrix products, arithmetic and copies ran while one was open for 6% -> 8% of each run, Pallas kernels for 13% -> 13%
where the time goes in v1:
time: 56.7 us; the launch traced here: 56.5 us
  starting transfers between devices  22.7 us (40%)
  waiting for transfers between devices  18.7 us (33%)
  Pallas kernels  8.92 us (16%)
  local copies, waits for them, and re-layouts  5.32 us (9%)
  between operations  0.76 us (1%)
    ppermute x6, waiting for transfers between devices, shift(): return lax.ppermute(value, 'space', pairs)  13.5 us
    ppermute x8, starting transfers between devices, swap_side(): return lax.ppermute(value, 'space', [(i, i ^ 1) for i in range(ring)])  10.8 us
    ppermute x6, starting transfers between devices, shift(): return lax.ppermute(value, 'space', pairs)  10.1 us
    unnamed x8, local copies, waits for them, and re-layouts  3.95 us
    pallas_call x2, Pallas kernels, conv(): call(lambda *refs: conv_kernel(places, *refs), jax.ShapeDtypeStruct((2, 2...  3.63 us
    ppermute x8, waiting for transfers between devices, swap_side(): return lax.ppermute(value, 'space', [(i, i ^ 1) for i in range(ring)])  3.35 us
    pallas_call x1, Pallas kernels, local(): call(filter_kernel, [chunk] * count, 9, [pltpu.VMEM((5, 2 * full, width),...  1.97 us
    ppermute x1, waiting for transfers between devices, outward(): return lax.ppermute(value, 'space', pairs)  1.81 us
  transfers between devices with their start and end apart: 21, of which 8 were waited for; matrix products, arithmetic and copies ran while one was open for 8% of the time, Pallas kernels for 13%

profile of v1, /device:TPU:0, one launch (start us, length us, event | category | flops | bytes accessed | tf_op | source)
XLA Modules:
  0.0 56.5 jit_solution(15727202000462743630)
XLA Ops:
  0.6 1.1 %copy.19 = f32[64,2,2,256]{3,0,2,1:T(8,128)S(1)} copy(f32[64,2,2,256]{3,2,1,0:T(2,128)} %param.3) | data formatting | bytes 524288 | tf_op args[0]
  1.8 3.0 %collective-permute-start.1 = (f32[2,2,64,256]{3,2,1,0:T(8,128)S(1)}, f32[2,2,64,256]{3,2,1,0:T(8,128)S(1)}, u32[]{:S(2)}, u32[]{:S(2)}) collective-permute-start(f32[2,2,64,256]{3,2,1,0:T(8,128)S(1)} %bitcast.27), channel_id=1, source_target_pairs={{0,2},{2,0},{4,6},{6,4},{8,10},{10,8},{12,14},{14,12},{1,3},{3,1},... | collective-permute-start | bytes 786440 | tf_op jit(solution)/shard_map/ppermute | solution.py:209
  4.8 1.0 %copy.18 = f32[64,2,2,256]{3,0,2,1:T(8,128)S(1)} copy(f32[64,2,2,256]{3,2,1,0:T(2,128)} %param.5) | data formatting | bytes 524288 | tf_op args[2]
  6.6 1.3 %collective-permute-start.2 = (f32[2,2,64,256]{3,2,1,0:T(8,128)S(1)}, f32[2,2,64,256]{3,2,1,0:T(8,128)S(1)}, u32[]{:S(2)}, u32[]{:S(2)}) collective-permute-start(f32[2,2,64,256]{3,2,1,0:T(8,128)S(1)} %pad_maximum_fusion), channel_id=1, source_target_pairs={{2,6},{4,0},{6,10},{8,4},{10,14},{12,8},{3,7},{5,1},{7,11},{9,5},{... | collective-permute-start | bytes 786440 | tf_op jit(solution)/shard_map/ppermute | solution.py:222
  8.5 2.7 %collective-permute-start.3 = (f32[2,2,32,256]{3,2,1,0:T(8,128)}, f32[2,2,32,256]{3,2,1,0:T(8,128)S(1)}, u32[]{:S(2)}, u32[]{:S(2)}) collective-permute-start(f32[2,2,32,256]{3,2,1,0:T(8,128)} %dynamic-slice_bitcast_fusion.1), channel_id=1, source_target_pairs={{0,2},{2,0},{4,6},{6,4},{8,10},{10,8},{12,14},{14,12},{1,3},{3,1},... | collective-permute-start | bytes 393224 | tf_op jit(solution)/shard_map/ppermute | solution.py:209
  11.3 1.2 %shard_map.58 = (bf16[3,384,256]{2,1,0:T(8,128)(2,1)S(1)}, bf16[3,384,256]{2,1,0:T(8,128)(2,1)S(1)}, bf16[3,384,256]{2,1,0:T(8,128)(2,1)S(1)}, bf16[3,384,256]{2,1,0:T(8,128)(2,1)S(1)}, f32[8,128]{1,0:T(8,128)S(1)}) custom-call(s32[3]{0:T(128)S(1)} %pad_add_fusion.at.refs_0_, f32[27,128,128]{2,1,0:T(8,128)S(1)} %bitcast.31), custom_call_target="tpu_custom_call" | custom-call | tf_op jit(solution)/shard_map/pallas_call | solution.py:237
  12.5 1.9 %collective-permute-done.3.g_pair = f32[2,2,32,256]{3,2,1,0:T(8,128)S(1)} collective-permute-done((f32[2,2,32,256]{3,2,1,0:T(8,128)}, f32[2,2,32,256]{3,2,1,0:T(8,128)S(1)}, u32[]{:S(2)}, u32[]{:S(2)}) %collective-permute-start.3) | collective-permute-done | bytes 131104 | tf_op jit(solution)/shard_map/ppermute | solution.py:209
  14.4 1.8 %collective-permute-done.2.edge = f32[2,2,64,256]{3,2,1,0:T(8,128)S(1)} collective-permute-done((f32[2,2,64,256]{3,2,1,0:T(8,128)S(1)}, f32[2,2,64,256]{3,2,1,0:T(8,128)S(1)}, u32[]{:S(2)}, u32[]{:S(2)}) %collective-permute-start.2) | collective-permute-done | bytes 262176 | tf_op jit(solution)/shard_map/ppermute | solution.py:222
  16.9 1.8 %collective-permute-start.10 = (f32[2,64,256]{2,1,0:T(8,128)S(1)}, f32[2,64,256]{2,1,0:T(8,128)S(1)}, u32[]{:S(2)}, u32[]{:S(2)}) collective-permute-start(f32[2,64,256]{2,1,0:T(8,128)S(1)} %copy-done.1), channel_id=1, source_target_pairs={{0,2},{2,0},{4,6},{6,4},{8,10},{10,8},{12,14},{14,12},{1,3},{3,1},... | collective-permute-start | bytes 393224 | tf_op jit(solution)/shard_map/ppermute | solution.py:209
  18.8 2.0 %shard_map.59 = (f32[27,8,128]{2,1,0:T(8,128)S(1)}, f32[27,8,128]{2,1,0:T(8,128)S(1)}, f32[27,8,128]{2,1,0:T(8,128)S(1)}, f32[27,8,128]{2,1,0:T(8,128)S(1)}) custom-call(s32[3]{0:T(128)S(1)} %pad_add_fusion.at.refs_0_, f32[2,2,64,256]{3,2,1,0:T(8,128)S(1)} %bitcast.29, f32[2,2,64,256]{3,2,1,0:T(8,128)S(1)} %collective-permute-done.own2.refs_2_, ...), custom_call_target="tpu_custom_call" | custom-call | tf_op jit(solution)/shard_map/pallas_call | solution.py:251
  20.7 1.6 %collective-permute-start.6 = (f32[27,8,128]{2,1,0:T(8,128)S(1)}, f32[27,8,128]{2,1,0:T(8,128)S(1)}, u32[]{:S(2)}, u32[]{:S(2)}) collective-permute-start(f32[27,8,128]{2,1,0:T(8,128)S(1)} %get-tuple-element.29), channel_id=1, source_target_pairs={{0,4},{2,6},{4,8},{6,10},{8,12},{10,14},{12,0},{14,2},{1,5},{3,7},... | collective-permute-start | bytes 331784 | tf_op jit(solution)/shard_map/ppermute | solution.py:213
  22.4 1.2 %collective-permute-start.7 = (f32[27,8,128]{2,1,0:T(8,128)S(1)}, f32[27,8,128]{2,1,0:T(8,128)S(1)}, u32[]{:S(2)}, u32[]{:S(2)}) collective-permute-start(f32[27,8,128]{2,1,0:T(8,128)S(1)} %get-tuple-element.30), channel_id=1, source_target_pairs={{0,8},{2,10},{4,12},{6,14},{8,0},{10,2},{12,4},{14,6},{1,9},{3,11}... | collective-permute-start | bytes 331784 | tf_op jit(solution)/shard_map/ppermute | solution.py:213
  23.5 2.8 %collective-permute-start.8 = (f32[27,8,128]{2,1,0:T(8,128)S(1)}, f32[27,8,128]{2,1,0:T(8,128)S(1)}, u32[]{:S(2)}, u32[]{:S(2)}) collective-permute-start(f32[27,8,128]{2,1,0:T(8,128)S(1)} %get-tuple-element.31), channel_id=1, source_target_pairs={{0,12},{2,14},{4,0},{6,2},{8,4},{10,6},{12,8},{14,10},{1,13},{3,15... | collective-permute-start | bytes 331784 | tf_op jit(solution)/shard_map/ppermute | solution.py:213
  26.3 1.4 %collective-permute-done.10.refs_5_ = f32[2,64,256]{2,1,0:T(8,128)S(1)} collective-permute-done((f32[2,64,256]{2,1,0:T(8,128)S(1)}, f32[2,64,256]{2,1,0:T(8,128)S(1)}, u32[]{:S(2)}, u32[]{:S(2)}) %collective-permute-start.10) | collective-permute-done | bytes 131104 | tf_op jit(solution)/shard_map/ppermute | solution.py:209
  28.5 3.5 %collective-permute-done.7.refs_3_ = f32[27,8,128]{2,1,0:T(8,128)S(1)} collective-permute-done((f32[27,8,128]{2,1,0:T(8,128)S(1)}, f32[27,8,128]{2,1,0:T(8,128)S(1)}, u32[]{:S(2)}, u32[]{:S(2)}) %collective-permute-start.7) | collective-permute-done | bytes 110624 | tf_op jit(solution)/shard_map/ppermute | solution.py:213
  32.6 3.9 %collective-permute-start.11 = (f32[27,8,128]{2,1,0:T(8,128)S(1)}, f32[27,8,128]{2,1,0:T(8,128)S(1)}, u32[]{:S(2)}, u32[]{:S(2)}) collective-permute-start(f32[27,8,128]{2,1,0:T(8,128)S(1)} %shard_map.60.refs_0_), channel_id=1, source_target_pairs={{0,12},{2,14},{4,0},{6,2},{8,4},{10,6},{12,8},{14,10},{1,13},{3,15... | collective-permute-start | bytes 331784 | tf_op jit(solution)/shard_map/ppermute | solution.py:213
  37.1 2.8 %collective-permute-done.11.refs_3_ = f32[27,8,128]{2,1,0:T(8,128)S(1)} collective-permute-done((f32[27,8,128]{2,1,0:T(8,128)S(1)}, f32[27,8,128]{2,1,0:T(8,128)S(1)}, u32[]{:S(2)}, u32[]{:S(2)}) %collective-permute-start.11) | collective-permute-done | bytes 110624 | tf_op jit(solution)/shard_map/ppermute | solution.py:213
  40.4 3.9 %collective-permute-done.16.refs_1_ = f32[27,8,128]{2,1,0:T(8,128)S(1)} collective-permute-done((f32[27,8,128]{2,1,0:T(8,128)S(1)}, f32[27,8,128]{2,1,0:T(8,128)S(1)}, u32[]{:S(2)}, u32[]{:S(2)}) %collective-permute-start.16) | collective-permute-done | bytes 110624 | tf_op jit(solution)/shard_map/ppermute | solution.py:213
  44.8 2.6 %collective-permute-done.17.refs_2_ = f32[27,8,128]{2,1,0:T(8,128)S(1)} collective-permute-done((f32[27,8,128]{2,1,0:T(8,128)S(1)}, f32[27,8,128]{2,1,0:T(8,128)S(1)}, u32[]{:S(2)}, u32[]{:S(2)}) %collective-permute-start.17) | collective-permute-done | bytes 110624 | tf_op jit(solution)/shard_map/ppermute | solution.py:213
  48.0 1.4 %collective-permute-start.20 = (f32[27,8,128]{2,1,0:T(8,128)S(1)}, f32[27,8,128]{2,1,0:T(8,128)S(1)}, u32[]{:S(2)}, u32[]{:S(2)}) collective-permute-start(f32[27,8,128]{2,1,0:T(8,128)S(1)} %collective-permute-done.17.refs_2_), channel_id=1, source_target_pairs={{0,2},{2,0},{4,6},{6,4},{8,10},{10,8},{12,14},{14,12},{1,3},{3,1},... | collective-permute-start | bytes 331784 | tf_op jit(solution)/shard_map/ppermute | solution.py:209
  49.4 1.8 %shard_map.61 = f32[2,2,64,256]{3,2,1,0:T(8,128)S(1)} custom-call(s32[3]{0:T(128)S(1)} %pad_add_fusion.at.refs_0_, f32[2,2,64,256]{3,2,1,0:T(8,128)S(1)} %bitcast.30, f32[2,2,64,256]{3,2,1,0:T(8,128)S(1)} %collective-permute-done.own2.refs_2_, f32[2,2,64,256]{3,2,1,0:T(8,128)S(1)} %collective-permute-done.1.pair.refs_3_, ...), custom_call_target="tpu_custom_call" | custom-call | tf_op jit(solution)/shard_map/pallas_call | solution.py:273
  51.2 1.8 %shard_map.62 = f32[2,2,64,256]{3,2,1,0:T(8,128)S(1)} custom-call(s32[3]{0:T(128)S(1)} %pad_add_fusion.at.refs_0_, f32[2,2,64,256]{3,2,1,0:T(8,128)S(1)} %bitcast.26, f32[2,2,64,256]{3,2,1,0:T(8,128)S(1)} %collective-permute-done.14.refs_2_, f32[2,2,64,256]{3,2,1,0:T(8,128)S(1)} %collective-permute-done.9.refs_5_.refs_3_, ...), custom_call_target="tpu_custom_call" | custom-call | tf_op jit(solution)/shard_map/pallas_call | solution.py:273
  53.1 0.9 %copy.12 = f32[64,2,2,256]{3,2,1,0:T(2,128)} copy(f32[64,2,2,256]{3,0,2,1:T(8,128)S(1)} %bitcast.32) | data formatting | bytes 524288
  54.9 1.6 %shard_map.63 = f32[27,8,8,128]{3,2,1,0:T(8,128)} custom-call(s32[3]{0:T(128)S(1)} %pad_add_fusion.at.refs_0_, f32[27,8,128]{2,1,0:T(8,128)S(1)} %shard_map.60.refs_0_, f32[27,8,128]{2,1,0:T(8,128)S(1)} %collective-permute-done.16.refs_1_, f32[27,8,128]{2,1,0:T(8,128)S(1)} %collective-permute-done.17.refs_2_, ...), custom_call_target="tpu_custom_call" | custom-call | tf_op jit(solution)/shard_map/pallas_call | solution.py:302
  (37 shorter events, 6.7 us)
Async XLA Ops:
  0.6 10.7 %copy-start = (f32[128,27,128]{2,0,1:T(8,128)S(1)}, f32[128,27,128]{2,0,1:T(8,128)}, u32[]{:S(2)}) copy-start(f32[128,27,128]{2,0,1:T(8,128)} %param.4) | copy-start | bytes 5308420
  1.8 12.6 %collective-permute-start.1 = (f32[2,2,64,256]{3,2,1,0:T(8,128)S(1)}, f32[2,2,64,256]{3,2,1,0:T(8,128)S(1)}, u32[]{:S(2)}, u32[]{:S(2)}) collective-permute-start(f32[2,2,64,256]{3,2,1,0:T(8,128)S(1)} %bitcast.27), channel_id=1, source_target_pairs={{0,2},{2,0},{4,6},{6,4},{8,10},{10,8},{12,14},{14,12},{1,3},{3,1},... | collective-permute-start | bytes 786440 | tf_op jit(solution)/shard_map/ppermute | solution.py:209
  6.6 9.7 %collective-permute-start.2 = (f32[2,2,64,256]{3,2,1,0:T(8,128)S(1)}, f32[2,2,64,256]{3,2,1,0:T(8,128)S(1)}, u32[]{:S(2)}, u32[]{:S(2)}) collective-permute-start(f32[2,2,64,256]{3,2,1,0:T(8,128)S(1)} %pad_maximum_fusion), channel_id=1, source_target_pairs={{2,6},{4,0},{6,10},{8,4},{10,14},{12,8},{3,7},{5,1},{7,11},{9,5},{... | collective-permute-start | bytes 786440 | tf_op jit(solution)/shard_map/ppermute | solution.py:222
  8.5 5.9 %collective-permute-start.3 = (f32[2,2,32,256]{3,2,1,0:T(8,128)}, f32[2,2,32,256]{3,2,1,0:T(8,128)S(1)}, u32[]{:S(2)}, u32[]{:S(2)}) collective-permute-start(f32[2,2,32,256]{3,2,1,0:T(8,128)} %dynamic-slice_bitcast_fusion.1), channel_id=1, source_target_pairs={{0,2},{2,0},{4,6},{6,4},{8,10},{10,8},{12,14},{14,12},{1,3},{3,1},... | collective-permute-start | bytes 393224 | tf_op jit(solution)/shard_map/ppermute | solution.py:209
  11.2 7.5 %collective-permute-start = (f32[2,2,64,256]{3,2,1,0:T(8,128)S(1)}, f32[2,2,64,256]{3,2,1,0:T(8,128)S(1)}, u32[]{:S(2)}, u32[]{:S(2)}) collective-permute-start(f32[2,2,64,256]{3,2,1,0:T(8,128)S(1)} %bitcast.28), channel_id=1, source_target_pairs={{0,1},{1,0},{2,3},{3,2},{4,5},{5,4},{6,7},{7,6},{8,9},{9,8},{10,11... | collective-permute-start | bytes 786440 | tf_op jit(solution)/shard_map/ppermute | solution.py:206
  11.2 5.7 %copy-start.1 = (f32[2,64,256]{2,1,0:T(8,128)S(1)}, f32[2,64,256]{2,1,0:T(8,128)}, u32[]{:S(2)}) copy-start(f32[2,64,256]{2,1,0:T(8,128)} %get-tuple-element.48) | copy-start | bytes 393220
  16.2 2.5 %collective-permute-start.4 = (f32[2,2,64,256]{3,2,1,0:T(8,128)S(1)}, f32[2,2,64,256]{3,2,1,0:T(8,128)S(1)}, u32[]{:S(2)}, u32[]{:S(2)}) collective-permute-start(f32[2,2,64,256]{3,2,1,0:T(8,128)S(1)} %collective-permute-done.1.pair.refs_3_), channel_id=1, source_target_pairs={{0,1},{1,0},{2,3},{3,2},{4,5},{5,4},{6,7},{7,6},{8,9},{9,8},{10,11... | collective-permute-start | bytes 786440 | tf_op jit(solution)/shard_map/ppermute | solution.py:206
  16.2 2.5 %collective-permute-start.5 = (f32[2,2,64,256]{3,2,1,0:T(8,128)S(1)}, f32[2,2,64,256]{3,2,1,0:T(8,128)S(1)}, u32[]{:S(2)}, u32[]{:S(2)}) collective-permute-start(f32[2,2,64,256]{3,2,1,0:T(8,128)S(1)} %collective-permute-done.2.edge), channel_id=1, source_target_pairs={{0,1},{1,0},{2,3},{3,2},{4,5},{5,4},{6,7},{7,6},{8,9},{9,8},{10,11... | collective-permute-start | bytes 786440 | tf_op jit(solution)/shard_map/ppermute | solution.py:206
  16.7 11.0 %collective-permute-start.9 = (f32[2,2,64,256]{3,2,1,0:T(8,128)S(1)}, f32[2,2,64,256]{3,2,1,0:T(8,128)S(1)}, u32[]{:S(2)}, u32[]{:S(2)}) collective-permute-start(f32[2,2,64,256]{3,2,1,0:T(8,128)S(1)} %collective-permute-done.2.edge), channel_id=1, source_target_pairs={{0,2},{2,0},{4,6},{6,4},{8,10},{10,8},{12,14},{14,12},{1,3},{3,1},... | collective-permute-start | bytes 786440 | tf_op jit(solution)/shard_map/ppermute | solution.py:209
  16.9 10.8 %collective-permute-start.10 = (f32[2,64,256]{2,1,0:T(8,128)S(1)}, f32[2,64,256]{2,1,0:T(8,128)S(1)}, u32[]{:S(2)}, u32[]{:S(2)}) collective-permute-start(f32[2,64,256]{2,1,0:T(8,128)S(1)} %copy-done.1), channel_id=1, source_target_pairs={{0,2},{2,0},{4,6},{6,4},{8,10},{10,8},{12,14},{14,12},{1,3},{3,1},... | collective-permute-start | bytes 393224 | tf_op jit(solution)/shard_map/ppermute | solution.py:209
  20.7 7.8 %collective-permute-start.6 = (f32[27,8,128]{2,1,0:T(8,128)S(1)}, f32[27,8,128]{2,1,0:T(8,128)S(1)}, u32[]{:S(2)}, u32[]{:S(2)}) collective-permute-start(f32[27,8,128]{2,1,0:T(8,128)S(1)} %get-tuple-element.29), channel_id=1, source_target_pairs={{0,4},{2,6},{4,8},{6,10},{8,12},{10,14},{12,0},{14,2},{1,5},{3,7},... | collective-permute-start | bytes 331784 | tf_op jit(solution)/shard_map/ppermute | solution.py:213
  22.4 9.6 %collective-permute-start.7 = (f32[27,8,128]{2,1,0:T(8,128)S(1)}, f32[27,8,128]{2,1,0:T(8,128)S(1)}, u32[]{:S(2)}, u32[]{:S(2)}) collective-permute-start(f32[27,8,128]{2,1,0:T(8,128)S(1)} %get-tuple-element.30), channel_id=1, source_target_pairs={{0,8},{2,10},{4,12},{6,14},{8,0},{10,2},{12,4},{14,6},{1,9},{3,11}... | collective-permute-start | bytes 331784 | tf_op jit(solution)/shard_map/ppermute | solution.py:213
  23.5 8.5 %collective-permute-start.8 = (f32[27,8,128]{2,1,0:T(8,128)S(1)}, f32[27,8,128]{2,1,0:T(8,128)S(1)}, u32[]{:S(2)}, u32[]{:S(2)}) collective-permute-start(f32[27,8,128]{2,1,0:T(8,128)S(1)} %get-tuple-element.31), channel_id=1, source_target_pairs={{0,12},{2,14},{4,0},{6,2},{8,4},{10,6},{12,8},{14,10},{1,13},{3,15... | collective-permute-start | bytes 331784 | tf_op jit(solution)/shard_map/ppermute | solution.py:213
  27.7 9.4 %collective-permute-start.14 = (f32[2,2,64,256]{3,2,1,0:T(8,128)S(1)}, f32[2,2,64,256]{3,2,1,0:T(8,128)S(1)}, u32[]{:S(2)}, u32[]{:S(2)}) collective-permute-start(f32[2,2,64,256]{3,2,1,0:T(8,128)S(1)} %bitcast.25), channel_id=1, source_target_pairs={{0,1},{1,0},{2,3},{3,2},{4,5},{5,4},{6,7},{7,6},{8,9},{9,8},{10,11... | collective-permute-start | bytes 786440 | tf_op jit(solution)/shard_map/ppermute | solution.py:206
  32.0 16.0 %collective-permute-start.13 = (f32[2,2,64,256]{3,2,1,0:T(8,128)S(1)}, f32[2,2,64,256]{3,2,1,0:T(8,128)S(1)}, u32[]{:S(2)}, u32[]{:S(2)}) collective-permute-start(f32[2,2,64,256]{3,2,1,0:T(8,128)S(1)} %collective-permute-done.9.refs_5_.refs_3_), channel_id=1, source_target_pairs={{0,1},{1,0},{2,3},{3,2},{4,5},{5,4},{6,7},{7,6},{8,9},{9,8},{10,11... | collective-permute-start | bytes 786440 | tf_op jit(solution)/shard_map/ppermute | solution.py:206
  32.6 7.3 %collective-permute-start.11 = (f32[27,8,128]{2,1,0:T(8,128)S(1)}, f32[27,8,128]{2,1,0:T(8,128)S(1)}, u32[]{:S(2)}, u32[]{:S(2)}) collective-permute-start(f32[27,8,128]{2,1,0:T(8,128)S(1)} %shard_map.60.refs_0_), channel_id=1, source_target_pairs={{0,12},{2,14},{4,0},{6,2},{8,4},{10,6},{12,8},{14,10},{1,13},{3,15... | collective-permute-start | bytes 331784 | tf_op jit(solution)/shard_map/ppermute | solution.py:213
  36.5 7.8 %collective-permute-start.16 = (f32[27,8,128]{2,1,0:T(8,128)S(1)}, f32[27,8,128]{2,1,0:T(8,128)S(1)}, u32[]{:S(2)}, u32[]{:S(2)}) collective-permute-start(f32[27,8,128]{2,1,0:T(8,128)S(1)} %shard_map.60.refs_0_), channel_id=1, source_target_pairs={{0,4},{2,6},{4,8},{6,10},{8,12},{10,14},{12,0},{14,2},{1,5},{3,7},... | collective-permute-start | bytes 331784 | tf_op jit(solution)/shard_map/ppermute | solution.py:213
  36.5 10.9 %collective-permute-start.17 = (f32[27,8,128]{2,1,0:T(8,128)S(1)}, f32[27,8,128]{2,1,0:T(8,128)S(1)}, u32[]{:S(2)}, u32[]{:S(2)}) collective-permute-start(f32[27,8,128]{2,1,0:T(8,128)S(1)} %shard_map.60.refs_0_), channel_id=1, source_target_pairs={{0,8},{2,10},{4,12},{6,14},{8,0},{10,2},{12,4},{14,6},{1,9},{3,11}... | collective-permute-start | bytes 331784 | tf_op jit(solution)/shard_map/ppermute | solution.py:213
  37.1 14.1 %collective-permute-start.15 = (f32[2,64,256]{2,1,0:T(8,128)S(1)}, f32[2,64,256]{2,1,0:T(8,128)S(1)}, u32[]{:S(2)}, u32[]{:S(2)}) collective-permute-start(f32[2,64,256]{2,1,0:T(8,128)S(1)} %collective-permute-done.10.refs_5_), channel_id=1, source_target_pairs={{0,1},{1,0},{2,3},{3,2},{4,5},{5,4},{6,7},{7,6},{8,9},{9,8},{10,11... | collective-permute-start | bytes 393224 | tf_op jit(solution)/shard_map/ppermute | solution.py:206
  39.9 13.2 %collective-permute-start.12 = (f32[27,8,128]{2,1,0:T(8,128)S(1)}, f32[27,8,128]{2,1,0:T(8,128)S(1)}, u32[]{:S(2)}, u32[]{:S(2)}) collective-permute-start(f32[27,8,128]{2,1,0:T(8,128)S(1)} %collective-permute-done.11.refs_3_), channel_id=1, source_target_pairs={{0,2},{2,0},{4,6},{6,4},{8,10},{10,8},{12,14},{14,12},{1,3},{3,1},... | collective-permute-start | bytes 331784 | tf_op jit(solution)/shard_map/ppermute | solution.py:209
  44.3 10.6 %collective-permute-start.18 = (f32[27,8,128]{2,1,0:T(8,128)S(1)}, f32[27,8,128]{2,1,0:T(8,128)S(1)}, u32[]{:S(2)}, u32[]{:S(2)}) collective-permute-start(f32[27,8,128]{2,1,0:T(8,128)S(1)} %shard_map.60.refs_0_), channel_id=1, source_target_pairs={{0,2},{2,0},{4,6},{6,4},{8,10},{10,8},{12,14},{14,12},{1,3},{3,1},... | collective-permute-start | bytes 331784 | tf_op jit(solution)/shard_map/ppermute | solution.py:209
  47.4 7.5 %collective-permute-start.19 = (f32[27,8,128]{2,1,0:T(8,128)S(1)}, f32[27,8,128]{2,1,0:T(8,128)S(1)}, u32[]{:S(2)}, u32[]{:S(2)}) collective-permute-start(f32[27,8,128]{2,1,0:T(8,128)S(1)} %collective-permute-done.16.refs_1_), channel_id=1, source_target_pairs={{0,2},{2,0},{4,6},{6,4},{8,10},{10,8},{12,14},{14,12},{1,3},{3,1},... | collective-permute-start | bytes 331784 | tf_op jit(solution)/shard_map/ppermute | solution.py:209
  48.0 6.9 %collective-permute-start.20 = (f32[27,8,128]{2,1,0:T(8,128)S(1)}, f32[27,8,128]{2,1,0:T(8,128)S(1)}, u32[]{:S(2)}, u32[]{:S(2)}) collective-permute-start(f32[27,8,128]{2,1,0:T(8,128)S(1)} %collective-permute-done.17.refs_2_), channel_id=1, source_target_pairs={{0,2},{2,0},{4,6},{6,4},{8,10},{10,8},{12,14},{14,12},{1,3},{3,1},... | collective-permute-start | bytes 331784 | tf_op jit(solution)/shard_map/ppermute | solution.py:209

commit v2 on v1

--- a/solution.py
+++ b/solution.py
@@ -297,8 +297,11 @@
     scale = float(1.0 / cells**0.5)
     shard = call(lambda *refs: sum_kernel(scale, *refs), chunk, count)(at, *got)
     mine = [shard] + [shift(shard, k) for k in range(1, count)]
-    theirs = [swap_side(value) for value in mine]
-    theirs[-1], outputs, in_grad = lax.optimization_barrier((theirs[-1], outputs, in_grad))
+    theirs = [swap_side(shard)]
+    mine[1], outputs, in_grad, theirs[0] = lax.optimization_barrier(
+        (mine[1], outputs, in_grad, theirs[0])
+    )
+    theirs += [swap_side(value) for value in mine[1:]]
     joined = call(
         join_kernel,
         jax.ShapeDtypeStruct((27, half // 8, 8, full), F32),

time: 56.7 us -> 53 us (0.935)
  waiting for transfers between devices: 18.7 us -> 13.2 us
  starting transfers between devices: 22.7 us -> 24.1 us
    ppermute x6, waiting for transfers between devices: 13.5 us -> 5.65 us  [shift(): return lax.ppermute(value, 'space', pairs)]
    ppermute x8, waiting for transfers between devices: 3.35 us -> 5.71 us  [swap_side(): return lax.ppermute(value, 'space', [(i, i ^ 1) for i in range(ring)])]
    ppermute x6, starting transfers between devices: 10.1 us -> 10.7 us  [shift(): return lax.ppermute(value, 'space', pairs)]
  transfers between devices with their start and end apart: 21 -> 21, of which waited for: 8 -> 7; matrix products, arithmetic and copies ran while one was open for 8% -> 8% of each run, Pallas kernels for 13% -> 14%
where the time goes in v2:
time: 53 us; the launch traced here: 52.4 us
  starting transfers between devices  24.1 us (45%)
  waiting for transfers between devices  13.2 us (25%)
  Pallas kernels  8.92 us (17%)
  local copies, waits for them, and re-layouts  5.32 us (10%)
  between operations  0.75 us (1%)
    ppermute x8, starting transfers between devices, swap_side(): return lax.ppermute(value, 'space', [(i, i ^ 1) for i in range(ring)])  11.1 us
    ppermute x6, starting transfers between devices, shift(): return lax.ppermute(value, 'space', pairs)  10.7 us
    ppermute x8, waiting for transfers between devices, swap_side(): return lax.ppermute(value, 'space', [(i, i ^ 1) for i in range(ring)])  5.71 us
    ppermute x6, waiting for transfers between devices, shift(): return lax.ppermute(value, 'space', pairs)  5.65 us
    unnamed x8, local copies, waits for them, and re-layouts  3.95 us
    pallas_call x2, Pallas kernels, conv(): call(lambda *refs: conv_kernel(places, *refs), jax.ShapeDtypeStruct((2, 2...  3.63 us
    pallas_call x1, Pallas kernels, local(): call(filter_kernel, [chunk] * count, 9, [pltpu.VMEM((5, 2 * full, width),...  1.97 us
    ppermute x1, waiting for transfers between devices, outward(): return lax.ppermute(value, 'space', pairs)  1.81 us
  transfers between devices with their start and end apart: 21, of which 7 were waited for; matrix products, arithmetic and copies ran while one was open for 8% of the time, Pallas kernels for 14%

profile of v2, /device:TPU:0, one launch (start us, length us, event | category | flops | bytes accessed | tf_op | source)
XLA Modules:
  0.0 52.4 jit_solution(3048555109631667138)
XLA Ops:
  0.6 1.1 %copy.19 = f32[64,2,2,256]{3,0,2,1:T(8,128)S(1)} copy(f32[64,2,2,256]{3,2,1,0:T(2,128)} %param.3) | data formatting | bytes 524288 | tf_op args[0]
  1.8 3.0 %collective-permute-start.1 = (f32[2,2,64,256]{3,2,1,0:T(8,128)S(1)}, f32[2,2,64,256]{3,2,1,0:T(8,128)S(1)}, u32[]{:S(2)}, u32[]{:S(2)}) collective-permute-start(f32[2,2,64,256]{3,2,1,0:T(8,128)S(1)} %bitcast.27), channel_id=1, source_target_pairs={{0,2},{2,0},{4,6},{6,4},{8,10},{10,8},{12,14},{14,12},{1,3},{3,1},... | collective-permute-start | bytes 786440 | tf_op jit(solution)/shard_map/ppermute | solution.py:209
  4.8 1.0 %copy.18 = f32[64,2,2,256]{3,0,2,1:T(8,128)S(1)} copy(f32[64,2,2,256]{3,2,1,0:T(2,128)} %param.5) | data formatting | bytes 524288 | tf_op args[2]
  6.6 1.3 %collective-permute-start.2 = (f32[2,2,64,256]{3,2,1,0:T(8,128)S(1)}, f32[2,2,64,256]{3,2,1,0:T(8,128)S(1)}, u32[]{:S(2)}, u32[]{:S(2)}) collective-permute-start(f32[2,2,64,256]{3,2,1,0:T(8,128)S(1)} %pad_maximum_fusion), channel_id=1, source_target_pairs={{2,6},{4,0},{6,10},{8,4},{10,14},{12,8},{3,7},{5,1},{7,11},{9,5},{... | collective-permute-start | bytes 786440 | tf_op jit(solution)/shard_map/ppermute | solution.py:222
  8.5 2.7 %collective-permute-start.3 = (f32[2,2,32,256]{3,2,1,0:T(8,128)}, f32[2,2,32,256]{3,2,1,0:T(8,128)S(1)}, u32[]{:S(2)}, u32[]{:S(2)}) collective-permute-start(f32[2,2,32,256]{3,2,1,0:T(8,128)} %dynamic-slice_bitcast_fusion.1), channel_id=1, source_target_pairs={{0,2},{2,0},{4,6},{6,4},{8,10},{10,8},{12,14},{14,12},{1,3},{3,1},... | collective-permute-start | bytes 393224 | tf_op jit(solution)/shard_map/ppermute | solution.py:209
  11.3 1.2 %shard_map.58 = (bf16[3,384,256]{2,1,0:T(8,128)(2,1)S(1)}, bf16[3,384,256]{2,1,0:T(8,128)(2,1)S(1)}, bf16[3,384,256]{2,1,0:T(8,128)(2,1)S(1)}, bf16[3,384,256]{2,1,0:T(8,128)(2,1)S(1)}, f32[8,128]{1,0:T(8,128)S(1)}) custom-call(s32[3]{0:T(128)S(1)} %pad_add_fusion.at.refs_0_, f32[27,128,128]{2,1,0:T(8,128)S(1)} %bitcast.31), custom_call_target="tpu_custom_call" | custom-call | tf_op jit(solution)/shard_map/pallas_call | solution.py:237
  12.5 1.9 %collective-permute-done.3.g_pair = f32[2,2,32,256]{3,2,1,0:T(8,128)S(1)} collective-permute-done((f32[2,2,32,256]{3,2,1,0:T(8,128)}, f32[2,2,32,256]{3,2,1,0:T(8,128)S(1)}, u32[]{:S(2)}, u32[]{:S(2)}) %collective-permute-start.3) | collective-permute-done | bytes 131104 | tf_op jit(solution)/shard_map/ppermute | solution.py:209
  14.4 1.8 %collective-permute-done.2.edge = f32[2,2,64,256]{3,2,1,0:T(8,128)S(1)} collective-permute-done((f32[2,2,64,256]{3,2,1,0:T(8,128)S(1)}, f32[2,2,64,256]{3,2,1,0:T(8,128)S(1)}, u32[]{:S(2)}, u32[]{:S(2)}) %collective-permute-start.2) | collective-permute-done | bytes 262176 | tf_op jit(solution)/shard_map/ppermute | solution.py:222
  16.9 1.8 %collective-permute-start.10 = (f32[2,64,256]{2,1,0:T(8,128)S(1)}, f32[2,64,256]{2,1,0:T(8,128)S(1)}, u32[]{:S(2)}, u32[]{:S(2)}) collective-permute-start(f32[2,64,256]{2,1,0:T(8,128)S(1)} %copy-done.1), channel_id=1, source_target_pairs={{0,2},{2,0},{4,6},{6,4},{8,10},{10,8},{12,14},{14,12},{1,3},{3,1},... | collective-permute-start | bytes 393224 | tf_op jit(solution)/shard_map/ppermute | solution.py:209
  18.8 2.0 %shard_map.59 = (f32[27,8,128]{2,1,0:T(8,128)S(1)}, f32[27,8,128]{2,1,0:T(8,128)S(1)}, f32[27,8,128]{2,1,0:T(8,128)S(1)}, f32[27,8,128]{2,1,0:T(8,128)S(1)}) custom-call(s32[3]{0:T(128)S(1)} %pad_add_fusion.at.refs_0_, f32[2,2,64,256]{3,2,1,0:T(8,128)S(1)} %bitcast.29, f32[2,2,64,256]{3,2,1,0:T(8,128)S(1)} %collective-permute-done.own2.refs_2_, ...), custom_call_target="tpu_custom_call" | custom-call | tf_op jit(solution)/shard_map/pallas_call | solution.py:251
  20.7 1.6 %collective-permute-start.6 = (f32[27,8,128]{2,1,0:T(8,128)S(1)}, f32[27,8,128]{2,1,0:T(8,128)S(1)}, u32[]{:S(2)}, u32[]{:S(2)}) collective-permute-start(f32[27,8,128]{2,1,0:T(8,128)S(1)} %get-tuple-element.30), channel_id=1, source_target_pairs={{0,4},{2,6},{4,8},{6,10},{8,12},{10,14},{12,0},{14,2},{1,5},{3,7},... | collective-permute-start | bytes 331784 | tf_op jit(solution)/shard_map/ppermute | solution.py:213
  22.4 1.2 %collective-permute-start.7 = (f32[27,8,128]{2,1,0:T(8,128)S(1)}, f32[27,8,128]{2,1,0:T(8,128)S(1)}, u32[]{:S(2)}, u32[]{:S(2)}) collective-permute-start(f32[27,8,128]{2,1,0:T(8,128)S(1)} %get-tuple-element.31), channel_id=1, source_target_pairs={{0,8},{2,10},{4,12},{6,14},{8,0},{10,2},{12,4},{14,6},{1,9},{3,11}... | collective-permute-start | bytes 331784 | tf_op jit(solution)/shard_map/ppermute | solution.py:213
  23.5 2.8 %collective-permute-start.8 = (f32[27,8,128]{2,1,0:T(8,128)S(1)}, f32[27,8,128]{2,1,0:T(8,128)S(1)}, u32[]{:S(2)}, u32[]{:S(2)}) collective-permute-start(f32[27,8,128]{2,1,0:T(8,128)S(1)} %get-tuple-element.32), channel_id=1, source_target_pairs={{0,12},{2,14},{4,0},{6,2},{8,4},{10,6},{12,8},{14,10},{1,13},{3,15... | collective-permute-start | bytes 331784 | tf_op jit(solution)/shard_map/ppermute | solution.py:213
  26.3 1.4 %collective-permute-done.10.refs_5_ = f32[2,64,256]{2,1,0:T(8,128)S(1)} collective-permute-done((f32[2,64,256]{2,1,0:T(8,128)S(1)}, f32[2,64,256]{2,1,0:T(8,128)S(1)}, u32[]{:S(2)}, u32[]{:S(2)}) %collective-permute-start.10) | collective-permute-done | bytes 131104 | tf_op jit(solution)/shard_map/ppermute | solution.py:209
  28.5 3.5 %collective-permute-done.7.refs_3_ = f32[27,8,128]{2,1,0:T(8,128)S(1)} collective-permute-done((f32[27,8,128]{2,1,0:T(8,128)S(1)}, f32[27,8,128]{2,1,0:T(8,128)S(1)}, u32[]{:S(2)}, u32[]{:S(2)}) %collective-permute-start.7) | collective-permute-done | bytes 110624 | tf_op jit(solution)/shard_map/ppermute | solution.py:213
  33.1 1.8 %collective-permute-start.16 = (f32[27,8,128]{2,1,0:T(8,128)S(1)}, f32[27,8,128]{2,1,0:T(8,128)S(1)}, u32[]{:S(2)}, u32[]{:S(2)}) collective-permute-start(f32[27,8,128]{2,1,0:T(8,128)S(1)} %shard_map.60.refs_0_), channel_id=1, source_target_pairs={{0,8},{2,10},{4,12},{6,14},{8,0},{10,2},{12,4},{14,6},{1,9},{3,11}... | collective-permute-start | bytes 331784 | tf_op jit(solution)/shard_map/ppermute | solution.py:213
  34.9 3.3 %collective-permute-start.17 = (f32[27,8,128]{2,1,0:T(8,128)S(1)}, f32[27,8,128]{2,1,0:T(8,128)S(1)}, u32[]{:S(2)}, u32[]{:S(2)}) collective-permute-start(f32[27,8,128]{2,1,0:T(8,128)S(1)} %shard_map.60.refs_0_), channel_id=1, source_target_pairs={{0,12},{2,14},{4,0},{6,2},{8,4},{10,6},{12,8},{14,10},{1,13},{3,15... | collective-permute-start | bytes 331784 | tf_op jit(solution)/shard_map/ppermute | solution.py:213
  38.9 1.8 %shard_map.61 = f32[2,2,64,256]{3,2,1,0:T(8,128)S(1)} custom-call(s32[3]{0:T(128)S(1)} %pad_add_fusion.at.refs_0_, f32[2,2,64,256]{3,2,1,0:T(8,128)S(1)} %bitcast.30, f32[2,2,64,256]{3,2,1,0:T(8,128)S(1)} %collective-permute-done.own2.refs_2_, f32[2,2,64,256]{3,2,1,0:T(8,128)S(1)} %collective-permute-done.1.pair.refs_3_, ...), custom_call_target="tpu_custom_call" | custom-call | tf_op jit(solution)/shard_map/pallas_call | solution.py:273
  40.7 1.5 %collective-permute-start.19 = (f32[27,8,128]{2,1,0:T(8,128)S(1)}, f32[27,8,128]{2,1,0:T(8,128)S(1)}, u32[]{:S(2)}, u32[]{:S(2)}) collective-permute-start(f32[27,8,128]{2,1,0:T(8,128)S(1)} %collective-permute-done.16.refs_2_), channel_id=1, source_target_pairs={{0,2},{2,0},{4,6},{6,4},{8,10},{10,8},{12,14},{14,12},{1,3},{3,1},... | collective-permute-start | bytes 331784 | tf_op jit(solution)/shard_map/ppermute | solution.py:209
  42.8 1.8 %shard_map.62 = f32[2,2,64,256]{3,2,1,0:T(8,128)S(1)} custom-call(s32[3]{0:T(128)S(1)} %pad_add_fusion.at.refs_0_, f32[2,2,64,256]{3,2,1,0:T(8,128)S(1)} %bitcast.26, f32[2,2,64,256]{3,2,1,0:T(8,128)S(1)} %collective-permute-done.13.refs_2_, f32[2,2,64,256]{3,2,1,0:T(8,128)S(1)} %collective-permute-done.9.refs_5_.refs_3_, ...), custom_call_target="tpu_custom_call" | custom-call | tf_op jit(solution)/shard_map/pallas_call | solution.py:273
  44.7 1.4 %collective-permute-done.11.refs_1_ = f32[27,8,128]{2,1,0:T(8,128)S(1)} collective-permute-done((f32[27,8,128]{2,1,0:T(8,128)S(1)}, f32[27,8,128]{2,1,0:T(8,128)S(1)}, u32[]{:S(2)}, u32[]{:S(2)}) %collective-permute-start.11) | collective-permute-done | bytes 110624 | tf_op jit(solution)/shard_map/ppermute | solution.py:213
  46.6 0.9 %copy.12 = f32[64,2,2,256]{3,2,1,0:T(2,128)} copy(f32[64,2,2,256]{3,0,2,1:T(8,128)S(1)} %bitcast.32) | data formatting | bytes 524288
  48.5 2.4 %collective-permute-done.18.refs_5_ = f32[27,8,128]{2,1,0:T(8,128)S(1)} collective-permute-done((f32[27,8,128]{2,1,0:T(8,128)S(1)}, f32[27,8,128]{2,1,0:T(8,128)S(1)}, u32[]{:S(2)}, u32[]{:S(2)}) %collective-permute-start.18) | collective-permute-done | bytes 110624 | tf_op jit(solution)/shard_map/ppermute | solution.py:209
  50.8 1.6 %shard_map.63 = f32[27,8,8,128]{3,2,1,0:T(8,128)} custom-call(s32[3]{0:T(128)S(1)} %pad_add_fusion.at.refs_0_, f32[27,8,128]{2,1,0:T(8,128)S(1)} %shard_map.60.refs_0_, f32[27,8,128]{2,1,0:T(8,128)S(1)} %collective-permute-done.11.refs_1_, f32[27,8,128]{2,1,0:T(8,128)S(1)} %collective-permute-done.16.refs_2_, ...), custom_call_target="tpu_custom_call" | custom-call | tf_op jit(solution)/shard_map/pallas_call | solution.py:305
  (37 shorter events, 6.9 us)
Async XLA Ops:
  0.6 10.7 %copy-start = (f32[128,27,128]{2,0,1:T(8,128)S(1)}, f32[128,27,128]{2,0,1:T(8,128)}, u32[]{:S(2)}) copy-start(f32[128,27,128]{2,0,1:T(8,128)} %param.4) | copy-start | bytes 5308420
  1.8 12.6 %collective-permute-start.1 = (f32[2,2,64,256]{3,2,1,0:T(8,128)S(1)}, f32[2,2,64,256]{3,2,1,0:T(8,128)S(1)}, u32[]{:S(2)}, u32[]{:S(2)}) collective-permute-start(f32[2,2,64,256]{3,2,1,0:T(8,128)S(1)} %bitcast.27), channel_id=1, source_target_pairs={{0,2},{2,0},{4,6},{6,4},{8,10},{10,8},{12,14},{14,12},{1,3},{3,1},... | collective-permute-start | bytes 786440 | tf_op jit(solution)/shard_map/ppermute | solution.py:209
  6.6 9.7 %collective-permute-start.2 = (f32[2,2,64,256]{3,2,1,0:T(8,128)S(1)}, f32[2,2,64,256]{3,2,1,0:T(8,128)S(1)}, u32[]{:S(2)}, u32[]{:S(2)}) collective-permute-start(f32[2,2,64,256]{3,2,1,0:T(8,128)S(1)} %pad_maximum_fusion), channel_id=1, source_target_pairs={{2,6},{4,0},{6,10},{8,4},{10,14},{12,8},{3,7},{5,1},{7,11},{9,5},{... | collective-permute-start | bytes 786440 | tf_op jit(solution)/shard_map/ppermute | solution.py:222
  8.5 5.9 %collective-permute-start.3 = (f32[2,2,32,256]{3,2,1,0:T(8,128)}, f32[2,2,32,256]{3,2,1,0:T(8,128)S(1)}, u32[]{:S(2)}, u32[]{:S(2)}) collective-permute-start(f32[2,2,32,256]{3,2,1,0:T(8,128)} %dynamic-slice_bitcast_fusion.1), channel_id=1, source_target_pairs={{0,2},{2,0},{4,6},{6,4},{8,10},{10,8},{12,14},{14,12},{1,3},{3,1},... | collective-permute-start | bytes 393224 | tf_op jit(solution)/shard_map/ppermute | solution.py:209
  11.2 7.5 %collective-permute-start = (f32[2,2,64,256]{3,2,1,0:T(8,128)S(1)}, f32[2,2,64,256]{3,2,1,0:T(8,128)S(1)}, u32[]{:S(2)}, u32[]{:S(2)}) collective-permute-start(f32[2,2,64,256]{3,2,1,0:T(8,128)S(1)} %bitcast.28), channel_id=1, source_target_pairs={{0,1},{1,0},{2,3},{3,2},{4,5},{5,4},{6,7},{7,6},{8,9},{9,8},{10,11... | collective-permute-start | bytes 786440 | tf_op jit(solution)/shard_map/ppermute | solution.py:206
  11.2 5.7 %copy-start.1 = (f32[2,64,256]{2,1,0:T(8,128)S(1)}, f32[2,64,256]{2,1,0:T(8,128)}, u32[]{:S(2)}) copy-start(f32[2,64,256]{2,1,0:T(8,128)} %get-tuple-element.50) | copy-start | bytes 393220
  16.2 2.5 %collective-permute-start.4 = (f32[2,2,64,256]{3,2,1,0:T(8,128)S(1)}, f32[2,2,64,256]{3,2,1,0:T(8,128)S(1)}, u32[]{:S(2)}, u32[]{:S(2)}) collective-permute-start(f32[2,2,64,256]{3,2,1,0:T(8,128)S(1)} %collective-permute-done.1.pair.refs_3_), channel_id=1, source_target_pairs={{0,1},{1,0},{2,3},{3,2},{4,5},{5,4},{6,7},{7,6},{8,9},{9,8},{10,11... | collective-permute-start | bytes 786440 | tf_op jit(solution)/shard_map/ppermute | solution.py:206
  16.2 2.5 %collective-permute-start.5 = (f32[2,2,64,256]{3,2,1,0:T(8,128)S(1)}, f32[2,2,64,256]{3,2,1,0:T(8,128)S(1)}, u32[]{:S(2)}, u32[]{:S(2)}) collective-permute-start(f32[2,2,64,256]{3,2,1,0:T(8,128)S(1)} %collective-permute-done.2.edge), channel_id=1, source_target_pairs={{0,1},{1,0},{2,3},{3,2},{4,5},{5,4},{6,7},{7,6},{8,9},{9,8},{10,11... | collective-permute-start | bytes 786440 | tf_op jit(solution)/shard_map/ppermute | solution.py:206
  16.7 11.0 %collective-permute-start.9 = (f32[2,2,64,256]{3,2,1,0:T(8,128)S(1)}, f32[2,2,64,256]{3,2,1,0:T(8,128)S(1)}, u32[]{:S(2)}, u32[]{:S(2)}) collective-permute-start(f32[2,2,64,256]{3,2,1,0:T(8,128)S(1)} %collective-permute-done.2.edge), channel_id=1, source_target_pairs={{0,2},{2,0},{4,6},{6,4},{8,10},{10,8},{12,14},{14,12},{1,3},{3,1},... | collective-permute-start | bytes 786440 | tf_op jit(solution)/shard_map/ppermute | solution.py:209
  16.9 10.8 %collective-permute-start.10 = (f32[2,64,256]{2,1,0:T(8,128)S(1)}, f32[2,64,256]{2,1,0:T(8,128)S(1)}, u32[]{:S(2)}, u32[]{:S(2)}) collective-permute-start(f32[2,64,256]{2,1,0:T(8,128)S(1)} %copy-done.1), channel_id=1, source_target_pairs={{0,2},{2,0},{4,6},{6,4},{8,10},{10,8},{12,14},{14,12},{1,3},{3,1},... | collective-permute-start | bytes 393224 | tf_op jit(solution)/shard_map/ppermute | solution.py:209
  20.7 7.8 %collective-permute-start.6 = (f32[27,8,128]{2,1,0:T(8,128)S(1)}, f32[27,8,128]{2,1,0:T(8,128)S(1)}, u32[]{:S(2)}, u32[]{:S(2)}) collective-permute-start(f32[27,8,128]{2,1,0:T(8,128)S(1)} %get-tuple-element.30), channel_id=1, source_target_pairs={{0,4},{2,6},{4,8},{6,10},{8,12},{10,14},{12,0},{14,2},{1,5},{3,7},... | collective-permute-start | bytes 331784 | tf_op jit(solution)/shard_map/ppermute | solution.py:213
  22.4 9.6 %collective-permute-start.7 = (f32[27,8,128]{2,1,0:T(8,128)S(1)}, f32[27,8,128]{2,1,0:T(8,128)S(1)}, u32[]{:S(2)}, u32[]{:S(2)}) collective-permute-start(f32[27,8,128]{2,1,0:T(8,128)S(1)} %get-tuple-element.31), channel_id=1, source_target_pairs={{0,8},{2,10},{4,12},{6,14},{8,0},{10,2},{12,4},{14,6},{1,9},{3,11}... | collective-permute-start | bytes 331784 | tf_op jit(solution)/shard_map/ppermute | solution.py:213
  23.5 8.5 %collective-permute-start.8 = (f32[27,8,128]{2,1,0:T(8,128)S(1)}, f32[27,8,128]{2,1,0:T(8,128)S(1)}, u32[]{:S(2)}, u32[]{:S(2)}) collective-permute-start(f32[27,8,128]{2,1,0:T(8,128)S(1)} %get-tuple-element.32), channel_id=1, source_target_pairs={{0,12},{2,14},{4,0},{6,2},{8,4},{10,6},{12,8},{14,10},{1,13},{3,15... | collective-permute-start | bytes 331784 | tf_op jit(solution)/shard_map/ppermute | solution.py:213
  27.7 10.5 %collective-permute-start.13 = (f32[2,2,64,256]{3,2,1,0:T(8,128)S(1)}, f32[2,2,64,256]{3,2,1,0:T(8,128)S(1)}, u32[]{:S(2)}, u32[]{:S(2)}) collective-permute-start(f32[2,2,64,256]{3,2,1,0:T(8,128)S(1)} %bitcast.25), channel_id=1, source_target_pairs={{0,1},{1,0},{2,3},{3,2},{4,5},{5,4},{6,7},{7,6},{8,9},{9,8},{10,11... | collective-permute-start | bytes 786440 | tf_op jit(solution)/shard_map/ppermute | solution.py:206
  32.0 6.2 %collective-permute-start.12 = (f32[2,2,64,256]{3,2,1,0:T(8,128)S(1)}, f32[2,2,64,256]{3,2,1,0:T(8,128)S(1)}, u32[]{:S(2)}, u32[]{:S(2)}) collective-permute-start(f32[2,2,64,256]{3,2,1,0:T(8,128)S(1)} %collective-permute-done.9.refs_5_.refs_3_), channel_id=1, source_target_pairs={{0,1},{1,0},{2,3},{3,2},{4,5},{5,4},{6,7},{7,6},{8,9},{9,8},{10,11... | collective-permute-start | bytes 786440 | tf_op jit(solution)/shard_map/ppermute | solution.py:206
  32.0 10.8 %collective-permute-start.14 = (f32[2,64,256]{2,1,0:T(8,128)S(1)}, f32[2,64,256]{2,1,0:T(8,128)S(1)}, u32[]{:S(2)}, u32[]{:S(2)}) collective-permute-start(f32[2,64,256]{2,1,0:T(8,128)S(1)} %collective-permute-done.10.refs_5_), channel_id=1, source_target_pairs={{0,1},{1,0},{2,3},{3,2},{4,5},{5,4},{6,7},{7,6},{8,9},{9,8},{10,11... | collective-permute-start | bytes 393224 | tf_op jit(solution)/shard_map/ppermute | solution.py:206
  33.1 7.6 %collective-permute-start.16 = (f32[27,8,128]{2,1,0:T(8,128)S(1)}, f32[27,8,128]{2,1,0:T(8,128)S(1)}, u32[]{:S(2)}, u32[]{:S(2)}) collective-permute-start(f32[27,8,128]{2,1,0:T(8,128)S(1)} %shard_map.60.refs_0_), channel_id=1, source_target_pairs={{0,8},{2,10},{4,12},{6,14},{8,0},{10,2},{12,4},{14,6},{1,9},{3,11}... | collective-permute-start | bytes 331784 | tf_op jit(solution)/shard_map/ppermute | solution.py:213
  34.9 7.3 %collective-permute-start.17 = (f32[27,8,128]{2,1,0:T(8,128)S(1)}, f32[27,8,128]{2,1,0:T(8,128)S(1)}, u32[]{:S(2)}, u32[]{:S(2)}) collective-permute-start(f32[27,8,128]{2,1,0:T(8,128)S(1)} %shard_map.60.refs_0_), channel_id=1, source_target_pairs={{0,12},{2,14},{4,0},{6,2},{8,4},{10,6},{12,8},{14,10},{1,13},{3,15... | collective-permute-start | bytes 331784 | tf_op jit(solution)/shard_map/ppermute | solution.py:213
  38.2 7.8 %collective-permute-start.11 = (f32[27,8,128]{2,1,0:T(8,128)S(1)}, f32[27,8,128]{2,1,0:T(8,128)S(1)}, u32[]{:S(2)}, u32[]{:S(2)}) collective-permute-start(f32[27,8,128]{2,1,0:T(8,128)S(1)} %shard_map.60.refs_0_), channel_id=1, source_target_pairs={{0,4},{2,6},{4,8},{6,10},{8,12},{10,14},{12,0},{14,2},{1,5},{3,7},... | collective-permute-start | bytes 331784 | tf_op jit(solution)/shard_map/ppermute | solution.py:213
  38.2 7.8 %collective-permute-start.15 = (f32[27,8,128]{2,1,0:T(8,128)S(1)}, f32[27,8,128]{2,1,0:T(8,128)S(1)}, u32[]{:S(2)}, u32[]{:S(2)}) collective-permute-start(f32[27,8,128]{2,1,0:T(8,128)S(1)} %shard_map.60.refs_0_), channel_id=1, source_target_pairs={{0,2},{2,0},{4,6},{6,4},{8,10},{10,8},{12,14},{14,12},{1,3},{3,1},... | collective-permute-start | bytes 331784 | tf_op jit(solution)/shard_map/ppermute | solution.py:209
  40.7 7.7 %collective-permute-start.19 = (f32[27,8,128]{2,1,0:T(8,128)S(1)}, f32[27,8,128]{2,1,0:T(8,128)S(1)}, u32[]{:S(2)}, u32[]{:S(2)}) collective-permute-start(f32[27,8,128]{2,1,0:T(8,128)S(1)} %collective-permute-done.16.refs_2_), channel_id=1, source_target_pairs={{0,2},{2,0},{4,6},{6,4},{8,10},{10,8},{12,14},{14,12},{1,3},{3,1},... | collective-permute-start | bytes 331784 | tf_op jit(solution)/shard_map/ppermute | solution.py:209
  42.2 6.2 %collective-permute-start.20 = (f32[27,8,128]{2,1,0:T(8,128)S(1)}, f32[27,8,128]{2,1,0:T(8,128)S(1)}, u32[]{:S(2)}, u32[]{:S(2)}) collective-permute-start(f32[27,8,128]{2,1,0:T(8,128)S(1)} %collective-permute-done.17.refs_3_), channel_id=1, source_target_pairs={{0,2},{2,0},{4,6},{6,4},{8,10},{10,8},{12,14},{14,12},{1,3},{3,1},... | collective-permute-start | bytes 331784 | tf_op jit(solution)/shard_map/ppermute | solution.py:209
  46.1 4.7 %collective-permute-start.18 = (f32[27,8,128]{2,1,0:T(8,128)S(1)}, f32[27,8,128]{2,1,0:T(8,128)S(1)}, u32[]{:S(2)}, u32[]{:S(2)}) collective-permute-start(f32[27,8,128]{2,1,0:T(8,128)S(1)} %collective-permute-done.11.refs_1_), channel_id=1, source_target_pairs={{0,2},{2,0},{4,6},{6,4},{8,10},{10,8},{12,14},{14,12},{1,3},{3,1},... | collective-permute-start | bytes 331784 | tf_op jit(solution)/shard_map/ppermute | solution.py:209

commit v3 on v2

--- a/solution.py
+++ b/solution.py
@@ -72,12 +72,18 @@
                     b_lo[back_at, row : row + half, low * full : low * full + full] = back[1]
 
 
+def put_pieces(hi, lo, pieces):
+    depth = hi.shape[0] // 2
+    for piece, first in pieces:
+        count = piece.shape[1]
+        for z in range(2):
+            rows = pl.ds(pl.multiple_of(z * depth + first, count), count)
+            hi[rows, :], lo[rows, :] = halves(piece[z])
+
+
 def put_slab(hi, lo, chan, own, other):
     half = own.shape[1]
-    for z in range(2):
-        for piece, place in ((own, chan), (other, 1 - chan)):
-            rows = pl.ds(pl.multiple_of((2 * z + place) * half, half), half)
-            hi[rows, :], lo[rows, :] = halves(piece[z])
+    put_pieces(hi, lo, ((own, chan * half), (other, (1 - chan) * half)))
 
 
 def conv_kernel(places, at, *refs):
@@ -85,13 +91,7 @@
     side, chan = at[1], at[2]
     half, width = out.shape[2:]
     for t in range(4):
-        put_slab(
-            x_hi.at[t],
-            x_lo.at[t],
-            chan,
-            places[t](blocks, 0, side),
-            places[t](blocks, 1, side),
-        )
+        put_pieces(x_hi.at[t], x_lo.at[t], places[t](blocks, side, chan))
     for t in range(2):
         total = jnp.zeros((6 * half, width), F32)
         for d in range(3):
@@ -104,44 +104,69 @@
             out[slab, z] = mid + moved(low, 1) + moved(high, -1)
 
 
-def filter_kernel(at, own, own2, pair, pair2, edge, edge2, g_own, g_pair, _, *rest):
+def put_grad(hi, lo, load, part):
+    for z in range(2):
+        value = load(z)
+        for c, shifted in enumerate((moved(value, -1), value, moved(value, 1))):
+            row = (3 * z + c) * part
+            hi[row : row + part, :], lo[row : row + part, :] = halves(shifted)
+
+
+def own_kernel(at, own, own2, g_own, _, acc, x1_hi, x1_lo, g1_hi, g1_lo, token, x_hi, x_lo, g_hi, g_lo):
+    token[...] = jnp.zeros(token.shape, F32)
+    side, chan = at[1], at[2]
+    part = own.shape[2] // 2
+    group = 6 * part
+    mine = pl.ds(pl.multiple_of(side * part, part), part)
+    for t, slab in enumerate((side, 1 - side)):
+        put_slab(x_hi.at[t], x_lo.at[t], chan, own.at[slab], own2.at[slab])
+        rows = pl.ds(t * group, group)
+        put_grad(g_hi.at[rows], g_lo.at[rows], lambda z: g_own[slab, z, mine, :], part)
+    x1_hi[...] = x_hi[1]
+    x1_lo[...] = x_lo[1]
+    g1_hi[...] = g_hi[group:, :]
+    g1_lo[...] = g_lo[group:, :]
+    later = dot3(g_hi[...], g_lo[...], x_hi[0], x_lo[0], NT)
+    early = dot3(g_hi[...], g_lo[...], x_hi[1], x_lo[1], NT)
+    acc[:group, :] = early[:group, :]
+    acc[group : 2 * group, :] = early[group:, :] + later[:group, :]
+    acc[2 * group :, :] = later[group:, :]
+
+
+def filter_kernel(at, acc, x1_hi, x1_lo, g1_hi, g1_lo, pair, pair2, edge, edge2, g_pair, _, *rest):
     count = len(rest) - 6
     outs = rest[:count]
-    x_hi, x_lo, g_hi, g_lo, acc, flat = rest[count:]
+    x_hi, x_lo, g_hi, g_lo, sums, flat = rest[count:]
     z_at, side, chan = at[0], at[1], at[2]
-    half = own.shape[2]
+    half = pair.shape[2]
     part = half // 2
     group = 6 * part
     slabs = (
-        (own.at[side], own2.at[side]),
-        (own.at[1 - side], own2.at[1 - side]),
         (pair.at[side], pair2.at[side]),
         (pair.at[1 - side], pair2.at[1 - side]),
         (edge.at[0], edge2.at[0]),
     )
     mine = pl.ds(pl.multiple_of(side * part, part), part)
     grads = (
-        lambda z: g_own[side, z, mine, :],
-        lambda z: g_own[1 - side, z, mine, :],
         lambda z: g_pair[side, z],
         lambda z: g_pair[1 - side, z],
         lambda z: edge[1, z, mine, :],
     )
-    for t in range(5):
+    g_hi[:group, :] = g1_hi[...]
+    g_lo[:group, :] = g1_lo[...]
+    for t in range(3):
         put_slab(x_hi.at[t], x_lo.at[t], chan, *slabs[t])
-        for z in range(2):
-            value = grads[t](z)
-            for c, shifted in enumerate((moved(value, -1), value, moved(value, 1))):
-                row = t * group + (3 * z + c) * part
-                g_hi[row : row + part, :], g_lo[row : row + part, :] = halves(shifted)
-
-    def term(first, last, t):
+        rows = pl.ds((t + 1) * group, group)
+        put_grad(g_hi.at[rows], g_lo.at[rows], grads[t], part)
+
+    def term(first, last, hi, lo):
         rows = slice(first * group, last * group)
-        return dot3(g_hi[rows, :], g_lo[rows, :], x_hi[t], x_lo[t], NT)
-
-    acc[...] = term(0, 3, 1) + term(1, 4, 2) + term(2, 5, 3)
-    acc[group:, :] += term(0, 2, 0)
-    acc[:group, :] += term(3, 4, 4)
+        return dot3(g_hi[rows, :], g_lo[rows, :], hi, lo, NT)
+
+    sums[...] = acc[...] + term(0, 3, x_hi[0], x_lo[0]) + term(1, 4, x_hi[1], x_lo[1])
+    sums[2 * group :, :] += term(1, 2, x1_hi[...], x1_lo[...])
+    sums[:group, :] += term(2, 3, x_hi[2], x_lo[2])
+    acc = sums
 
     full = 2 * half
     tiles = flat.shape[0]
@@ -228,7 +253,10 @@
     x_pair = swap_side(x_own)
     x_own2 = swap_chan(x_own)
     g_own = out_grad.transpose(1, 2, 0, 3)
-    g_pair = swap_side(lax.dynamic_slice_in_dim(g_own, (1 - side) * (half // 2), half // 2, 2))
+    g_theirs = lax.dynamic_slice_in_dim(g_own, (1 - side) * (half // 2), half // 2, 2)
+    g_ours = lax.dynamic_slice_in_dim(g_own, side * (half // 2), half // 2, 2)
+    g_ours = lax.dynamic_slice_in_dim(g_ours, 1 - side, 1, 0)
+    g_pair = swap_side(jnp.concatenate([g_theirs, g_ours]))
     edge = outward(jnp.stack([slab(x_own, side), slab(g_own, side)]))
     g_own2 = swap_chan(g_own)
 
@@ -240,34 +268,40 @@
         1,
         [pltpu.VMEM((full, full), F32)],
     )(at, w_taps)
-    x_pair, edge, token, _ = lax.optimization_barrier((x_pair, edge, token, g_pair))
+    group = 3 * half
+    slab_half = jax.ShapeDtypeStruct((2 * full, width), BF16)
+    grad_half = jax.ShapeDtypeStruct((group, width), BF16)
+    *inner, done = call(
+        own_kernel,
+        [jax.ShapeDtypeStruct((3 * group, 2 * full), F32)]
+        + [slab_half] * 2
+        + [grad_half] * 2
+        + [jax.ShapeDtypeStruct((8, full), F32)],
+        4,
+        [pltpu.VMEM((2, 2 * full, width), BF16)] * 2 + [pltpu.VMEM((2 * group, width), BF16)] * 2,
+    )(at, x_own, x_own2, g_own, token)
+    x_pair, done = lax.optimization_barrier((x_pair, done))
+    edge, _ = lax.optimization_barrier((edge, g_pair))
     x_pair2 = swap_chan(x_pair)
     edge2 = swap_chan(edge)
 
     tiles = 27 * (half // 2) // 8
     each = -(-tiles // count)
     chunk = jax.ShapeDtypeStruct((each, 8, full), F32)
-    group = 3 * half
     parts = call(
         filter_kernel,
         [chunk] * count,
-        9,
-        [
-            pltpu.VMEM((5, 2 * full, width), BF16),
-            pltpu.VMEM((5, 2 * full, width), BF16),
-            pltpu.VMEM((5 * group, width), BF16),
-            pltpu.VMEM((5 * group, width), BF16),
-            pltpu.VMEM((3 * group, 2 * full), F32),
-            pltpu.VMEM((each * count, 8, full), F32),
-        ],
-    )(at, x_own, x_own2, x_pair, x_pair2, edge, edge2, g_own, g_pair, token)
+        11,
+        [pltpu.VMEM((3, 2 * full, width), BF16)] * 2
+        + [pltpu.VMEM((4 * group, width), BF16)] * 2
+        + [pltpu.VMEM((3 * group, 2 * full), F32), pltpu.VMEM((each * count, 8, full), F32)],
+    )(at, *inner, x_pair, x_pair2, edge, edge2, g_pair, done)
 
     late = swap_side(edge)
-    next_g = swap_side(slab(g_own, 1 - side))
     got = [parts[0]] + [shift(parts[k], k) for k in range(1, count)]
-    *got, late, next_g = lax.optimization_barrier((*got, late, next_g))
+    *got, late = lax.optimization_barrier((*got, late))
     late2 = swap_chan(late)
-    next_g2 = swap_chan(next_g)
+    g_pair2 = swap_chan(g_pair)
 
     def conv(places, *operands):
         return call(
@@ -277,20 +311,31 @@
             [pltpu.VMEM((4, 2 * full, width), BF16)] * 2,
         )(at, *operands)
 
+    def both(own, other, chan):
+        return ((own, chan * half), (other, (1 - chan) * half))
+
+    def quarters(r, side, chan):
+        part = half // 2
+        return tuple(
+            (block, core * half + which * part)
+            for pair, core in ((r[4], chan), (r[5], 1 - chan))
+            for block, which in ((pair.at[side], side), (pair.at[2], 1 - side))
+        )
+
     x_places = (
-        lambda r, k, side: r[4 + k].at[0],
-        lambda r, k, side: r[k].at[side],
-        lambda r, k, side: r[k].at[1 - side],
-        lambda r, k, side: r[2 + k].at[side],
+        lambda r, side, chan: both(r[4].at[0], r[5].at[0], chan),
+        lambda r, side, chan: both(r[0].at[side], r[1].at[side], chan),
+        lambda r, side, chan: both(r[0].at[1 - side], r[1].at[1 - side], chan),
+        lambda r, side, chan: both(r[2].at[side], r[3].at[side], chan),
     )
     g_places = (
-        lambda r, k, side: r[2 + k].at[1],
-        lambda r, k, side: r[k].at[side],
-        lambda r, k, side: r[k].at[1 - side],
-        lambda r, k, side: r[4 + k],
+        lambda r, side, chan: both(r[2].at[1], r[3].at[1], chan),
+        lambda r, side, chan: both(r[0].at[side], r[1].at[side], chan),
+        lambda r, side, chan: both(r[0].at[1 - side], r[1].at[1 - side], chan),
+        quarters,
     )
     outputs = conv(x_places, x_own, x_own2, x_pair, x_pair2, late, late2, a_hi, a_lo)
-    in_grad = conv(g_places, g_own, g_own2, late, late2, next_g, next_g2, b_hi, b_lo)
+    in_grad = conv(g_places, g_own, g_own2, late, late2, g_pair, g_pair2, b_hi, b_lo)
     outputs = outputs.transpose(2, 0, 1, 3)
     in_grad = in_grad.transpose(2, 0, 1, 3)
     cells = inputs.shape[1] * ring * inputs.shape[2] * width

time: 53 us -> 52.3 us (0.987)
  waiting for transfers between devices: 13.2 us -> 11.4 us
  local copies, waits for them, and re-layouts: 5.32 us -> 4.01 us
  starting transfers between devices: 24.1 us -> 25.1 us
  Pallas kernels: 8.92 us -> 9.65 us
  other arithmetic: 0.09 us -> 0.79 us
    ppermute x1, waiting for transfers between devices: 1.81 us -> 0.24 us  [outward(): return lax.ppermute(value, 'space', pairs)]
    ppermute x8 -> x7, waiting for transfers between devices: 5.71 us -> 4.3 us  [swap_side(): return lax.ppermute(value, 'space', [(i, i ^ 1) for i in range(ring)])]
    ppermute x6, waiting for transfers between devices: 5.65 us -> 6.82 us  [shift(): return lax.ppermute(value, 'space', pairs)]
    ppermute x8 -> x7, starting transfers between devices: 11.1 us -> 11.8 us  [swap_side(): return lax.ppermute(value, 'space', [(i, i ^ 1) for i in range(ring)])]
    pallas_call x1 -> x2, Pallas kernels: 1.97 us -> 2.69 us  [the longest x1 1.56 us: local(): call(filter_kernel, [chunk] * count, 11, [pltpu.VMEM((3, 2 * full, width)...]
    concatenate x0 -> x1, other arithmetic: none -> 0.69 us  [local(): g_pair = swap_side(jnp.concatenate([g_theirs, g_ours]))]
    squeeze x1 -> x0, local copies, waits for them, and re-layouts: 0.68 us -> none  [slab(): return lax.dynamic_index_in_dim(field, index, 0, keepdims=False)]
    dynamic_slice x1, local copies, waits for them, and re-layouts: 0.67 us -> 0.02 us  [local(): lax.dynamic_slice_in_dim(g_own, (1 - side) * (half // 2), half // 2, 2)]
  transfers between devices with their start and end apart: 21 -> 20, of which waited for: 7 -> 6; matrix products, arithmetic and copies ran while one was open for 8% -> 7% of each run, Pallas kernels for 14% -> 16%
where the time goes in v3:
time: 52.3 us; the launch traced here: 51.7 us
  starting transfers between devices  25.1 us (48%)
  waiting for transfers between devices  11.4 us (22%)
  Pallas kernels  9.65 us (18%)
  local copies, waits for them, and re-layouts  4.01 us (8%)
  between operations  0.82 us (2%)
  other arithmetic  0.79 us (2%)
    ppermute x7, starting transfers between devices, swap_side(): return lax.ppermute(value, 'space', [(i, i ^ 1) for i in range(ring)])  11.8 us
    ppermute x6, starting transfers between devices, shift(): return lax.ppermute(value, 'space', pairs)  10.8 us
    ppermute x6, waiting for transfers between devices, shift(): return lax.ppermute(value, 'space', pairs)  6.82 us
    ppermute x7, waiting for transfers between devices, swap_side(): return lax.ppermute(value, 'space', [(i, i ^ 1) for i in range(ring)])  4.3 us
    unnamed x6, local copies, waits for them, and re-layouts  3.95 us
    pallas_call x2, Pallas kernels, conv(): call(lambda *refs: conv_kernel(places, *refs), jax.ShapeDtypeStruct((2, 2...  3.64 us
    pallas_call x1, Pallas kernels, local(): call(join_kernel, jax.ShapeDtypeStruct((27, half // 8, 8, full), F32), 2...  1.57 us
    pallas_call x1, Pallas kernels, local(): call(filter_kernel, [chunk] * count, 11, [pltpu.VMEM((3, 2 * full, width)...  1.56 us
  transfers between devices with their start and end apart: 20, of which 6 were waited for; matrix products, arithmetic and copies ran while one was open for 7% of the time, Pallas kernels for 16%

profile of v3, /device:TPU:0, one launch (start us, length us, event | category | flops | bytes accessed | tf_op | source)
XLA Modules:
  0.0 51.7 jit_solution(3119656101717984826)
XLA Ops:
  0.6 1.1 %copy.18 = f32[64,2,2,256]{3,0,2,1:T(8,128)S(1)} copy(f32[64,2,2,256]{3,2,1,0:T(2,128)} %param.3) | data formatting | bytes 524288 | tf_op args[0]
  2.3 2.6 %collective-permute-start.1 = (f32[2,2,64,256]{3,2,1,0:T(8,128)S(1)}, f32[2,2,64,256]{3,2,1,0:T(8,128)S(1)}, u32[]{:S(2)}, u32[]{:S(2)}) collective-permute-start(f32[2,2,64,256]{3,2,1,0:T(8,128)S(1)} %bitcast.25), channel_id=1, source_target_pairs={{0,2},{2,0},{4,6},{6,4},{8,10},{10,8},{12,14},{14,12},{1,3},{3,1},... | collective-permute-start | bytes 786440 | tf_op jit(solution)/shard_map/ppermute | solution.py:234
  4.9 1.0 %copy.19 = f32[64,2,2,256]{3,0,2,1:T(8,128)S(1)} copy(f32[64,2,2,256]{3,2,1,0:T(2,128)} %param.5) | data formatting | bytes 524288 | tf_op args[2]
  6.0 1.3 %collective-permute-start.3 = (f32[2,2,64,256]{3,2,1,0:T(8,128)S(1)}, f32[2,2,64,256]{3,2,1,0:T(8,128)S(1)}, u32[]{:S(2)}, u32[]{:S(2)}) collective-permute-start(f32[2,2,64,256]{3,2,1,0:T(8,128)S(1)} %pad_maximum_fusion), channel_id=1, source_target_pairs={{2,6},{4,0},{6,10},{8,4},{10,14},{12,8},{3,7},{5,1},{7,11},{9,5},{... | collective-permute-start | bytes 786440 | tf_op jit(solution)/shard_map/ppermute | solution.py:247
  8.0 2.7 %collective-permute-start.4 = (f32[3,2,32,256]{3,2,1,0:T(8,128)}, f32[3,2,32,256]{3,2,1,0:T(8,128)S(1)}, u32[]{:S(2)}, u32[]{:S(2)}) collective-permute-start(f32[3,2,32,256]{3,2,1,0:T(8,128)} %pad_maximum_fusion.1), channel_id=1, source_target_pairs={{0,2},{2,0},{4,6},{6,4},{8,10},{10,8},{12,14},{14,12},{1,3},{3,1},... | collective-permute-start | bytes 589832 | tf_op jit(solution)/shard_map/ppermute | solution.py:234
  10.8 1.2 %shard_map.58 = (bf16[3,384,256]{2,1,0:T(8,128)(2,1)S(1)}, bf16[3,384,256]{2,1,0:T(8,128)(2,1)S(1)}, bf16[3,384,256]{2,1,0:T(8,128)(2,1)S(1)}, bf16[3,384,256]{2,1,0:T(8,128)(2,1)S(1)}, f32[8,128]{1,0:T(8,128)S(1)}) custom-call(s32[3]{0:T(128)S(1)} %pad_add_fusion.at.refs_0_, f32[27,128,128]{2,1,0:T(8,128)S(1)} %bitcast.28), custom_call_target="tpu_custom_call" | custom-call | tf_op jit(solution)/shard_map/pallas_call | solution.py:265
  12.0 1.1 %shard_map.59 = (f32[576,256]{1,0:T(8,128)S(1)}, bf16[256,256]{1,0:T(8,128)(2,1)S(1)}, bf16[256,256]{1,0:T(8,128)(2,1)S(1)}, bf16[192,256]{1,0:T(8,128)(2,1)S(1)...) custom-call(s32[3]{0:T(128)S(1)} %pad_add_fusion.at.refs_0_, f32[2,2,64,256]{3,2,1,0:T(8,128)S(1)} %bitcast.26, ...), custom_call_target="tpu_custom_call" | custom-call | tf_op jit(solution)/shard_map/pallas_call | solution.py:274
  13.3 2.7 %collective-permute-done.4.g_pair.refs_5_ = f32[3,2,32,256]{3,2,1,0:T(8,128)S(1)} collective-permute-done((f32[3,2,32,256]{3,2,1,0:T(8,128)}, f32[3,2,32,256]{3,2,1,0:T(8,128)S(1)}, u32[]{:S(2)}, u32[]{:S(2)}) %collective-permute-start.4) | collective-permute-done | bytes 196640 | tf_op jit(solution)/shard_map/ppermute | solution.py:234
  16.2 1.5 %collective-permute-start.9 = (f32[2,2,64,256]{3,2,1,0:T(8,128)S(1)}, f32[2,2,64,256]{3,2,1,0:T(8,128)S(1)}, u32[]{:S(2)}, u32[]{:S(2)}) collective-permute-start(f32[2,2,64,256]{3,2,1,0:T(8,128)S(1)} %collective-permute-done.3.edge), channel_id=1, source_target_pairs={{0,2},{2,0},{4,6},{6,4},{8,10},{10,8},{12,14},{14,12},{1,3},{3,1},... | collective-permute-start | bytes 786440 | tf_op jit(solution)/shard_map/ppermute | solution.py:234
  17.8 1.6 %shard_map.60 = (f32[27,8,128]{2,1,0:T(8,128)S(1)}, f32[27,8,128]{2,1,0:T(8,128)S(1)}, f32[27,8,128]{2,1,0:T(8,128)S(1)}, f32[27,8,128]{2,1,0:T(8,128)S(1)}) custom-call(s32[3]{0:T(128)S(1)} %pad_add_fusion.at.refs_0_, f32[576,256]{1,0:T(8,128)S(1)} %get-tuple-element.31.acc, bf16[256,256]{1,0:T(8,128)(2,1)S(1)} %get-tuple-element.32.x1_hi, ...), custom_call_target="tpu_custom_call" | custom-call | tf_op jit(solution)/shard_map/pallas_call | solution.py:291
  19.3 1.6 %collective-permute-start.6 = (f32[27,8,128]{2,1,0:T(8,128)S(1)}, f32[27,8,128]{2,1,0:T(8,128)S(1)}, u32[]{:S(2)}, u32[]{:S(2)}) collective-permute-start(f32[27,8,128]{2,1,0:T(8,128)S(1)} %get-tuple-element.41), channel_id=1, source_target_pairs={{0,4},{2,6},{4,8},{6,10},{8,12},{10,14},{12,0},{14,2},{1,5},{3,7},... | collective-permute-start | bytes 331784 | tf_op jit(solution)/shard_map/ppermute | solution.py:238
  21.0 2.6 %collective-permute-start.7 = (f32[27,8,128]{2,1,0:T(8,128)S(1)}, f32[27,8,128]{2,1,0:T(8,128)S(1)}, u32[]{:S(2)}, u32[]{:S(2)}) collective-permute-start(f32[27,8,128]{2,1,0:T(8,128)S(1)} %get-tuple-element.42), channel_id=1, source_target_pairs={{0,8},{2,10},{4,12},{6,14},{8,0},{10,2},{12,4},{14,6},{1,9},{3,11}... | collective-permute-start | bytes 331784 | tf_op jit(solution)/shard_map/ppermute | solution.py:238
  23.6 1.4 %collective-permute-start.8 = (f32[27,8,128]{2,1,0:T(8,128)S(1)}, f32[27,8,128]{2,1,0:T(8,128)S(1)}, u32[]{:S(2)}, u32[]{:S(2)}) collective-permute-start(f32[27,8,128]{2,1,0:T(8,128)S(1)} %get-tuple-element.43), channel_id=1, source_target_pairs={{0,12},{2,14},{4,0},{6,2},{8,4},{10,6},{12,8},{14,10},{1,13},{3,15... | collective-permute-start | bytes 331784 | tf_op jit(solution)/shard_map/ppermute | solution.py:238
  25.0 2.2 %collective-permute-done.6.refs_2_ = f32[27,8,128]{2,1,0:T(8,128)S(1)} collective-permute-done((f32[27,8,128]{2,1,0:T(8,128)S(1)}, f32[27,8,128]{2,1,0:T(8,128)S(1)}, u32[]{:S(2)}, u32[]{:S(2)}) %collective-permute-start.6) | collective-permute-done | bytes 110624 | tf_op jit(solution)/shard_map/ppermute | solution.py:238
  27.2 4.1 %collective-permute-done.7.refs_3_ = f32[27,8,128]{2,1,0:T(8,128)S(1)} collective-permute-done((f32[27,8,128]{2,1,0:T(8,128)S(1)}, f32[27,8,128]{2,1,0:T(8,128)S(1)}, u32[]{:S(2)}, u32[]{:S(2)}) %collective-permute-start.7) | collective-permute-done | bytes 110624 | tf_op jit(solution)/shard_map/ppermute | solution.py:238
  32.4 1.9 %collective-permute-start.15 = (f32[27,8,128]{2,1,0:T(8,128)S(1)}, f32[27,8,128]{2,1,0:T(8,128)S(1)}, u32[]{:S(2)}, u32[]{:S(2)}) collective-permute-start(f32[27,8,128]{2,1,0:T(8,128)S(1)} %shard_map.61.refs_0_), channel_id=1, source_target_pairs={{0,8},{2,10},{4,12},{6,14},{8,0},{10,2},{12,4},{14,6},{1,9},{3,11}... | collective-permute-start | bytes 331784 | tf_op jit(solution)/shard_map/ppermute | solution.py:238
  34.3 3.4 %collective-permute-start.16 = (f32[27,8,128]{2,1,0:T(8,128)S(1)}, f32[27,8,128]{2,1,0:T(8,128)S(1)}, u32[]{:S(2)}, u32[]{:S(2)}) collective-permute-start(f32[27,8,128]{2,1,0:T(8,128)S(1)} %shard_map.61.refs_0_), channel_id=1, source_target_pairs={{0,12},{2,14},{4,0},{6,2},{8,4},{10,6},{12,8},{14,10},{1,13},{3,15... | collective-permute-start | bytes 331784 | tf_op jit(solution)/shard_map/ppermute | solution.py:238
  37.6 1.5 %collective-permute-start.14 = (f32[27,8,128]{2,1,0:T(8,128)S(1)}, f32[27,8,128]{2,1,0:T(8,128)S(1)}, u32[]{:S(2)}, u32[]{:S(2)}) collective-permute-start(f32[27,8,128]{2,1,0:T(8,128)S(1)} %shard_map.61.refs_0_), channel_id=1, source_target_pairs={{0,2},{2,0},{4,6},{6,4},{8,10},{10,8},{12,14},{14,12},{1,3},{3,1},... | collective-permute-start | bytes 331784 | tf_op jit(solution)/shard_map/ppermute | solution.py:234
  39.1 1.8 %shard_map.62 = f32[2,2,64,256]{3,2,1,0:T(8,128)S(1)} custom-call(s32[3]{0:T(128)S(1)} %pad_add_fusion.at.refs_0_, f32[2,2,64,256]{3,2,1,0:T(8,128)S(1)} %bitcast.27, f32[2,2,64,256]{3,2,1,0:T(8,128)S(1)} %collective-permute-done.own2.refs_2_, f32[2,2,64,256]{3,2,1,0:T(8,128)S(1)} %collective-permute-done.1.pair.refs_3_, ...), custom_call_target="tpu_custom_call" | custom-call | tf_op jit(solution)/shard_map/pallas_call | solution.py:307
  41.6 1.4 %collective-permute-start.19 = (f32[27,8,128]{2,1,0:T(8,128)S(1)}, f32[27,8,128]{2,1,0:T(8,128)S(1)}, u32[]{:S(2)}, u32[]{:S(2)}) collective-permute-start(f32[27,8,128]{2,1,0:T(8,128)S(1)} %collective-permute-done.16.refs_3_), channel_id=1, source_target_pairs={{0,2},{2,0},{4,6},{6,4},{8,10},{10,8},{12,14},{14,12},{1,3},{3,1},... | collective-permute-start | bytes 331784 | tf_op jit(solution)/shard_map/ppermute | solution.py:234
  43.1 1.8 %shard_map.63 = f32[2,2,64,256]{3,2,1,0:T(8,128)S(1)} custom-call(s32[3]{0:T(128)S(1)} %pad_add_fusion.at.refs_0_, f32[2,2,64,256]{3,2,1,0:T(8,128)S(1)} %bitcast.23, f32[2,2,64,256]{3,2,1,0:T(8,128)S(1)} %collective-permute-done.12.refs_2_, f32[2,2,64,256]{3,2,1,0:T(8,128)S(1)} %collective-permute-done.9.refs_5_.refs_3_, ...), custom_call_target="tpu_custom_call" | custom-call | tf_op jit(solution)/shard_map/pallas_call | solution.py:307
  45.4 1.4 %collective-permute-start.17 = (f32[27,8,128]{2,1,0:T(8,128)S(1)}, f32[27,8,128]{2,1,0:T(8,128)S(1)}, u32[]{:S(2)}, u32[]{:S(2)}) collective-permute-start(f32[27,8,128]{2,1,0:T(8,128)S(1)} %collective-permute-done.10.refs_1_), channel_id=1, source_target_pairs={{0,2},{2,0},{4,6},{6,4},{8,10},{10,8},{12,14},{14,12},{1,3},{3,1},... | collective-permute-start | bytes 331784 | tf_op jit(solution)/shard_map/ppermute | solution.py:234
  48.7 1.5 %collective-permute-done.17.refs_5_ = f32[27,8,128]{2,1,0:T(8,128)S(1)} collective-permute-done((f32[27,8,128]{2,1,0:T(8,128)S(1)}, f32[27,8,128]{2,1,0:T(8,128)S(1)}, u32[]{:S(2)}, u32[]{:S(2)}) %collective-permute-start.17) | collective-permute-done | bytes 110624 | tf_op jit(solution)/shard_map/ppermute | solution.py:234
  50.2 1.6 %shard_map.64 = f32[27,8,8,128]{3,2,1,0:T(8,128)} custom-call(s32[3]{0:T(128)S(1)} %pad_add_fusion.at.refs_0_, f32[27,8,128]{2,1,0:T(8,128)S(1)} %shard_map.61.refs_0_, f32[27,8,128]{2,1,0:T(8,128)S(1)} %collective-permute-done.10.refs_1_, f32[27,8,128]{2,1,0:T(8,128)S(1)} %collective-permute-done.15.refs_2_, ...), custom_call_target="tpu_custom_call" | custom-call | tf_op jit(solution)/shard_map/pallas_call | solution.py:350
  (36 shorter events, 5.8 us)
Async XLA Ops:
  0.6 10.2 %copy-start = (f32[128,27,128]{2,0,1:T(8,128)S(1)}, f32[128,27,128]{2,0,1:T(8,128)}, u32[]{:S(2)}) copy-start(f32[128,27,128]{2,0,1:T(8,128)} %param.4) | copy-start | bytes 5308420
  1.8 10.2 %collective-permute-start = (f32[2,2,64,256]{3,2,1,0:T(8,128)S(1)}, f32[2,2,64,256]{3,2,1,0:T(8,128)S(1)}, u32[]{:S(2)}, u32[]{:S(2)}) collective-permute-start(f32[2,2,64,256]{3,2,1,0:T(8,128)S(1)} %bitcast.24), channel_id=1, source_target_pairs={{0,1},{1,0},{2,3},{3,2},{4,5},{5,4},{6,7},{7,6},{8,9},{9,8},{10,11... | collective-permute-start | bytes 786440 | tf_op jit(solution)/shard_map/ppermute | solution.py:231
  2.3 10.9 %collective-permute-start.1 = (f32[2,2,64,256]{3,2,1,0:T(8,128)S(1)}, f32[2,2,64,256]{3,2,1,0:T(8,128)S(1)}, u32[]{:S(2)}, u32[]{:S(2)}) collective-permute-start(f32[2,2,64,256]{3,2,1,0:T(8,128)S(1)} %bitcast.25), channel_id=1, source_target_pairs={{0,2},{2,0},{4,6},{6,4},{8,10},{10,8},{12,14},{14,12},{1,3},{3,1},... | collective-permute-start | bytes 786440 | tf_op jit(solution)/shard_map/ppermute | solution.py:234
  6.0 10.3 %collective-permute-start.3 = (f32[2,2,64,256]{3,2,1,0:T(8,128)S(1)}, f32[2,2,64,256]{3,2,1,0:T(8,128)S(1)}, u32[]{:S(2)}, u32[]{:S(2)}) collective-permute-start(f32[2,2,64,256]{3,2,1,0:T(8,128)S(1)} %pad_maximum_fusion), channel_id=1, source_target_pairs={{2,6},{4,0},{6,10},{8,4},{10,14},{12,8},{3,7},{5,1},{7,11},{9,5},{... | collective-permute-start | bytes 786440 | tf_op jit(solution)/shard_map/ppermute | solution.py:247
  8.0 7.9 %collective-permute-start.4 = (f32[3,2,32,256]{3,2,1,0:T(8,128)}, f32[3,2,32,256]{3,2,1,0:T(8,128)S(1)}, u32[]{:S(2)}, u32[]{:S(2)}) collective-permute-start(f32[3,2,32,256]{3,2,1,0:T(8,128)} %pad_maximum_fusion.1), channel_id=1, source_target_pairs={{0,2},{2,0},{4,6},{6,4},{8,10},{10,8},{12,14},{14,12},{1,3},{3,1},... | collective-permute-start | bytes 589832 | tf_op jit(solution)/shard_map/ppermute | solution.py:234
  13.2 4.6 %collective-permute-start.2 = (f32[2,2,64,256]{3,2,1,0:T(8,128)S(1)}, f32[2,2,64,256]{3,2,1,0:T(8,128)S(1)}, u32[]{:S(2)}, u32[]{:S(2)}) collective-permute-start(f32[2,2,64,256]{3,2,1,0:T(8,128)S(1)} %collective-permute-done.1.pair.refs_3_), channel_id=1, source_target_pairs={{0,1},{1,0},{2,3},{3,2},{4,5},{5,4},{6,7},{7,6},{8,9},{9,8},{10,11... | collective-permute-start | bytes 786440 | tf_op jit(solution)/shard_map/ppermute | solution.py:231
  16.2 1.5 %collective-permute-start.5 = (f32[2,2,64,256]{3,2,1,0:T(8,128)S(1)}, f32[2,2,64,256]{3,2,1,0:T(8,128)S(1)}, u32[]{:S(2)}, u32[]{:S(2)}) collective-permute-start(f32[2,2,64,256]{3,2,1,0:T(8,128)S(1)} %collective-permute-done.3.edge), channel_id=1, source_target_pairs={{0,1},{1,0},{2,3},{3,2},{4,5},{5,4},{6,7},{7,6},{8,9},{9,8},{10,11... | collective-permute-start | bytes 786440 | tf_op jit(solution)/shard_map/ppermute | solution.py:231
  16.2 8.7 %collective-permute-start.9 = (f32[2,2,64,256]{3,2,1,0:T(8,128)S(1)}, f32[2,2,64,256]{3,2,1,0:T(8,128)S(1)}, u32[]{:S(2)}, u32[]{:S(2)}) collective-permute-start(f32[2,2,64,256]{3,2,1,0:T(8,128)S(1)} %collective-permute-done.3.edge), channel_id=1, source_target_pairs={{0,2},{2,0},{4,6},{6,4},{8,10},{10,8},{12,14},{14,12},{1,3},{3,1},... | collective-permute-start | bytes 786440 | tf_op jit(solution)/shard_map/ppermute | solution.py:234
  19.3 7.8 %collective-permute-start.6 = (f32[27,8,128]{2,1,0:T(8,128)S(1)}, f32[27,8,128]{2,1,0:T(8,128)S(1)}, u32[]{:S(2)}, u32[]{:S(2)}) collective-permute-start(f32[27,8,128]{2,1,0:T(8,128)S(1)} %get-tuple-element.41), channel_id=1, source_target_pairs={{0,4},{2,6},{4,8},{6,10},{8,12},{10,14},{12,0},{14,2},{1,5},{3,7},... | collective-permute-start | bytes 331784 | tf_op jit(solution)/shard_map/ppermute | solution.py:238
  21.0 10.3 %collective-permute-start.7 = (f32[27,8,128]{2,1,0:T(8,128)S(1)}, f32[27,8,128]{2,1,0:T(8,128)S(1)}, u32[]{:S(2)}, u32[]{:S(2)}) collective-permute-start(f32[27,8,128]{2,1,0:T(8,128)S(1)} %get-tuple-element.42), channel_id=1, source_target_pairs={{0,8},{2,10},{4,12},{6,14},{8,0},{10,2},{12,4},{14,6},{1,9},{3,11}... | collective-permute-start | bytes 331784 | tf_op jit(solution)/shard_map/ppermute | solution.py:238
  23.6 7.7 %collective-permute-start.8 = (f32[27,8,128]{2,1,0:T(8,128)S(1)}, f32[27,8,128]{2,1,0:T(8,128)S(1)}, u32[]{:S(2)}, u32[]{:S(2)}) collective-permute-start(f32[27,8,128]{2,1,0:T(8,128)S(1)} %get-tuple-element.43), channel_id=1, source_target_pairs={{0,12},{2,14},{4,0},{6,2},{8,4},{10,6},{12,8},{14,10},{1,13},{3,15... | collective-permute-start | bytes 331784 | tf_op jit(solution)/shard_map/ppermute | solution.py:238
  24.9 12.7 %collective-permute-start.12 = (f32[2,2,64,256]{3,2,1,0:T(8,128)S(1)}, f32[2,2,64,256]{3,2,1,0:T(8,128)S(1)}, u32[]{:S(2)}, u32[]{:S(2)}) collective-permute-start(f32[2,2,64,256]{3,2,1,0:T(8,128)S(1)} %bitcast.22), channel_id=1, source_target_pairs={{0,1},{1,0},{2,3},{3,2},{4,5},{5,4},{6,7},{7,6},{8,9},{9,8},{10,11... | collective-permute-start | bytes 786440 | tf_op jit(solution)/shard_map/ppermute | solution.py:231
  31.3 6.4 %collective-permute-start.11 = (f32[2,2,64,256]{3,2,1,0:T(8,128)S(1)}, f32[2,2,64,256]{3,2,1,0:T(8,128)S(1)}, u32[]{:S(2)}, u32[]{:S(2)}) collective-permute-start(f32[2,2,64,256]{3,2,1,0:T(8,128)S(1)} %collective-permute-done.9.refs_5_.refs_3_), channel_id=1, source_target_pairs={{0,1},{1,0},{2,3},{3,2},{4,5},{5,4},{6,7},{7,6},{8,9},{9,8},{10,11... | collective-permute-start | bytes 786440 | tf_op jit(solution)/shard_map/ppermute | solution.py:231
  31.3 11.8 %collective-permute-start.13 = (f32[3,2,32,256]{3,2,1,0:T(8,128)S(1)}, f32[3,2,32,256]{3,2,1,0:T(8,128)S(1)}, u32[]{:S(2)}, u32[]{:S(2)}) collective-permute-start(f32[3,2,32,256]{3,2,1,0:T(8,128)S(1)} %collective-permute-done.4.g_pair.refs_5_), channel_id=1, source_target_pairs={{0,1},{1,0},{2,3},{3,2},{4,5},{5,4},{6,7},{7,6},{8,9},{9,8},{10,11... | collective-permute-start | bytes 589832 | tf_op jit(solution)/shard_map/ppermute | solution.py:231
  32.4 8.6 %collective-permute-start.15 = (f32[27,8,128]{2,1,0:T(8,128)S(1)}, f32[27,8,128]{2,1,0:T(8,128)S(1)}, u32[]{:S(2)}, u32[]{:S(2)}) collective-permute-start(f32[27,8,128]{2,1,0:T(8,128)S(1)} %shard_map.61.refs_0_), channel_id=1, source_target_pairs={{0,8},{2,10},{4,12},{6,14},{8,0},{10,2},{12,4},{14,6},{1,9},{3,11}... | collective-permute-start | bytes 331784 | tf_op jit(solution)/shard_map/ppermute | solution.py:238
  34.3 7.4 %collective-permute-start.16 = (f32[27,8,128]{2,1,0:T(8,128)S(1)}, f32[27,8,128]{2,1,0:T(8,128)S(1)}, u32[]{:S(2)}, u32[]{:S(2)}) collective-permute-start(f32[27,8,128]{2,1,0:T(8,128)S(1)} %shard_map.61.refs_0_), channel_id=1, source_target_pairs={{0,12},{2,14},{4,0},{6,2},{8,4},{10,6},{12,8},{14,10},{1,13},{3,15... | collective-permute-start | bytes 331784 | tf_op jit(solution)/shard_map/ppermute | solution.py:238
  37.6 7.8 %collective-permute-start.10 = (f32[27,8,128]{2,1,0:T(8,128)S(1)}, f32[27,8,128]{2,1,0:T(8,128)S(1)}, u32[]{:S(2)}, u32[]{:S(2)}) collective-permute-start(f32[27,8,128]{2,1,0:T(8,128)S(1)} %shard_map.61.refs_0_), channel_id=1, source_target_pairs={{0,4},{2,6},{4,8},{6,10},{8,12},{10,14},{12,0},{14,2},{1,5},{3,7},... | collective-permute-start | bytes 331784 | tf_op jit(solution)/shard_map/ppermute | solution.py:238
  37.6 7.8 %collective-permute-start.14 = (f32[27,8,128]{2,1,0:T(8,128)S(1)}, f32[27,8,128]{2,1,0:T(8,128)S(1)}, u32[]{:S(2)}, u32[]{:S(2)}) collective-permute-start(f32[27,8,128]{2,1,0:T(8,128)S(1)} %shard_map.61.refs_0_), channel_id=1, source_target_pairs={{0,2},{2,0},{4,6},{6,4},{8,10},{10,8},{12,14},{14,12},{1,3},{3,1},... | collective-permute-start | bytes 331784 | tf_op jit(solution)/shard_map/ppermute | solution.py:234
  41.0 7.7 %collective-permute-start.18 = (f32[27,8,128]{2,1,0:T(8,128)S(1)}, f32[27,8,128]{2,1,0:T(8,128)S(1)}, u32[]{:S(2)}, u32[]{:S(2)}) collective-permute-start(f32[27,8,128]{2,1,0:T(8,128)S(1)} %collective-permute-done.15.refs_2_), channel_id=1, source_target_pairs={{0,2},{2,0},{4,6},{6,4},{8,10},{10,8},{12,14},{14,12},{1,3},{3,1},... | collective-permute-start | bytes 331784 | tf_op jit(solution)/shard_map/ppermute | solution.py:234
  41.6 7.0 %collective-permute-start.19 = (f32[27,8,128]{2,1,0:T(8,128)S(1)}, f32[27,8,128]{2,1,0:T(8,128)S(1)}, u32[]{:S(2)}, u32[]{:S(2)}) collective-permute-start(f32[27,8,128]{2,1,0:T(8,128)S(1)} %collective-permute-done.16.refs_3_), channel_id=1, source_target_pairs={{0,2},{2,0},{4,6},{6,4},{8,10},{10,8},{12,14},{14,12},{1,3},{3,1},... | collective-permute-start | bytes 331784 | tf_op jit(solution)/shard_map/ppermute | solution.py:234
  45.4 4.7 %collective-permute-start.17 = (f32[27,8,128]{2,1,0:T(8,128)S(1)}, f32[27,8,128]{2,1,0:T(8,128)S(1)}, u32[]{:S(2)}, u32[]{:S(2)}) collective-permute-start(f32[27,8,128]{2,1,0:T(8,128)S(1)} %collective-permute-done.10.refs_1_), channel_id=1, source_target_pairs={{0,2},{2,0},{4,6},{6,4},{8,10},{10,8},{12,14},{14,12},{1,3},{3,1},... | collective-permute-start | bytes 331784 | tf_op jit(solution)/shard_map/ppermute | solution.py:234

commit v4 on v3

--- a/solution.py
+++ b/solution.py
@@ -251,8 +251,9 @@
 
     x_own = inputs.transpose(1, 2, 0, 3)
     x_pair = swap_side(x_own)
-    x_own2 = swap_chan(x_own)
     g_own = out_grad.transpose(1, 2, 0, 3)
+    x_next, g_own = lax.optimization_barrier((x_own, g_own))
+    x_own2 = swap_chan(x_next)
     g_theirs = lax.dynamic_slice_in_dim(g_own, (1 - side) * (half // 2), half // 2, 2)
     g_ours = lax.dynamic_slice_in_dim(g_own, side * (half // 2), half // 2, 2)
     g_ours = lax.dynamic_slice_in_dim(g_ours, 1 - side, 1, 0)

time: 52.3 us -> 51.7 us (0.989)
  local copies, waits for them, and re-layouts: 4.01 us -> 3.14 us
    unnamed x6 -> x5, local copies, waits for them, and re-layouts: 3.95 us -> 3.08 us
  transfers between devices with their start and end apart: 20 -> 20, of which waited for: 6 -> 6; matrix products, arithmetic and copies ran while one was open for 7% -> 5% of each run, Pallas kernels for 16% -> 16%
where the time goes in v4:
time: 51.7 us; the launch traced here: 51.2 us
  starting transfers between devices  25.1 us (49%)
  waiting for transfers between devices  11.7 us (23%)
  Pallas kernels  9.66 us (19%)
  local copies, waits for them, and re-layouts  3.14 us (6%)
  between operations  0.81 us (2%)
  other arithmetic  0.79 us (2%)
    ppermute x7, starting transfers between devices, swap_side(): return lax.ppermute(value, 'space', [(i, i ^ 1) for i in range(ring)])  12.4 us
    ppermute x6, starting transfers between devices, shift(): return lax.ppermute(value, 'space', pairs)  10.8 us
    ppermute x6, waiting for transfers between devices, shift(): return lax.ppermute(value, 'space', pairs)  6.86 us
    ppermute x7, waiting for transfers between devices, swap_side(): return lax.ppermute(value, 'space', [(i, i ^ 1) for i in range(ring)])  4.68 us
    pallas_call x2, Pallas kernels, conv(): call(lambda *refs: conv_kernel(places, *refs), jax.ShapeDtypeStruct((2, 2...  3.64 us
    unnamed x5, local copies, waits for them, and re-layouts  3.08 us
    pallas_call x1, Pallas kernels, local(): call(join_kernel, jax.ShapeDtypeStruct((27, half // 8, 8, full), F32), 2...  1.57 us
    pallas_call x1, Pallas kernels, local(): call(filter_kernel, [chunk] * count, 11, [pltpu.VMEM((3, 2 * full, width)...  1.57 us
  transfers between devices with their start and end apart: 20, of which 6 were waited for; matrix products, arithmetic and copies ran while one was open for 5% of the time, Pallas kernels for 16%

profile of v4, /device:TPU:0, one launch (start us, length us, event | category | flops | bytes accessed | tf_op | source)
XLA Modules:
  0.0 51.2 jit_solution(17955729876780241516)
XLA Ops:
  0.6 1.3 %fusion = (f32[64,2,2,256]{3,0,2,1:T(8,128)S(1)}, f32[2,2,64,256]{3,2,1,0:T(8,128)S(1)}, f32[2,2,64,256]{3,2,1,0:T(8,128)S(1)}) fusion(f32[64,2,2,256]{3,2,1,0:T(2,128)} %param.3, f32[64,2,2,256]{3,2,1,0:T(2,128)} %param.5), kind=kLoop, calls=%fused_computation.9 | loop fusion | bytes 1310720 | tf_op args[0]
  1.9 3.0 %collective-permute-start.1 = (f32[2,2,64,256]{3,2,1,0:T(8,128)S(1)}, f32[2,2,64,256]{3,2,1,0:T(8,128)S(1)}, u32[]{:S(2)}, u32[]{:S(2)}) collective-permute-start(f32[2,2,64,256]{3,2,1,0:T(8,128)S(1)} %get-tuple-element.32.own.refs_1_), channel_id=1, source_target_pairs={{0,2},{2,0},{4,6},{6,4},{8,10},{10,8},{12,14},{14,12},{1,3},{3,1},... | collective-permute-start | bytes 786440 | tf_op jit(solution)/shard_map/ppermute | solution.py:234
  5.0 1.3 %collective-permute-start.3 = (f32[2,2,64,256]{3,2,1,0:T(8,128)S(1)}, f32[2,2,64,256]{3,2,1,0:T(8,128)S(1)}, u32[]{:S(2)}, u32[]{:S(2)}) collective-permute-start(f32[2,2,64,256]{3,2,1,0:T(8,128)S(1)} %pad_maximum_fusion), channel_id=1, source_target_pairs={{2,6},{4,0},{6,10},{8,4},{10,14},{12,8},{3,7},{5,1},{7,11},{9,5},{... | collective-permute-start | bytes 786440 | tf_op jit(solution)/shard_map/ppermute | solution.py:247
  7.1 2.7 %collective-permute-start.4 = (f32[3,2,32,256]{3,2,1,0:T(8,128)}, f32[3,2,32,256]{3,2,1,0:T(8,128)S(1)}, u32[]{:S(2)}, u32[]{:S(2)}) collective-permute-start(f32[3,2,32,256]{3,2,1,0:T(8,128)} %pad_maximum_fusion.1), channel_id=1, source_target_pairs={{0,2},{2,0},{4,6},{6,4},{8,10},{10,8},{12,14},{14,12},{1,3},{3,1},... | collective-permute-start | bytes 589832 | tf_op jit(solution)/shard_map/ppermute | solution.py:234
  9.9 1.2 %shard_map.58 = (bf16[3,384,256]{2,1,0:T(8,128)(2,1)S(1)}, bf16[3,384,256]{2,1,0:T(8,128)(2,1)S(1)}, bf16[3,384,256]{2,1,0:T(8,128)(2,1)S(1)}, bf16[3,384,256]{2,1,0:T(8,128)(2,1)S(1)}, f32[8,128]{1,0:T(8,128)S(1)}) custom-call(s32[3]{0:T(128)S(1)} %pad_add_fusion.at.refs_0_, f32[27,128,128]{2,1,0:T(8,128)S(1)} %bitcast.15), custom_call_target="tpu_custom_call" | custom-call | tf_op jit(solution)/shard_map/pallas_call | solution.py:266
  11.1 1.1 %shard_map.59 = (f32[576,256]{1,0:T(8,128)S(1)}, bf16[256,256]{1,0:T(8,128)(2,1)S(1)}, bf16[256,256]{1,0:T(8,128)(2,1)S(1)}, bf16[192,256]{1,0:T(8,128)(2,1)S(1)...) custom-call(s32[3]{0:T(128)S(1)} %pad_add_fusion.at.refs_0_, f32[2,2,64,256]{3,2,1,0:T(8,128)S(1)} %get-tuple-element.32.own.refs_1_, ...), custom_call_target="tpu_custom_call" | custom-call | tf_op jit(solution)/shard_map/pallas_call | solution.py:275
  12.3 3.2 %collective-permute-done.4.g_pair.refs_5_ = f32[3,2,32,256]{3,2,1,0:T(8,128)S(1)} collective-permute-done((f32[3,2,32,256]{3,2,1,0:T(8,128)}, f32[3,2,32,256]{3,2,1,0:T(8,128)S(1)}, u32[]{:S(2)}, u32[]{:S(2)}) %collective-permute-start.4) | collective-permute-done | bytes 196640 | tf_op jit(solution)/shard_map/ppermute | solution.py:234
  15.6 1.6 %collective-permute-start.9 = (f32[2,2,64,256]{3,2,1,0:T(8,128)S(1)}, f32[2,2,64,256]{3,2,1,0:T(8,128)S(1)}, u32[]{:S(2)}, u32[]{:S(2)}) collective-permute-start(f32[2,2,64,256]{3,2,1,0:T(8,128)S(1)} %collective-permute-done.3.edge), channel_id=1, source_target_pairs={{0,2},{2,0},{4,6},{6,4},{8,10},{10,8},{12,14},{14,12},{1,3},{3,1},... | collective-permute-start | bytes 786440 | tf_op jit(solution)/shard_map/ppermute | solution.py:234
  17.2 1.6 %shard_map.60 = (f32[27,8,128]{2,1,0:T(8,128)S(1)}, f32[27,8,128]{2,1,0:T(8,128)S(1)}, f32[27,8,128]{2,1,0:T(8,128)S(1)}, f32[27,8,128]{2,1,0:T(8,128)S(1)}) custom-call(s32[3]{0:T(128)S(1)} %pad_add_fusion.at.refs_0_, f32[576,256]{1,0:T(8,128)S(1)} %get-tuple-element.35.acc, bf16[256,256]{1,0:T(8,128)(2,1)S(1)} %get-tuple-element.36.x1_hi, ...), custom_call_target="tpu_custom_call" | custom-call | tf_op jit(solution)/shard_map/pallas_call | solution.py:292
  18.8 1.6 %collective-permute-start.6 = (f32[27,8,128]{2,1,0:T(8,128)S(1)}, f32[27,8,128]{2,1,0:T(8,128)S(1)}, u32[]{:S(2)}, u32[]{:S(2)}) collective-permute-start(f32[27,8,128]{2,1,0:T(8,128)S(1)} %get-tuple-element.45), channel_id=1, source_target_pairs={{0,4},{2,6},{4,8},{6,10},{8,12},{10,14},{12,0},{14,2},{1,5},{3,7},... | collective-permute-start | bytes 331784 | tf_op jit(solution)/shard_map/ppermute | solution.py:238
  20.4 2.6 %collective-permute-start.7 = (f32[27,8,128]{2,1,0:T(8,128)S(1)}, f32[27,8,128]{2,1,0:T(8,128)S(1)}, u32[]{:S(2)}, u32[]{:S(2)}) collective-permute-start(f32[27,8,128]{2,1,0:T(8,128)S(1)} %get-tuple-element.46), channel_id=1, source_target_pairs={{0,8},{2,10},{4,12},{6,14},{8,0},{10,2},{12,4},{14,6},{1,9},{3,11}... | collective-permute-start | bytes 331784 | tf_op jit(solution)/shard_map/ppermute | solution.py:238
  23.0 1.3 %collective-permute-start.8 = (f32[27,8,128]{2,1,0:T(8,128)S(1)}, f32[27,8,128]{2,1,0:T(8,128)S(1)}, u32[]{:S(2)}, u32[]{:S(2)}) collective-permute-start(f32[27,8,128]{2,1,0:T(8,128)S(1)} %get-tuple-element.47), channel_id=1, source_target_pairs={{0,12},{2,14},{4,0},{6,2},{8,4},{10,6},{12,8},{14,10},{1,13},{3,15... | collective-permute-start | bytes 331784 | tf_op jit(solution)/shard_map/ppermute | solution.py:238
  24.4 2.3 %collective-permute-done.6.refs_2_ = f32[27,8,128]{2,1,0:T(8,128)S(1)} collective-permute-done((f32[27,8,128]{2,1,0:T(8,128)S(1)}, f32[27,8,128]{2,1,0:T(8,128)S(1)}, u32[]{:S(2)}, u32[]{:S(2)}) %collective-permute-start.6) | collective-permute-done | bytes 110624 | tf_op jit(solution)/shard_map/ppermute | solution.py:238
  26.6 4.1 %collective-permute-done.7.refs_3_ = f32[27,8,128]{2,1,0:T(8,128)S(1)} collective-permute-done((f32[27,8,128]{2,1,0:T(8,128)S(1)}, f32[27,8,128]{2,1,0:T(8,128)S(1)}, u32[]{:S(2)}, u32[]{:S(2)}) %collective-permute-start.7) | collective-permute-done | bytes 110624 | tf_op jit(solution)/shard_map/ppermute | solution.py:238
  31.8 1.9 %collective-permute-start.15 = (f32[27,8,128]{2,1,0:T(8,128)S(1)}, f32[27,8,128]{2,1,0:T(8,128)S(1)}, u32[]{:S(2)}, u32[]{:S(2)}) collective-permute-start(f32[27,8,128]{2,1,0:T(8,128)S(1)} %shard_map.61.refs_0_), channel_id=1, source_target_pairs={{0,8},{2,10},{4,12},{6,14},{8,0},{10,2},{12,4},{14,6},{1,9},{3,11}... | collective-permute-start | bytes 331784 | tf_op jit(solution)/shard_map/ppermute | solution.py:238
  33.7 3.4 %collective-permute-start.16 = (f32[27,8,128]{2,1,0:T(8,128)S(1)}, f32[27,8,128]{2,1,0:T(8,128)S(1)}, u32[]{:S(2)}, u32[]{:S(2)}) collective-permute-start(f32[27,8,128]{2,1,0:T(8,128)S(1)} %shard_map.61.refs_0_), channel_id=1, source_target_pairs={{0,12},{2,14},{4,0},{6,2},{8,4},{10,6},{12,8},{14,10},{1,13},{3,15... | collective-permute-start | bytes 331784 | tf_op jit(solution)/shard_map/ppermute | solution.py:238
  37.1 1.5 %collective-permute-start.14 = (f32[27,8,128]{2,1,0:T(8,128)S(1)}, f32[27,8,128]{2,1,0:T(8,128)S(1)}, u32[]{:S(2)}, u32[]{:S(2)}) collective-permute-start(f32[27,8,128]{2,1,0:T(8,128)S(1)} %shard_map.61.refs_0_), channel_id=1, source_target_pairs={{0,2},{2,0},{4,6},{6,4},{8,10},{10,8},{12,14},{14,12},{1,3},{3,1},... | collective-permute-start | bytes 331784 | tf_op jit(solution)/shard_map/ppermute | solution.py:234
  38.6 1.8 %shard_map.62 = f32[2,2,64,256]{3,2,1,0:T(8,128)S(1)} custom-call(s32[3]{0:T(128)S(1)} %pad_add_fusion.at.refs_0_, f32[2,2,64,256]{3,2,1,0:T(8,128)S(1)} %get-tuple-element.32.own.refs_1_, f32[2,2,64,256]{3,2,1,0:T(8,128)S(1)} %collective-permute-done.own2.refs_2_, f32[2,2,64,256]{3,2,1,0:T(8,128)S(1)} %collective-permute-done.1.pair.refs_3_, ...), custom_call_target="tpu_custom_call" | custom-call | tf_op jit(solution)/shard_map/pallas_call | solution.py:308
  41.1 1.4 %collective-permute-start.19 = (f32[27,8,128]{2,1,0:T(8,128)S(1)}, f32[27,8,128]{2,1,0:T(8,128)S(1)}, u32[]{:S(2)}, u32[]{:S(2)}) collective-permute-start(f32[27,8,128]{2,1,0:T(8,128)S(1)} %collective-permute-done.16.refs_3_), channel_id=1, source_target_pairs={{0,2},{2,0},{4,6},{6,4},{8,10},{10,8},{12,14},{14,12},{1,3},{3,1},... | collective-permute-start | bytes 331784 | tf_op jit(solution)/shard_map/ppermute | solution.py:234
  42.5 1.8 %shard_map.63 = f32[2,2,64,256]{3,2,1,0:T(8,128)S(1)} custom-call(s32[3]{0:T(128)S(1)} %pad_add_fusion.at.refs_0_, f32[2,2,64,256]{3,2,1,0:T(8,128)S(1)} %get-tuple-element.33.g_own.refs_1_, f32[2,2,64,256]{3,2,1,0:T(8,128)S(1)} %collective-permute-done.12.refs_2_, f32[2,2,64,256]{3,2,1,0:T(8,128)S(1)} %collective-permute-done.9.refs_5_.refs_3_, ...), custom_call_target="tpu_custom_call" | custom-call | tf_op jit(solution)/shard_map/pallas_call | solution.py:308
  44.9 1.4 %collective-permute-start.17 = (f32[27,8,128]{2,1,0:T(8,128)S(1)}, f32[27,8,128]{2,1,0:T(8,128)S(1)}, u32[]{:S(2)}, u32[]{:S(2)}) collective-permute-start(f32[27,8,128]{2,1,0:T(8,128)S(1)} %collective-permute-done.10.refs_1_), channel_id=1, source_target_pairs={{0,2},{2,0},{4,6},{6,4},{8,10},{10,8},{12,14},{14,12},{1,3},{3,1},... | collective-permute-start | bytes 331784 | tf_op jit(solution)/shard_map/ppermute | solution.py:234
  46.3 0.9 %copy.10 = f32[64,2,2,256]{3,2,1,0:T(2,128)} copy(f32[64,2,2,256]{3,0,2,1:T(8,128)S(1)} %bitcast.17) | data formatting | bytes 524288
  48.1 1.5 %collective-permute-done.17.refs_5_ = f32[27,8,128]{2,1,0:T(8,128)S(1)} collective-permute-done((f32[27,8,128]{2,1,0:T(8,128)S(1)}, f32[27,8,128]{2,1,0:T(8,128)S(1)}, u32[]{:S(2)}, u32[]{:S(2)}) %collective-permute-start.17) | collective-permute-done | bytes 110624 | tf_op jit(solution)/shard_map/ppermute | solution.py:234
  49.6 1.6 %shard_map.64 = f32[27,8,8,128]{3,2,1,0:T(8,128)} custom-call(s32[3]{0:T(128)S(1)} %pad_add_fusion.at.refs_0_, f32[27,8,128]{2,1,0:T(8,128)S(1)} %shard_map.61.refs_0_, f32[27,8,128]{2,1,0:T(8,128)S(1)} %collective-permute-done.10.refs_1_, f32[27,8,128]{2,1,0:T(8,128)S(1)} %collective-permute-done.15.refs_2_, ...), custom_call_target="tpu_custom_call" | custom-call | tf_op jit(solution)/shard_map/pallas_call | solution.py:351
  (35 shorter events, 4.3 us)
Async XLA Ops:
  0.6 9.2 %copy-start = (f32[128,27,128]{2,0,1:T(8,128)S(1)}, f32[128,27,128]{2,0,1:T(8,128)}, u32[]{:S(2)}) copy-start(f32[128,27,128]{2,0,1:T(8,128)} %param.4) | copy-start | bytes 5308420
  1.9 10.3 %collective-permute-start.1 = (f32[2,2,64,256]{3,2,1,0:T(8,128)S(1)}, f32[2,2,64,256]{3,2,1,0:T(8,128)S(1)}, u32[]{:S(2)}, u32[]{:S(2)}) collective-permute-start(f32[2,2,64,256]{3,2,1,0:T(8,128)S(1)} %get-tuple-element.32.own.refs_1_), channel_id=1, source_target_pairs={{0,2},{2,0},{4,6},{6,4},{8,10},{10,8},{12,14},{14,12},{1,3},{3,1},... | collective-permute-start | bytes 786440 | tf_op jit(solution)/shard_map/ppermute | solution.py:234
  4.9 6.1 %collective-permute-start = (f32[2,2,64,256]{3,2,1,0:T(8,128)S(1)}, f32[2,2,64,256]{3,2,1,0:T(8,128)S(1)}, u32[]{:S(2)}, u32[]{:S(2)}) collective-permute-start(f32[2,2,64,256]{3,2,1,0:T(8,128)S(1)} %get-tuple-element.32.own.refs_1_), channel_id=1, source_target_pairs={{0,1},{1,0},{2,3},{3,2},{4,5},{5,4},{6,7},{7,6},{8,9},{9,8},{10,11... | collective-permute-start | bytes 786440 | tf_op jit(solution)/shard_map/ppermute | solution.py:231
  5.0 10.6 %collective-permute-start.3 = (f32[2,2,64,256]{3,2,1,0:T(8,128)S(1)}, f32[2,2,64,256]{3,2,1,0:T(8,128)S(1)}, u32[]{:S(2)}, u32[]{:S(2)}) collective-permute-start(f32[2,2,64,256]{3,2,1,0:T(8,128)S(1)} %pad_maximum_fusion), channel_id=1, source_target_pairs={{2,6},{4,0},{6,10},{8,4},{10,14},{12,8},{3,7},{5,1},{7,11},{9,5},{... | collective-permute-start | bytes 786440 | tf_op jit(solution)/shard_map/ppermute | solution.py:247
  7.1 8.4 %collective-permute-start.4 = (f32[3,2,32,256]{3,2,1,0:T(8,128)}, f32[3,2,32,256]{3,2,1,0:T(8,128)S(1)}, u32[]{:S(2)}, u32[]{:S(2)}) collective-permute-start(f32[3,2,32,256]{3,2,1,0:T(8,128)} %pad_maximum_fusion.1), channel_id=1, source_target_pairs={{0,2},{2,0},{4,6},{6,4},{8,10},{10,8},{12,14},{14,12},{1,3},{3,1},... | collective-permute-start | bytes 589832 | tf_op jit(solution)/shard_map/ppermute | solution.py:234
  12.2 5.0 %collective-permute-start.2 = (f32[2,2,64,256]{3,2,1,0:T(8,128)S(1)}, f32[2,2,64,256]{3,2,1,0:T(8,128)S(1)}, u32[]{:S(2)}, u32[]{:S(2)}) collective-permute-start(f32[2,2,64,256]{3,2,1,0:T(8,128)S(1)} %collective-permute-done.1.pair.refs_3_), channel_id=1, source_target_pairs={{0,1},{1,0},{2,3},{3,2},{4,5},{5,4},{6,7},{7,6},{8,9},{9,8},{10,11... | collective-permute-start | bytes 786440 | tf_op jit(solution)/shard_map/ppermute | solution.py:231
  15.6 1.6 %collective-permute-start.5 = (f32[2,2,64,256]{3,2,1,0:T(8,128)S(1)}, f32[2,2,64,256]{3,2,1,0:T(8,128)S(1)}, u32[]{:S(2)}, u32[]{:S(2)}) collective-permute-start(f32[2,2,64,256]{3,2,1,0:T(8,128)S(1)} %collective-permute-done.3.edge), channel_id=1, source_target_pairs={{0,1},{1,0},{2,3},{3,2},{4,5},{5,4},{6,7},{7,6},{8,9},{9,8},{10,11... | collective-permute-start | bytes 786440 | tf_op jit(solution)/shard_map/ppermute | solution.py:231
  15.6 8.7 %collective-permute-start.9 = (f32[2,2,64,256]{3,2,1,0:T(8,128)S(1)}, f32[2,2,64,256]{3,2,1,0:T(8,128)S(1)}, u32[]{:S(2)}, u32[]{:S(2)}) collective-permute-start(f32[2,2,64,256]{3,2,1,0:T(8,128)S(1)} %collective-permute-done.3.edge), channel_id=1, source_target_pairs={{0,2},{2,0},{4,6},{6,4},{8,10},{10,8},{12,14},{14,12},{1,3},{3,1},... | collective-permute-start | bytes 786440 | tf_op jit(solution)/shard_map/ppermute | solution.py:234
  18.8 7.8 %collective-permute-start.6 = (f32[27,8,128]{2,1,0:T(8,128)S(1)}, f32[27,8,128]{2,1,0:T(8,128)S(1)}, u32[]{:S(2)}, u32[]{:S(2)}) collective-permute-start(f32[27,8,128]{2,1,0:T(8,128)S(1)} %get-tuple-element.45), channel_id=1, source_target_pairs={{0,4},{2,6},{4,8},{6,10},{8,12},{10,14},{12,0},{14,2},{1,5},{3,7},... | collective-permute-start | bytes 331784 | tf_op jit(solution)/shard_map/ppermute | solution.py:238
  20.4 10.3 %collective-permute-start.7 = (f32[27,8,128]{2,1,0:T(8,128)S(1)}, f32[27,8,128]{2,1,0:T(8,128)S(1)}, u32[]{:S(2)}, u32[]{:S(2)}) collective-permute-start(f32[27,8,128]{2,1,0:T(8,128)S(1)} %get-tuple-element.46), channel_id=1, source_target_pairs={{0,8},{2,10},{4,12},{6,14},{8,0},{10,2},{12,4},{14,6},{1,9},{3,11}... | collective-permute-start | bytes 331784 | tf_op jit(solution)/shard_map/ppermute | solution.py:238
  23.0 7.7 %collective-permute-start.8 = (f32[27,8,128]{2,1,0:T(8,128)S(1)}, f32[27,8,128]{2,1,0:T(8,128)S(1)}, u32[]{:S(2)}, u32[]{:S(2)}) collective-permute-start(f32[27,8,128]{2,1,0:T(8,128)S(1)} %get-tuple-element.47), channel_id=1, source_target_pairs={{0,12},{2,14},{4,0},{6,2},{8,4},{10,6},{12,8},{14,10},{1,13},{3,15... | collective-permute-start | bytes 331784 | tf_op jit(solution)/shard_map/ppermute | solution.py:238
  24.4 12.7 %collective-permute-start.12 = (f32[2,2,64,256]{3,2,1,0:T(8,128)S(1)}, f32[2,2,64,256]{3,2,1,0:T(8,128)S(1)}, u32[]{:S(2)}, u32[]{:S(2)}) collective-permute-start(f32[2,2,64,256]{3,2,1,0:T(8,128)S(1)} %get-tuple-element.33.g_own.refs_1_), channel_id=1, source_target_pairs={{0,1},{1,0},{2,3},{3,2},{4,5},{5,4},{6,7},{7,6},{8,9},{9,8},{10,11... | collective-permute-start | bytes 786440 | tf_op jit(solution)/shard_map/ppermute | solution.py:231
  30.7 6.4 %collective-permute-start.11 = (f32[2,2,64,256]{3,2,1,0:T(8,128)S(1)}, f32[2,2,64,256]{3,2,1,0:T(8,128)S(1)}, u32[]{:S(2)}, u32[]{:S(2)}) collective-permute-start(f32[2,2,64,256]{3,2,1,0:T(8,128)S(1)} %collective-permute-done.9.refs_5_.refs_3_), channel_id=1, source_target_pairs={{0,1},{1,0},{2,3},{3,2},{4,5},{5,4},{6,7},{7,6},{8,9},{9,8},{10,11... | collective-permute-start | bytes 786440 | tf_op jit(solution)/shard_map/ppermute | solution.py:231
  30.7 11.8 %collective-permute-start.13 = (f32[3,2,32,256]{3,2,1,0:T(8,128)S(1)}, f32[3,2,32,256]{3,2,1,0:T(8,128)S(1)}, u32[]{:S(2)}, u32[]{:S(2)}) collective-permute-start(f32[3,2,32,256]{3,2,1,0:T(8,128)S(1)} %collective-permute-done.4.g_pair.refs_5_), channel_id=1, source_target_pairs={{0,1},{1,0},{2,3},{3,2},{4,5},{5,4},{6,7},{7,6},{8,9},{9,8},{10,11... | collective-permute-start | bytes 589832 | tf_op jit(solution)/shard_map/ppermute | solution.py:231
  31.8 8.6 %collective-permute-start.15 = (f32[27,8,128]{2,1,0:T(8,128)S(1)}, f32[27,8,128]{2,1,0:T(8,128)S(1)}, u32[]{:S(2)}, u32[]{:S(2)}) collective-permute-start(f32[27,8,128]{2,1,0:T(8,128)S(1)} %shard_map.61.refs_0_), channel_id=1, source_target_pairs={{0,8},{2,10},{4,12},{6,14},{8,0},{10,2},{12,4},{14,6},{1,9},{3,11}... | collective-permute-start | bytes 331784 | tf_op jit(solution)/shard_map/ppermute | solution.py:238
  33.7 7.4 %collective-permute-start.16 = (f32[27,8,128]{2,1,0:T(8,128)S(1)}, f32[27,8,128]{2,1,0:T(8,128)S(1)}, u32[]{:S(2)}, u32[]{:S(2)}) collective-permute-start(f32[27,8,128]{2,1,0:T(8,128)S(1)} %shard_map.61.refs_0_), channel_id=1, source_target_pairs={{0,12},{2,14},{4,0},{6,2},{8,4},{10,6},{12,8},{14,10},{1,13},{3,15... | collective-permute-start | bytes 331784 | tf_op jit(solution)/shard_map/ppermute | solution.py:238
  37.1 7.8 %collective-permute-start.10 = (f32[27,8,128]{2,1,0:T(8,128)S(1)}, f32[27,8,128]{2,1,0:T(8,128)S(1)}, u32[]{:S(2)}, u32[]{:S(2)}) collective-permute-start(f32[27,8,128]{2,1,0:T(8,128)S(1)} %shard_map.61.refs_0_), channel_id=1, source_target_pairs={{0,4},{2,6},{4,8},{6,10},{8,12},{10,14},{12,0},{14,2},{1,5},{3,7},... | collective-permute-start | bytes 331784 | tf_op jit(solution)/shard_map/ppermute | solution.py:238
  37.1 7.8 %collective-permute-start.14 = (f32[27,8,128]{2,1,0:T(8,128)S(1)}, f32[27,8,128]{2,1,0:T(8,128)S(1)}, u32[]{:S(2)}, u32[]{:S(2)}) collective-permute-start(f32[27,8,128]{2,1,0:T(8,128)S(1)} %shard_map.61.refs_0_), channel_id=1, source_target_pairs={{0,2},{2,0},{4,6},{6,4},{8,10},{10,8},{12,14},{14,12},{1,3},{3,1},... | collective-permute-start | bytes 331784 | tf_op jit(solution)/shard_map/ppermute | solution.py:234
  40.4 7.7 %collective-permute-start.18 = (f32[27,8,128]{2,1,0:T(8,128)S(1)}, f32[27,8,128]{2,1,0:T(8,128)S(1)}, u32[]{:S(2)}, u32[]{:S(2)}) collective-permute-start(f32[27,8,128]{2,1,0:T(8,128)S(1)} %collective-permute-done.15.refs_2_), channel_id=1, source_target_pairs={{0,2},{2,0},{4,6},{6,4},{8,10},{10,8},{12,14},{14,12},{1,3},{3,1},... | collective-permute-start | bytes 331784 | tf_op jit(solution)/shard_map/ppermute | solution.py:234
  41.1 7.0 %collective-permute-start.19 = (f32[27,8,128]{2,1,0:T(8,128)S(1)}, f32[27,8,128]{2,1,0:T(8,128)S(1)}, u32[]{:S(2)}, u32[]{:S(2)}) collective-permute-start(f32[27,8,128]{2,1,0:T(8,128)S(1)} %collective-permute-done.16.refs_3_), channel_id=1, source_target_pairs={{0,2},{2,0},{4,6},{6,4},{8,10},{10,8},{12,14},{14,12},{1,3},{3,1},... | collective-permute-start | bytes 331784 | tf_op jit(solution)/shard_map/ppermute | solution.py:234
  44.9 4.7 %collective-permute-start.17 = (f32[27,8,128]{2,1,0:T(8,128)S(1)}, f32[27,8,128]{2,1,0:T(8,128)S(1)}, u32[]{:S(2)}, u32[]{:S(2)}) collective-permute-start(f32[27,8,128]{2,1,0:T(8,128)S(1)} %collective-permute-done.10.refs_1_), channel_id=1, source_target_pairs={{0,2},{2,0},{4,6},{6,4},{8,10},{10,8},{12,14},{14,12},{1,3},{3,1},... | collective-permute-start | bytes 331784 | tf_op jit(solution)/shard_map/ppermute | solution.py:234

commit v5 on v4

--- a/solution.py
+++ b/solution.py
@@ -302,7 +302,6 @@
     got = [parts[0]] + [shift(parts[k], k) for k in range(1, count)]
     *got, late = lax.optimization_barrier((*got, late))
     late2 = swap_chan(late)
-    g_pair2 = swap_chan(g_pair)
 
     def conv(places, *operands):
         return call(
@@ -336,12 +335,14 @@
         quarters,
     )
     outputs = conv(x_places, x_own, x_own2, x_pair, x_pair2, late, late2, a_hi, a_lo)
-    in_grad = conv(g_places, g_own, g_own2, late, late2, g_pair, g_pair2, b_hi, b_lo)
     outputs = outputs.transpose(2, 0, 1, 3)
-    in_grad = in_grad.transpose(2, 0, 1, 3)
     cells = inputs.shape[1] * ring * inputs.shape[2] * width
     scale = float(1.0 / cells**0.5)
     shard = call(lambda *refs: sum_kernel(scale, *refs), chunk, count)(at, *got)
+    shard, g_pair = lax.optimization_barrier((shard, g_pair))
+    g_pair2 = swap_chan(g_pair)
+    in_grad = conv(g_places, g_own, g_own2, late, late2, g_pair, g_pair2, b_hi, b_lo)
+    in_grad = in_grad.transpose(2, 0, 1, 3)
     mine = [shard] + [shift(shard, k) for k in range(1, count)]
     theirs = [swap_side(shard)]
     mine[1], outputs, in_grad, theirs[0] = lax.optimization_barrier(

time: 51.7 us -> 51.8 us (level)
  no operation moved by 1% of the time
where the time goes in v5:
time: 51.8 us; the launch traced here: 51.3 us
  starting transfers between devices  25.1 us (48%)
  waiting for transfers between devices  11.8 us (23%)
  Pallas kernels  9.66 us (19%)
  local copies, waits for them, and re-layouts  3.14 us (6%)
  between operations  0.81 us (2%)
  other arithmetic  0.79 us (2%)
    ppermute x7, starting transfers between devices, swap_side(): return lax.ppermute(value, 'space', [(i, i ^ 1) for i in range(ring)])  12.4 us
    ppermute x6, starting transfers between devices, shift(): return lax.ppermute(value, 'space', pairs)  10.8 us
    ppermute x6, waiting for transfers between devices, shift(): return lax.ppermute(value, 'space', pairs)  6.94 us
    ppermute x7, waiting for transfers between devices, swap_side(): return lax.ppermute(value, 'space', [(i, i ^ 1) for i in range(ring)])  4.68 us
    pallas_call x2, Pallas kernels, conv(): call(lambda *refs: conv_kernel(places, *refs), jax.ShapeDtypeStruct((2, 2...  3.64 us
    unnamed x5, local copies, waits for them, and re-layouts  3.08 us
    pallas_call x1, Pallas kernels, local(): call(join_kernel, jax.ShapeDtypeStruct((27, half // 8, 8, full), F32), 2...  1.57 us
    pallas_call x1, Pallas kernels, local(): call(filter_kernel, [chunk] * count, 11, [pltpu.VMEM((3, 2 * full, width)...  1.57 us
  transfers between devices with their start and end apart: 20, of which 6 were waited for; matrix products, arithmetic and copies ran while one was open for 5% of the time, Pallas kernels for 16%

profile of v5, /device:TPU:0, one launch (start us, length us, event | category | flops | bytes accessed | tf_op | source)
XLA Modules:
  0.0 51.3 jit_solution(13449407446087633340)
XLA Ops:
  0.6 1.3 %fusion = (f32[64,2,2,256]{3,0,2,1:T(8,128)S(1)}, f32[2,2,64,256]{3,2,1,0:T(8,128)S(1)}, f32[2,2,64,256]{3,2,1,0:T(8,128)S(1)}) fusion(f32[64,2,2,256]{3,2,1,0:T(2,128)} %param.3, f32[64,2,2,256]{3,2,1,0:T(2,128)} %param.5), kind=kLoop, calls=%fused_computation.9 | loop fusion | bytes 1310720 | tf_op args[0]
  1.9 3.0 %collective-permute-start.1 = (f32[2,2,64,256]{3,2,1,0:T(8,128)S(1)}, f32[2,2,64,256]{3,2,1,0:T(8,128)S(1)}, u32[]{:S(2)}, u32[]{:S(2)}) collective-permute-start(f32[2,2,64,256]{3,2,1,0:T(8,128)S(1)} %get-tuple-element.34.own.refs_1_), channel_id=1, source_target_pairs={{0,2},{2,0},{4,6},{6,4},{8,10},{10,8},{12,14},{14,12},{1,3},{3,1},... | collective-permute-start | bytes 786440 | tf_op jit(solution)/shard_map/ppermute | solution.py:234
  5.0 1.3 %collective-permute-start.3 = (f32[2,2,64,256]{3,2,1,0:T(8,128)S(1)}, f32[2,2,64,256]{3,2,1,0:T(8,128)S(1)}, u32[]{:S(2)}, u32[]{:S(2)}) collective-permute-start(f32[2,2,64,256]{3,2,1,0:T(8,128)S(1)} %pad_maximum_fusion), channel_id=1, source_target_pairs={{2,6},{4,0},{6,10},{8,4},{10,14},{12,8},{3,7},{5,1},{7,11},{9,5},{... | collective-permute-start | bytes 786440 | tf_op jit(solution)/shard_map/ppermute | solution.py:247
  7.1 2.7 %collective-permute-start.4 = (f32[3,2,32,256]{3,2,1,0:T(8,128)}, f32[3,2,32,256]{3,2,1,0:T(8,128)S(1)}, u32[]{:S(2)}, u32[]{:S(2)}) collective-permute-start(f32[3,2,32,256]{3,2,1,0:T(8,128)} %pad_maximum_fusion.1), channel_id=1, source_target_pairs={{0,2},{2,0},{4,6},{6,4},{8,10},{10,8},{12,14},{14,12},{1,3},{3,1},... | collective-permute-start | bytes 589832 | tf_op jit(solution)/shard_map/ppermute | solution.py:234
  9.9 1.2 %shard_map.58 = (bf16[3,384,256]{2,1,0:T(8,128)(2,1)S(1)}, bf16[3,384,256]{2,1,0:T(8,128)(2,1)S(1)}, bf16[3,384,256]{2,1,0:T(8,128)(2,1)S(1)}, bf16[3,384,256]{2,1,0:T(8,128)(2,1)S(1)}, f32[8,128]{1,0:T(8,128)S(1)}) custom-call(s32[3]{0:T(128)S(1)} %pad_add_fusion.at.refs_0_, f32[27,128,128]{2,1,0:T(8,128)S(1)} %bitcast.15), custom_call_target="tpu_custom_call" | custom-call | tf_op jit(solution)/shard_map/pallas_call | solution.py:266
  11.1 1.1 %shard_map.59 = (f32[576,256]{1,0:T(8,128)S(1)}, bf16[256,256]{1,0:T(8,128)(2,1)S(1)}, bf16[256,256]{1,0:T(8,128)(2,1)S(1)}, bf16[192,256]{1,0:T(8,128)(2,1)S(1)...) custom-call(s32[3]{0:T(128)S(1)} %pad_add_fusion.at.refs_0_, f32[2,2,64,256]{3,2,1,0:T(8,128)S(1)} %get-tuple-element.34.own.refs_1_, ...), custom_call_target="tpu_custom_call" | custom-call | tf_op jit(solution)/shard_map/pallas_call | solution.py:275
  12.3 3.2 %collective-permute-done.4.g_pair.refs_5_ = f32[3,2,32,256]{3,2,1,0:T(8,128)S(1)} collective-permute-done((f32[3,2,32,256]{3,2,1,0:T(8,128)}, f32[3,2,32,256]{3,2,1,0:T(8,128)S(1)}, u32[]{:S(2)}, u32[]{:S(2)}) %collective-permute-start.4) | collective-permute-done | bytes 196640 | tf_op jit(solution)/shard_map/ppermute | solution.py:234
  15.6 1.6 %collective-permute-start.9 = (f32[2,2,64,256]{3,2,1,0:T(8,128)S(1)}, f32[2,2,64,256]{3,2,1,0:T(8,128)S(1)}, u32[]{:S(2)}, u32[]{:S(2)}) collective-permute-start(f32[2,2,64,256]{3,2,1,0:T(8,128)S(1)} %collective-permute-done.3.edge), channel_id=1, source_target_pairs={{0,2},{2,0},{4,6},{6,4},{8,10},{10,8},{12,14},{14,12},{1,3},{3,1},... | collective-permute-start | bytes 786440 | tf_op jit(solution)/shard_map/ppermute | solution.py:234
  17.2 1.6 %shard_map.60 = (f32[27,8,128]{2,1,0:T(8,128)S(1)}, f32[27,8,128]{2,1,0:T(8,128)S(1)}, f32[27,8,128]{2,1,0:T(8,128)S(1)}, f32[27,8,128]{2,1,0:T(8,128)S(1)}) custom-call(s32[3]{0:T(128)S(1)} %pad_add_fusion.at.refs_0_, f32[576,256]{1,0:T(8,128)S(1)} %get-tuple-element.37.acc, bf16[256,256]{1,0:T(8,128)(2,1)S(1)} %get-tuple-element.38.x1_hi, ...), custom_call_target="tpu_custom_call" | custom-call | tf_op jit(solution)/shard_map/pallas_call | solution.py:292
  18.8 1.6 %collective-permute-start.6 = (f32[27,8,128]{2,1,0:T(8,128)S(1)}, f32[27,8,128]{2,1,0:T(8,128)S(1)}, u32[]{:S(2)}, u32[]{:S(2)}) collective-permute-start(f32[27,8,128]{2,1,0:T(8,128)S(1)} %get-tuple-element.47), channel_id=1, source_target_pairs={{0,4},{2,6},{4,8},{6,10},{8,12},{10,14},{12,0},{14,2},{1,5},{3,7},... | collective-permute-start | bytes 331784 | tf_op jit(solution)/shard_map/ppermute | solution.py:238
  20.4 2.6 %collective-permute-start.7 = (f32[27,8,128]{2,1,0:T(8,128)S(1)}, f32[27,8,128]{2,1,0:T(8,128)S(1)}, u32[]{:S(2)}, u32[]{:S(2)}) collective-permute-start(f32[27,8,128]{2,1,0:T(8,128)S(1)} %get-tuple-element.48), channel_id=1, source_target_pairs={{0,8},{2,10},{4,12},{6,14},{8,0},{10,2},{12,4},{14,6},{1,9},{3,11}... | collective-permute-start | bytes 331784 | tf_op jit(solution)/shard_map/ppermute | solution.py:238
  23.0 1.3 %collective-permute-start.8 = (f32[27,8,128]{2,1,0:T(8,128)S(1)}, f32[27,8,128]{2,1,0:T(8,128)S(1)}, u32[]{:S(2)}, u32[]{:S(2)}) collective-permute-start(f32[27,8,128]{2,1,0:T(8,128)S(1)} %get-tuple-element.49), channel_id=1, source_target_pairs={{0,12},{2,14},{4,0},{6,2},{8,4},{10,6},{12,8},{14,10},{1,13},{3,15... | collective-permute-start | bytes 331784 | tf_op jit(solution)/shard_map/ppermute | solution.py:238
  24.4 2.3 %collective-permute-done.6.refs_2_ = f32[27,8,128]{2,1,0:T(8,128)S(1)} collective-permute-done((f32[27,8,128]{2,1,0:T(8,128)S(1)}, f32[27,8,128]{2,1,0:T(8,128)S(1)}, u32[]{:S(2)}, u32[]{:S(2)}) %collective-permute-start.6) | collective-permute-done | bytes 110624 | tf_op jit(solution)/shard_map/ppermute | solution.py:238
  26.6 4.1 %collective-permute-done.7.refs_3_ = f32[27,8,128]{2,1,0:T(8,128)S(1)} collective-permute-done((f32[27,8,128]{2,1,0:T(8,128)S(1)}, f32[27,8,128]{2,1,0:T(8,128)S(1)}, u32[]{:S(2)}, u32[]{:S(2)}) %collective-permute-start.7) | collective-permute-done | bytes 110624 | tf_op jit(solution)/shard_map/ppermute | solution.py:238
  31.9 1.8 %collective-permute-start.15 = (f32[27,8,128]{2,1,0:T(8,128)S(1)}, f32[27,8,128]{2,1,0:T(8,128)S(1)}, u32[]{:S(2)}, u32[]{:S(2)}) collective-permute-start(f32[27,8,128]{2,1,0:T(8,128)S(1)} %shard_map.61.refs_0_), channel_id=1, source_target_pairs={{0,8},{2,10},{4,12},{6,14},{8,0},{10,2},{12,4},{14,6},{1,9},{3,11}... | collective-permute-start | bytes 331784 | tf_op jit(solution)/shard_map/ppermute | solution.py:238
  33.7 3.4 %collective-permute-start.16 = (f32[27,8,128]{2,1,0:T(8,128)S(1)}, f32[27,8,128]{2,1,0:T(8,128)S(1)}, u32[]{:S(2)}, u32[]{:S(2)}) collective-permute-start(f32[27,8,128]{2,1,0:T(8,128)S(1)} %shard_map.61.refs_0_), channel_id=1, source_target_pairs={{0,12},{2,14},{4,0},{6,2},{8,4},{10,6},{12,8},{14,10},{1,13},{3,15... | collective-permute-start | bytes 331784 | tf_op jit(solution)/shard_map/ppermute | solution.py:238
  37.1 1.5 %collective-permute-start.14 = (f32[27,8,128]{2,1,0:T(8,128)S(1)}, f32[27,8,128]{2,1,0:T(8,128)S(1)}, u32[]{:S(2)}, u32[]{:S(2)}) collective-permute-start(f32[27,8,128]{2,1,0:T(8,128)S(1)} %shard_map.61.refs_0_), channel_id=1, source_target_pairs={{0,2},{2,0},{4,6},{6,4},{8,10},{10,8},{12,14},{14,12},{1,3},{3,1},... | collective-permute-start | bytes 331784 | tf_op jit(solution)/shard_map/ppermute | solution.py:234
  38.6 1.8 %shard_map.62 = f32[2,2,64,256]{3,2,1,0:T(8,128)S(1)} custom-call(s32[3]{0:T(128)S(1)} %pad_add_fusion.at.refs_0_, f32[2,2,64,256]{3,2,1,0:T(8,128)S(1)} %get-tuple-element.34.own.refs_1_, f32[2,2,64,256]{3,2,1,0:T(8,128)S(1)} %collective-permute-done.own2.refs_2_, f32[2,2,64,256]{3,2,1,0:T(8,128)S(1)} %collective-permute-done.1.pair.refs_3_, ...), custom_call_target="tpu_custom_call" | custom-call | tf_op jit(solution)/shard_map/pallas_call | solution.py:307
  41.1 1.4 %collective-permute-start.19 = (f32[27,8,128]{2,1,0:T(8,128)S(1)}, f32[27,8,128]{2,1,0:T(8,128)S(1)}, u32[]{:S(2)}, u32[]{:S(2)}) collective-permute-start(f32[27,8,128]{2,1,0:T(8,128)S(1)} %collective-permute-done.16.refs_3_), channel_id=1, source_target_pairs={{0,2},{2,0},{4,6},{6,4},{8,10},{10,8},{12,14},{14,12},{1,3},{3,1},... | collective-permute-start | bytes 331784 | tf_op jit(solution)/shard_map/ppermute | solution.py:234
  42.5 1.8 %shard_map.63 = f32[2,2,64,256]{3,2,1,0:T(8,128)S(1)} custom-call(s32[3]{0:T(128)S(1)} %pad_add_fusion.at.refs_0_, f32[2,2,64,256]{3,2,1,0:T(8,128)S(1)} %get-tuple-element.35.g_own.refs_1_, f32[2,2,64,256]{3,2,1,0:T(8,128)S(1)} %collective-permute-done.12.refs_2_, f32[2,2,64,256]{3,2,1,0:T(8,128)S(1)} %collective-permute-done.9.refs_5_.refs_3_, ...), custom_call_target="tpu_custom_call" | custom-call | tf_op jit(solution)/shard_map/pallas_call | solution.py:307
  44.9 1.4 %collective-permute-start.17 = (f32[27,8,128]{2,1,0:T(8,128)S(1)}, f32[27,8,128]{2,1,0:T(8,128)S(1)}, u32[]{:S(2)}, u32[]{:S(2)}) collective-permute-start(f32[27,8,128]{2,1,0:T(8,128)S(1)} %collective-permute-done.10.refs_1_), channel_id=1, source_target_pairs={{0,2},{2,0},{4,6},{6,4},{8,10},{10,8},{12,14},{14,12},{1,3},{3,1},... | collective-permute-start | bytes 331784 | tf_op jit(solution)/shard_map/ppermute | solution.py:234
  46.4 0.9 %copy.10 = f32[64,2,2,256]{3,2,1,0:T(2,128)} copy(f32[64,2,2,256]{3,0,2,1:T(8,128)S(1)} %bitcast.17) | data formatting | bytes 524288
  48.2 1.5 %collective-permute-done.17.refs_5_ = f32[27,8,128]{2,1,0:T(8,128)S(1)} collective-permute-done((f32[27,8,128]{2,1,0:T(8,128)S(1)}, f32[27,8,128]{2,1,0:T(8,128)S(1)}, u32[]{:S(2)}, u32[]{:S(2)}) %collective-permute-start.17) | collective-permute-done | bytes 110624 | tf_op jit(solution)/shard_map/ppermute | solution.py:234
  49.7 1.6 %shard_map.64 = f32[27,8,8,128]{3,2,1,0:T(8,128)} custom-call(s32[3]{0:T(128)S(1)} %pad_add_fusion.at.refs_0_, f32[27,8,128]{2,1,0:T(8,128)S(1)} %shard_map.61.refs_0_, f32[27,8,128]{2,1,0:T(8,128)S(1)} %collective-permute-done.10.refs_1_, f32[27,8,128]{2,1,0:T(8,128)S(1)} %collective-permute-done.15.refs_2_, ...), custom_call_target="tpu_custom_call" | custom-call | tf_op jit(solution)/shard_map/pallas_call | solution.py:352
  (35 shorter events, 4.4 us)
Async XLA Ops:
  0.6 9.2 %copy-start = (f32[128,27,128]{2,0,1:T(8,128)S(1)}, f32[128,27,128]{2,0,1:T(8,128)}, u32[]{:S(2)}) copy-start(f32[128,27,128]{2,0,1:T(8,128)} %param.4) | copy-start | bytes 5308420
  1.9 10.3 %collective-permute-start.1 = (f32[2,2,64,256]{3,2,1,0:T(8,128)S(1)}, f32[2,2,64,256]{3,2,1,0:T(8,128)S(1)}, u32[]{:S(2)}, u32[]{:S(2)}) collective-permute-start(f32[2,2,64,256]{3,2,1,0:T(8,128)S(1)} %get-tuple-element.34.own.refs_1_), channel_id=1, source_target_pairs={{0,2},{2,0},{4,6},{6,4},{8,10},{10,8},{12,14},{14,12},{1,3},{3,1},... | collective-permute-start | bytes 786440 | tf_op jit(solution)/shard_map/ppermute | solution.py:234
  4.9 6.1 %collective-permute-start = (f32[2,2,64,256]{3,2,1,0:T(8,128)S(1)}, f32[2,2,64,256]{3,2,1,0:T(8,128)S(1)}, u32[]{:S(2)}, u32[]{:S(2)}) collective-permute-start(f32[2,2,64,256]{3,2,1,0:T(8,128)S(1)} %get-tuple-element.34.own.refs_1_), channel_id=1, source_target_pairs={{0,1},{1,0},{2,3},{3,2},{4,5},{5,4},{6,7},{7,6},{8,9},{9,8},{10,11... | collective-permute-start | bytes 786440 | tf_op jit(solution)/shard_map/ppermute | solution.py:231
  5.0 10.6 %collective-permute-start.3 = (f32[2,2,64,256]{3,2,1,0:T(8,128)S(1)}, f32[2,2,64,256]{3,2,1,0:T(8,128)S(1)}, u32[]{:S(2)}, u32[]{:S(2)}) collective-permute-start(f32[2,2,64,256]{3,2,1,0:T(8,128)S(1)} %pad_maximum_fusion), channel_id=1, source_target_pairs={{2,6},{4,0},{6,10},{8,4},{10,14},{12,8},{3,7},{5,1},{7,11},{9,5},{... | collective-permute-start | bytes 786440 | tf_op jit(solution)/shard_map/ppermute | solution.py:247
  7.1 8.4 %collective-permute-start.4 = (f32[3,2,32,256]{3,2,1,0:T(8,128)}, f32[3,2,32,256]{3,2,1,0:T(8,128)S(1)}, u32[]{:S(2)}, u32[]{:S(2)}) collective-permute-start(f32[3,2,32,256]{3,2,1,0:T(8,128)} %pad_maximum_fusion.1), channel_id=1, source_target_pairs={{0,2},{2,0},{4,6},{6,4},{8,10},{10,8},{12,14},{14,12},{1,3},{3,1},... | collective-permute-start | bytes 589832 | tf_op jit(solution)/shard_map/ppermute | solution.py:234
  12.2 5.0 %collective-permute-start.2 = (f32[2,2,64,256]{3,2,1,0:T(8,128)S(1)}, f32[2,2,64,256]{3,2,1,0:T(8,128)S(1)}, u32[]{:S(2)}, u32[]{:S(2)}) collective-permute-start(f32[2,2,64,256]{3,2,1,0:T(8,128)S(1)} %collective-permute-done.1.pair.refs_3_), channel_id=1, source_target_pairs={{0,1},{1,0},{2,3},{3,2},{4,5},{5,4},{6,7},{7,6},{8,9},{9,8},{10,11... | collective-permute-start | bytes 786440 | tf_op jit(solution)/shard_map/ppermute | solution.py:231
  15.6 1.6 %collective-permute-start.5 = (f32[2,2,64,256]{3,2,1,0:T(8,128)S(1)}, f32[2,2,64,256]{3,2,1,0:T(8,128)S(1)}, u32[]{:S(2)}, u32[]{:S(2)}) collective-permute-start(f32[2,2,64,256]{3,2,1,0:T(8,128)S(1)} %collective-permute-done.3.edge), channel_id=1, source_target_pairs={{0,1},{1,0},{2,3},{3,2},{4,5},{5,4},{6,7},{7,6},{8,9},{9,8},{10,11... | collective-permute-start | bytes 786440 | tf_op jit(solution)/shard_map/ppermute | solution.py:231
  15.6 8.7 %collective-permute-start.9 = (f32[2,2,64,256]{3,2,1,0:T(8,128)S(1)}, f32[2,2,64,256]{3,2,1,0:T(8,128)S(1)}, u32[]{:S(2)}, u32[]{:S(2)}) collective-permute-start(f32[2,2,64,256]{3,2,1,0:T(8,128)S(1)} %collective-permute-done.3.edge), channel_id=1, source_target_pairs={{0,2},{2,0},{4,6},{6,4},{8,10},{10,8},{12,14},{14,12},{1,3},{3,1},... | collective-permute-start | bytes 786440 | tf_op jit(solution)/shard_map/ppermute | solution.py:234
  18.8 7.8 %collective-permute-start.6 = (f32[27,8,128]{2,1,0:T(8,128)S(1)}, f32[27,8,128]{2,1,0:T(8,128)S(1)}, u32[]{:S(2)}, u32[]{:S(2)}) collective-permute-start(f32[27,8,128]{2,1,0:T(8,128)S(1)} %get-tuple-element.47), channel_id=1, source_target_pairs={{0,4},{2,6},{4,8},{6,10},{8,12},{10,14},{12,0},{14,2},{1,5},{3,7},... | collective-permute-start | bytes 331784 | tf_op jit(solution)/shard_map/ppermute | solution.py:238
  20.4 10.3 %collective-permute-start.7 = (f32[27,8,128]{2,1,0:T(8,128)S(1)}, f32[27,8,128]{2,1,0:T(8,128)S(1)}, u32[]{:S(2)}, u32[]{:S(2)}) collective-permute-start(f32[27,8,128]{2,1,0:T(8,128)S(1)} %get-tuple-element.48), channel_id=1, source_target_pairs={{0,8},{2,10},{4,12},{6,14},{8,0},{10,2},{12,4},{14,6},{1,9},{3,11}... | collective-permute-start | bytes 331784 | tf_op jit(solution)/shard_map/ppermute | solution.py:238
  23.0 7.7 %collective-permute-start.8 = (f32[27,8,128]{2,1,0:T(8,128)S(1)}, f32[27,8,128]{2,1,0:T(8,128)S(1)}, u32[]{:S(2)}, u32[]{:S(2)}) collective-permute-start(f32[27,8,128]{2,1,0:T(8,128)S(1)} %get-tuple-element.49), channel_id=1, source_target_pairs={{0,12},{2,14},{4,0},{6,2},{8,4},{10,6},{12,8},{14,10},{1,13},{3,15... | collective-permute-start | bytes 331784 | tf_op jit(solution)/shard_map/ppermute | solution.py:238
  24.4 12.7 %collective-permute-start.12 = (f32[2,2,64,256]{3,2,1,0:T(8,128)S(1)}, f32[2,2,64,256]{3,2,1,0:T(8,128)S(1)}, u32[]{:S(2)}, u32[]{:S(2)}) collective-permute-start(f32[2,2,64,256]{3,2,1,0:T(8,128)S(1)} %get-tuple-element.35.g_own.refs_1_), channel_id=1, source_target_pairs={{0,1},{1,0},{2,3},{3,2},{4,5},{5,4},{6,7},{7,6},{8,9},{9,8},{10,11... | collective-permute-start | bytes 786440 | tf_op jit(solution)/shard_map/ppermute | solution.py:231
  30.7 6.4 %collective-permute-start.11 = (f32[2,2,64,256]{3,2,1,0:T(8,128)S(1)}, f32[2,2,64,256]{3,2,1,0:T(8,128)S(1)}, u32[]{:S(2)}, u32[]{:S(2)}) collective-permute-start(f32[2,2,64,256]{3,2,1,0:T(8,128)S(1)} %collective-permute-done.9.refs_5_.refs_3_), channel_id=1, source_target_pairs={{0,1},{1,0},{2,3},{3,2},{4,5},{5,4},{6,7},{7,6},{8,9},{9,8},{10,11... | collective-permute-start | bytes 786440 | tf_op jit(solution)/shard_map/ppermute | solution.py:231
  31.3 11.2 %collective-permute-start.13 = (f32[3,2,32,256]{3,2,1,0:T(8,128)S(1)}, f32[3,2,32,256]{3,2,1,0:T(8,128)S(1)}, u32[]{:S(2)}, u32[]{:S(2)}) collective-permute-start(f32[3,2,32,256]{3,2,1,0:T(8,128)S(1)} %collective-permute-done.4.g_pair.refs_5_), channel_id=1, source_target_pairs={{0,1},{1,0},{2,3},{3,2},{4,5},{5,4},{6,7},{7,6},{8,9},{9,8},{10,11... | collective-permute-start | bytes 589832 | tf_op jit(solution)/shard_map/ppermute | solution.py:231
  31.9 8.5 %collective-permute-start.15 = (f32[27,8,128]{2,1,0:T(8,128)S(1)}, f32[27,8,128]{2,1,0:T(8,128)S(1)}, u32[]{:S(2)}, u32[]{:S(2)}) collective-permute-start(f32[27,8,128]{2,1,0:T(8,128)S(1)} %shard_map.61.refs_0_), channel_id=1, source_target_pairs={{0,8},{2,10},{4,12},{6,14},{8,0},{10,2},{12,4},{14,6},{1,9},{3,11}... | collective-permute-start | bytes 331784 | tf_op jit(solution)/shard_map/ppermute | solution.py:238
  33.7 7.4 %collective-permute-start.16 = (f32[27,8,128]{2,1,0:T(8,128)S(1)}, f32[27,8,128]{2,1,0:T(8,128)S(1)}, u32[]{:S(2)}, u32[]{:S(2)}) collective-permute-start(f32[27,8,128]{2,1,0:T(8,128)S(1)} %shard_map.61.refs_0_), channel_id=1, source_target_pairs={{0,12},{2,14},{4,0},{6,2},{8,4},{10,6},{12,8},{14,10},{1,13},{3,15... | collective-permute-start | bytes 331784 | tf_op jit(solution)/shard_map/ppermute | solution.py:238
  37.1 7.8 %collective-permute-start.10 = (f32[27,8,128]{2,1,0:T(8,128)S(1)}, f32[27,8,128]{2,1,0:T(8,128)S(1)}, u32[]{:S(2)}, u32[]{:S(2)}) collective-permute-start(f32[27,8,128]{2,1,0:T(8,128)S(1)} %shard_map.61.refs_0_), channel_id=1, source_target_pairs={{0,4},{2,6},{4,8},{6,10},{8,12},{10,14},{12,0},{14,2},{1,5},{3,7},... | collective-permute-start | bytes 331784 | tf_op jit(solution)/shard_map/ppermute | solution.py:238
  37.1 7.8 %collective-permute-start.14 = (f32[27,8,128]{2,1,0:T(8,128)S(1)}, f32[27,8,128]{2,1,0:T(8,128)S(1)}, u32[]{:S(2)}, u32[]{:S(2)}) collective-permute-start(f32[27,8,128]{2,1,0:T(8,128)S(1)} %shard_map.61.refs_0_), channel_id=1, source_target_pairs={{0,2},{2,0},{4,6},{6,4},{8,10},{10,8},{12,14},{14,12},{1,3},{3,1},... | collective-permute-start | bytes 331784 | tf_op jit(solution)/shard_map/ppermute | solution.py:234
  40.4 7.8 %collective-permute-start.18 = (f32[27,8,128]{2,1,0:T(8,128)S(1)}, f32[27,8,128]{2,1,0:T(8,128)S(1)}, u32[]{:S(2)}, u32[]{:S(2)}) collective-permute-start(f32[27,8,128]{2,1,0:T(8,128)S(1)} %collective-permute-done.15.refs_2_), channel_id=1, source_target_pairs={{0,2},{2,0},{4,6},{6,4},{8,10},{10,8},{12,14},{14,12},{1,3},{3,1},... | collective-permute-start | bytes 331784 | tf_op jit(solution)/shard_map/ppermute | solution.py:234
  41.1 7.1 %collective-permute-start.19 = (f32[27,8,128]{2,1,0:T(8,128)S(1)}, f32[27,8,128]{2,1,0:T(8,128)S(1)}, u32[]{:S(2)}, u32[]{:S(2)}) collective-permute-start(f32[27,8,128]{2,1,0:T(8,128)S(1)} %collective-permute-done.16.refs_3_), channel_id=1, source_target_pairs={{0,2},{2,0},{4,6},{6,4},{8,10},{10,8},{12,14},{14,12},{1,3},{3,1},... | collective-permute-start | bytes 331784 | tf_op jit(solution)/shard_map/ppermute | solution.py:234
  44.9 4.7 %collective-permute-start.17 = (f32[27,8,128]{2,1,0:T(8,128)S(1)}, f32[27,8,128]{2,1,0:T(8,128)S(1)}, u32[]{:S(2)}, u32[]{:S(2)}) collective-permute-start(f32[27,8,128]{2,1,0:T(8,128)S(1)} %collective-permute-done.10.refs_1_), channel_id=1, source_target_pairs={{0,2},{2,0},{4,6},{6,4},{8,10},{10,8},{12,14},{14,12},{1,3},{3,1},... | collective-permute-start | bytes 331784 | tf_op jit(solution)/shard_map/ppermute | solution.py:234

commit v6 on v5

--- a/solution.py
+++ b/solution.py
@@ -163,9 +163,12 @@
         rows = slice(first * group, last * group)
         return dot3(g_hi[rows, :], g_lo[rows, :], hi, lo, NT)
 
-    sums[...] = acc[...] + term(0, 3, x_hi[0], x_lo[0]) + term(1, 4, x_hi[1], x_lo[1])
-    sums[2 * group :, :] += term(1, 2, x1_hi[...], x1_lo[...])
-    sums[:group, :] += term(2, 3, x_hi[2], x_lo[2])
+    inner = term(0, 3, x_hi[0], x_lo[0]) + term(1, 4, x_hi[1], x_lo[1])
+    first = term(2, 3, x_hi[2], x_lo[2])
+    last = term(1, 2, x1_hi[...], x1_lo[...])
+    sums[:group, :] = acc[:group, :] + inner[:group, :] + first
+    sums[group : 2 * group, :] = acc[group : 2 * group, :] + inner[group : 2 * group, :]
+    sums[2 * group :, :] = acc[2 * group :, :] + inner[2 * group :, :] + last
     acc = sums
 
     full = 2 * half

time: 51.8 us -> 51.8 us (level)
  no operation moved by 1% of the time
where the time goes in v6:
time: 51.8 us; the launch traced here: 51.3 us
  starting transfers between devices  25.1 us (48%)
  waiting for transfers between devices  11.8 us (23%)
  Pallas kernels  9.67 us (19%)
  local copies, waits for them, and re-layouts  3.14 us (6%)
  between operations  0.82 us (2%)
  other arithmetic  0.79 us (2%)
    ppermute x7, starting transfers between devices, swap_side(): return lax.ppermute(value, 'space', [(i, i ^ 1) for i in range(ring)])  12.4 us
    ppermute x6, starting transfers between devices, shift(): return lax.ppermute(value, 'space', pairs)  10.8 us
    ppermute x6, waiting for transfers between devices, shift(): return lax.ppermute(value, 'space', pairs)  6.94 us
    ppermute x7, waiting for transfers between devices, swap_side(): return lax.ppermute(value, 'space', [(i, i ^ 1) for i in range(ring)])  4.68 us
    pallas_call x2, Pallas kernels, conv(): call(lambda *refs: conv_kernel(places, *refs), jax.ShapeDtypeStruct((2, 2...  3.64 us
    unnamed x5, local copies, waits for them, and re-layouts  3.08 us
    pallas_call x1, Pallas kernels, local(): call(filter_kernel, [chunk] * count, 11, [pltpu.VMEM((3, 2 * full, width)...  1.58 us
    pallas_call x1, Pallas kernels, local(): call(join_kernel, jax.ShapeDtypeStruct((27, half // 8, 8, full), F32), 2...  1.57 us
  transfers between devices with their start and end apart: 20, of which 6 were waited for; matrix products, arithmetic and copies ran while one was open for 5% of the time, Pallas kernels for 16%

profile of v6, /device:TPU:0, one launch (start us, length us, event | category | flops | bytes accessed | tf_op | source)
XLA Modules:
  0.0 51.3 jit_solution(14063483571952206350)
XLA Ops:
  0.6 1.3 %fusion = (f32[64,2,2,256]{3,0,2,1:T(8,128)S(1)}, f32[2,2,64,256]{3,2,1,0:T(8,128)S(1)}, f32[2,2,64,256]{3,2,1,0:T(8,128)S(1)}) fusion(f32[64,2,2,256]{3,2,1,0:T(2,128)} %param.3, f32[64,2,2,256]{3,2,1,0:T(2,128)} %param.5), kind=kLoop, calls=%fused_computation.9 | loop fusion | bytes 1310720 | tf_op args[0]
  1.9 3.0 %collective-permute-start.1 = (f32[2,2,64,256]{3,2,1,0:T(8,128)S(1)}, f32[2,2,64,256]{3,2,1,0:T(8,128)S(1)}, u32[]{:S(2)}, u32[]{:S(2)}) collective-permute-start(f32[2,2,64,256]{3,2,1,0:T(8,128)S(1)} %get-tuple-element.34.own.refs_1_), channel_id=1, source_target_pairs={{0,2},{2,0},{4,6},{6,4},{8,10},{10,8},{12,14},{14,12},{1,3},{3,1},... | collective-permute-start | bytes 786440 | tf_op jit(solution)/shard_map/ppermute | solution.py:237
  5.0 1.3 %collective-permute-start.3 = (f32[2,2,64,256]{3,2,1,0:T(8,128)S(1)}, f32[2,2,64,256]{3,2,1,0:T(8,128)S(1)}, u32[]{:S(2)}, u32[]{:S(2)}) collective-permute-start(f32[2,2,64,256]{3,2,1,0:T(8,128)S(1)} %pad_maximum_fusion), channel_id=1, source_target_pairs={{2,6},{4,0},{6,10},{8,4},{10,14},{12,8},{3,7},{5,1},{7,11},{9,5},{... | collective-permute-start | bytes 786440 | tf_op jit(solution)/shard_map/ppermute | solution.py:250
  7.1 2.7 %collective-permute-start.4 = (f32[3,2,32,256]{3,2,1,0:T(8,128)}, f32[3,2,32,256]{3,2,1,0:T(8,128)S(1)}, u32[]{:S(2)}, u32[]{:S(2)}) collective-permute-start(f32[3,2,32,256]{3,2,1,0:T(8,128)} %pad_maximum_fusion.1), channel_id=1, source_target_pairs={{0,2},{2,0},{4,6},{6,4},{8,10},{10,8},{12,14},{14,12},{1,3},{3,1},... | collective-permute-start | bytes 589832 | tf_op jit(solution)/shard_map/ppermute | solution.py:237
  9.9 1.2 %shard_map.58 = (bf16[3,384,256]{2,1,0:T(8,128)(2,1)S(1)}, bf16[3,384,256]{2,1,0:T(8,128)(2,1)S(1)}, bf16[3,384,256]{2,1,0:T(8,128)(2,1)S(1)}, bf16[3,384,256]{2,1,0:T(8,128)(2,1)S(1)}, f32[8,128]{1,0:T(8,128)S(1)}) custom-call(s32[3]{0:T(128)S(1)} %pad_add_fusion.at.refs_0_, f32[27,128,128]{2,1,0:T(8,128)S(1)} %bitcast.15), custom_call_target="tpu_custom_call" | custom-call | tf_op jit(solution)/shard_map/pallas_call | solution.py:269
  11.1 1.1 %shard_map.59 = (f32[576,256]{1,0:T(8,128)S(1)}, bf16[256,256]{1,0:T(8,128)(2,1)S(1)}, bf16[256,256]{1,0:T(8,128)(2,1)S(1)}, bf16[192,256]{1,0:T(8,128)(2,1)S(1)...) custom-call(s32[3]{0:T(128)S(1)} %pad_add_fusion.at.refs_0_, f32[2,2,64,256]{3,2,1,0:T(8,128)S(1)} %get-tuple-element.34.own.refs_1_, ...), custom_call_target="tpu_custom_call" | custom-call | tf_op jit(solution)/shard_map/pallas_call | solution.py:278
  12.3 3.2 %collective-permute-done.4.g_pair.refs_5_ = f32[3,2,32,256]{3,2,1,0:T(8,128)S(1)} collective-permute-done((f32[3,2,32,256]{3,2,1,0:T(8,128)}, f32[3,2,32,256]{3,2,1,0:T(8,128)S(1)}, u32[]{:S(2)}, u32[]{:S(2)}) %collective-permute-start.4) | collective-permute-done | bytes 196640 | tf_op jit(solution)/shard_map/ppermute | solution.py:237
  15.6 1.6 %collective-permute-start.9 = (f32[2,2,64,256]{3,2,1,0:T(8,128)S(1)}, f32[2,2,64,256]{3,2,1,0:T(8,128)S(1)}, u32[]{:S(2)}, u32[]{:S(2)}) collective-permute-start(f32[2,2,64,256]{3,2,1,0:T(8,128)S(1)} %collective-permute-done.3.edge), channel_id=1, source_target_pairs={{0,2},{2,0},{4,6},{6,4},{8,10},{10,8},{12,14},{14,12},{1,3},{3,1},... | collective-permute-start | bytes 786440 | tf_op jit(solution)/shard_map/ppermute | solution.py:237
  17.2 1.6 %shard_map.60 = (f32[27,8,128]{2,1,0:T(8,128)S(1)}, f32[27,8,128]{2,1,0:T(8,128)S(1)}, f32[27,8,128]{2,1,0:T(8,128)S(1)}, f32[27,8,128]{2,1,0:T(8,128)S(1)}) custom-call(s32[3]{0:T(128)S(1)} %pad_add_fusion.at.refs_0_, f32[576,256]{1,0:T(8,128)S(1)} %get-tuple-element.37.acc, bf16[256,256]{1,0:T(8,128)(2,1)S(1)} %get-tuple-element.38.x1_hi, ...), custom_call_target="tpu_custom_call" | custom-call | tf_op jit(solution)/shard_map/pallas_call | solution.py:295
  18.8 1.6 %collective-permute-start.6 = (f32[27,8,128]{2,1,0:T(8,128)S(1)}, f32[27,8,128]{2,1,0:T(8,128)S(1)}, u32[]{:S(2)}, u32[]{:S(2)}) collective-permute-start(f32[27,8,128]{2,1,0:T(8,128)S(1)} %get-tuple-element.47), channel_id=1, source_target_pairs={{0,4},{2,6},{4,8},{6,10},{8,12},{10,14},{12,0},{14,2},{1,5},{3,7},... | collective-permute-start | bytes 331784 | tf_op jit(solution)/shard_map/ppermute | solution.py:241
  20.4 2.6 %collective-permute-start.7 = (f32[27,8,128]{2,1,0:T(8,128)S(1)}, f32[27,8,128]{2,1,0:T(8,128)S(1)}, u32[]{:S(2)}, u32[]{:S(2)}) collective-permute-start(f32[27,8,128]{2,1,0:T(8,128)S(1)} %get-tuple-element.48), channel_id=1, source_target_pairs={{0,8},{2,10},{4,12},{6,14},{8,0},{10,2},{12,4},{14,6},{1,9},{3,11}... | collective-permute-start | bytes 331784 | tf_op jit(solution)/shard_map/ppermute | solution.py:241
  23.0 1.3 %collective-permute-start.8 = (f32[27,8,128]{2,1,0:T(8,128)S(1)}, f32[27,8,128]{2,1,0:T(8,128)S(1)}, u32[]{:S(2)}, u32[]{:S(2)}) collective-permute-start(f32[27,8,128]{2,1,0:T(8,128)S(1)} %get-tuple-element.49), channel_id=1, source_target_pairs={{0,12},{2,14},{4,0},{6,2},{8,4},{10,6},{12,8},{14,10},{1,13},{3,15... | collective-permute-start | bytes 331784 | tf_op jit(solution)/shard_map/ppermute | solution.py:241
  24.4 2.2 %collective-permute-done.6.refs_2_ = f32[27,8,128]{2,1,0:T(8,128)S(1)} collective-permute-done((f32[27,8,128]{2,1,0:T(8,128)S(1)}, f32[27,8,128]{2,1,0:T(8,128)S(1)}, u32[]{:S(2)}, u32[]{:S(2)}) %collective-permute-start.6) | collective-permute-done | bytes 110624 | tf_op jit(solution)/shard_map/ppermute | solution.py:241
  26.6 4.1 %collective-permute-done.7.refs_3_ = f32[27,8,128]{2,1,0:T(8,128)S(1)} collective-permute-done((f32[27,8,128]{2,1,0:T(8,128)S(1)}, f32[27,8,128]{2,1,0:T(8,128)S(1)}, u32[]{:S(2)}, u32[]{:S(2)}) %collective-permute-start.7) | collective-permute-done | bytes 110624 | tf_op jit(solution)/shard_map/ppermute | solution.py:241
  31.9 1.8 %collective-permute-start.15 = (f32[27,8,128]{2,1,0:T(8,128)S(1)}, f32[27,8,128]{2,1,0:T(8,128)S(1)}, u32[]{:S(2)}, u32[]{:S(2)}) collective-permute-start(f32[27,8,128]{2,1,0:T(8,128)S(1)} %shard_map.61.refs_0_), channel_id=1, source_target_pairs={{0,8},{2,10},{4,12},{6,14},{8,0},{10,2},{12,4},{14,6},{1,9},{3,11}... | collective-permute-start | bytes 331784 | tf_op jit(solution)/shard_map/ppermute | solution.py:241
  33.7 3.4 %collective-permute-start.16 = (f32[27,8,128]{2,1,0:T(8,128)S(1)}, f32[27,8,128]{2,1,0:T(8,128)S(1)}, u32[]{:S(2)}, u32[]{:S(2)}) collective-permute-start(f32[27,8,128]{2,1,0:T(8,128)S(1)} %shard_map.61.refs_0_), channel_id=1, source_target_pairs={{0,12},{2,14},{4,0},{6,2},{8,4},{10,6},{12,8},{14,10},{1,13},{3,15... | collective-permute-start | bytes 331784 | tf_op jit(solution)/shard_map/ppermute | solution.py:241
  37.1 1.5 %collective-permute-start.14 = (f32[27,8,128]{2,1,0:T(8,128)S(1)}, f32[27,8,128]{2,1,0:T(8,128)S(1)}, u32[]{:S(2)}, u32[]{:S(2)}) collective-permute-start(f32[27,8,128]{2,1,0:T(8,128)S(1)} %shard_map.61.refs_0_), channel_id=1, source_target_pairs={{0,2},{2,0},{4,6},{6,4},{8,10},{10,8},{12,14},{14,12},{1,3},{3,1},... | collective-permute-start | bytes 331784 | tf_op jit(solution)/shard_map/ppermute | solution.py:237
  38.6 1.8 %shard_map.62 = f32[2,2,64,256]{3,2,1,0:T(8,128)S(1)} custom-call(s32[3]{0:T(128)S(1)} %pad_add_fusion.at.refs_0_, f32[2,2,64,256]{3,2,1,0:T(8,128)S(1)} %get-tuple-element.34.own.refs_1_, f32[2,2,64,256]{3,2,1,0:T(8,128)S(1)} %collective-permute-done.own2.refs_2_, f32[2,2,64,256]{3,2,1,0:T(8,128)S(1)} %collective-permute-done.1.pair.refs_3_, ...), custom_call_target="tpu_custom_call" | custom-call | tf_op jit(solution)/shard_map/pallas_call | solution.py:310
  41.1 1.4 %collective-permute-start.19 = (f32[27,8,128]{2,1,0:T(8,128)S(1)}, f32[27,8,128]{2,1,0:T(8,128)S(1)}, u32[]{:S(2)}, u32[]{:S(2)}) collective-permute-start(f32[27,8,128]{2,1,0:T(8,128)S(1)} %collective-permute-done.16.refs_3_), channel_id=1, source_target_pairs={{0,2},{2,0},{4,6},{6,4},{8,10},{10,8},{12,14},{14,12},{1,3},{3,1},... | collective-permute-start | bytes 331784 | tf_op jit(solution)/shard_map/ppermute | solution.py:237
  42.5 1.8 %shard_map.63 = f32[2,2,64,256]{3,2,1,0:T(8,128)S(1)} custom-call(s32[3]{0:T(128)S(1)} %pad_add_fusion.at.refs_0_, f32[2,2,64,256]{3,2,1,0:T(8,128)S(1)} %get-tuple-element.35.g_own.refs_1_, f32[2,2,64,256]{3,2,1,0:T(8,128)S(1)} %collective-permute-done.12.refs_2_, f32[2,2,64,256]{3,2,1,0:T(8,128)S(1)} %collective-permute-done.9.refs_5_.refs_3_, ...), custom_call_target="tpu_custom_call" | custom-call | tf_op jit(solution)/shard_map/pallas_call | solution.py:310
  45.0 1.4 %collective-permute-start.17 = (f32[27,8,128]{2,1,0:T(8,128)S(1)}, f32[27,8,128]{2,1,0:T(8,128)S(1)}, u32[]{:S(2)}, u32[]{:S(2)}) collective-permute-start(f32[27,8,128]{2,1,0:T(8,128)S(1)} %collective-permute-done.10.refs_1_), channel_id=1, source_target_pairs={{0,2},{2,0},{4,6},{6,4},{8,10},{10,8},{12,14},{14,12},{1,3},{3,1},... | collective-permute-start | bytes 331784 | tf_op jit(solution)/shard_map/ppermute | solution.py:237
  46.4 0.9 %copy.10 = f32[64,2,2,256]{3,2,1,0:T(2,128)} copy(f32[64,2,2,256]{3,0,2,1:T(8,128)S(1)} %bitcast.17) | data formatting | bytes 524288
  48.2 1.5 %collective-permute-done.17.refs_5_ = f32[27,8,128]{2,1,0:T(8,128)S(1)} collective-permute-done((f32[27,8,128]{2,1,0:T(8,128)S(1)}, f32[27,8,128]{2,1,0:T(8,128)S(1)}, u32[]{:S(2)}, u32[]{:S(2)}) %collective-permute-start.17) | collective-permute-done | bytes 110624 | tf_op jit(solution)/shard_map/ppermute | solution.py:237
  49.7 1.6 %shard_map.64 = f32[27,8,8,128]{3,2,1,0:T(8,128)} custom-call(s32[3]{0:T(128)S(1)} %pad_add_fusion.at.refs_0_, f32[27,8,128]{2,1,0:T(8,128)S(1)} %shard_map.61.refs_0_, f32[27,8,128]{2,1,0:T(8,128)S(1)} %collective-permute-done.10.refs_1_, f32[27,8,128]{2,1,0:T(8,128)S(1)} %collective-permute-done.15.refs_2_, ...), custom_call_target="tpu_custom_call" | custom-call | tf_op jit(solution)/shard_map/pallas_call | solution.py:355
  (35 shorter events, 4.4 us)
Async XLA Ops:
  0.6 9.2 %copy-start = (f32[128,27,128]{2,0,1:T(8,128)S(1)}, f32[128,27,128]{2,0,1:T(8,128)}, u32[]{:S(2)}) copy-start(f32[128,27,128]{2,0,1:T(8,128)} %param.4) | copy-start | bytes 5308420
  1.9 10.3 %collective-permute-start.1 = (f32[2,2,64,256]{3,2,1,0:T(8,128)S(1)}, f32[2,2,64,256]{3,2,1,0:T(8,128)S(1)}, u32[]{:S(2)}, u32[]{:S(2)}) collective-permute-start(f32[2,2,64,256]{3,2,1,0:T(8,128)S(1)} %get-tuple-element.34.own.refs_1_), channel_id=1, source_target_pairs={{0,2},{2,0},{4,6},{6,4},{8,10},{10,8},{12,14},{14,12},{1,3},{3,1},... | collective-permute-start | bytes 786440 | tf_op jit(solution)/shard_map/ppermute | solution.py:237
  4.9 6.1 %collective-permute-start = (f32[2,2,64,256]{3,2,1,0:T(8,128)S(1)}, f32[2,2,64,256]{3,2,1,0:T(8,128)S(1)}, u32[]{:S(2)}, u32[]{:S(2)}) collective-permute-start(f32[2,2,64,256]{3,2,1,0:T(8,128)S(1)} %get-tuple-element.34.own.refs_1_), channel_id=1, source_target_pairs={{0,1},{1,0},{2,3},{3,2},{4,5},{5,4},{6,7},{7,6},{8,9},{9,8},{10,11... | collective-permute-start | bytes 786440 | tf_op jit(solution)/shard_map/ppermute | solution.py:234
  5.0 10.6 %collective-permute-start.3 = (f32[2,2,64,256]{3,2,1,0:T(8,128)S(1)}, f32[2,2,64,256]{3,2,1,0:T(8,128)S(1)}, u32[]{:S(2)}, u32[]{:S(2)}) collective-permute-start(f32[2,2,64,256]{3,2,1,0:T(8,128)S(1)} %pad_maximum_fusion), channel_id=1, source_target_pairs={{2,6},{4,0},{6,10},{8,4},{10,14},{12,8},{3,7},{5,1},{7,11},{9,5},{... | collective-permute-start | bytes 786440 | tf_op jit(solution)/shard_map/ppermute | solution.py:250
  7.1 8.4 %collective-permute-start.4 = (f32[3,2,32,256]{3,2,1,0:T(8,128)}, f32[3,2,32,256]{3,2,1,0:T(8,128)S(1)}, u32[]{:S(2)}, u32[]{:S(2)}) collective-permute-start(f32[3,2,32,256]{3,2,1,0:T(8,128)} %pad_maximum_fusion.1), channel_id=1, source_target_pairs={{0,2},{2,0},{4,6},{6,4},{8,10},{10,8},{12,14},{14,12},{1,3},{3,1},... | collective-permute-start | bytes 589832 | tf_op jit(solution)/shard_map/ppermute | solution.py:237
  12.2 5.0 %collective-permute-start.2 = (f32[2,2,64,256]{3,2,1,0:T(8,128)S(1)}, f32[2,2,64,256]{3,2,1,0:T(8,128)S(1)}, u32[]{:S(2)}, u32[]{:S(2)}) collective-permute-start(f32[2,2,64,256]{3,2,1,0:T(8,128)S(1)} %collective-permute-done.1.pair.refs_3_), channel_id=1, source_target_pairs={{0,1},{1,0},{2,3},{3,2},{4,5},{5,4},{6,7},{7,6},{8,9},{9,8},{10,11... | collective-permute-start | bytes 786440 | tf_op jit(solution)/shard_map/ppermute | solution.py:234
  15.6 1.6 %collective-permute-start.5 = (f32[2,2,64,256]{3,2,1,0:T(8,128)S(1)}, f32[2,2,64,256]{3,2,1,0:T(8,128)S(1)}, u32[]{:S(2)}, u32[]{:S(2)}) collective-permute-start(f32[2,2,64,256]{3,2,1,0:T(8,128)S(1)} %collective-permute-done.3.edge), channel_id=1, source_target_pairs={{0,1},{1,0},{2,3},{3,2},{4,5},{5,4},{6,7},{7,6},{8,9},{9,8},{10,11... | collective-permute-start | bytes 786440 | tf_op jit(solution)/shard_map/ppermute | solution.py:234
  15.6 8.8 %collective-permute-start.9 = (f32[2,2,64,256]{3,2,1,0:T(8,128)S(1)}, f32[2,2,64,256]{3,2,1,0:T(8,128)S(1)}, u32[]{:S(2)}, u32[]{:S(2)}) collective-permute-start(f32[2,2,64,256]{3,2,1,0:T(8,128)S(1)} %collective-permute-done.3.edge), channel_id=1, source_target_pairs={{0,2},{2,0},{4,6},{6,4},{8,10},{10,8},{12,14},{14,12},{1,3},{3,1},... | collective-permute-start | bytes 786440 | tf_op jit(solution)/shard_map/ppermute | solution.py:237
  18.8 7.8 %collective-permute-start.6 = (f32[27,8,128]{2,1,0:T(8,128)S(1)}, f32[27,8,128]{2,1,0:T(8,128)S(1)}, u32[]{:S(2)}, u32[]{:S(2)}) collective-permute-start(f32[27,8,128]{2,1,0:T(8,128)S(1)} %get-tuple-element.47), channel_id=1, source_target_pairs={{0,4},{2,6},{4,8},{6,10},{8,12},{10,14},{12,0},{14,2},{1,5},{3,7},... | collective-permute-start | bytes 331784 | tf_op jit(solution)/shard_map/ppermute | solution.py:241
  20.4 10.3 %collective-permute-start.7 = (f32[27,8,128]{2,1,0:T(8,128)S(1)}, f32[27,8,128]{2,1,0:T(8,128)S(1)}, u32[]{:S(2)}, u32[]{:S(2)}) collective-permute-start(f32[27,8,128]{2,1,0:T(8,128)S(1)} %get-tuple-element.48), channel_id=1, source_target_pairs={{0,8},{2,10},{4,12},{6,14},{8,0},{10,2},{12,4},{14,6},{1,9},{3,11}... | collective-permute-start | bytes 331784 | tf_op jit(solution)/shard_map/ppermute | solution.py:241
  23.0 7.7 %collective-permute-start.8 = (f32[27,8,128]{2,1,0:T(8,128)S(1)}, f32[27,8,128]{2,1,0:T(8,128)S(1)}, u32[]{:S(2)}, u32[]{:S(2)}) collective-permute-start(f32[27,8,128]{2,1,0:T(8,128)S(1)} %get-tuple-element.49), channel_id=1, source_target_pairs={{0,12},{2,14},{4,0},{6,2},{8,4},{10,6},{12,8},{14,10},{1,13},{3,15... | collective-permute-start | bytes 331784 | tf_op jit(solution)/shard_map/ppermute | solution.py:241
  24.4 12.7 %collective-permute-start.12 = (f32[2,2,64,256]{3,2,1,0:T(8,128)S(1)}, f32[2,2,64,256]{3,2,1,0:T(8,128)S(1)}, u32[]{:S(2)}, u32[]{:S(2)}) collective-permute-start(f32[2,2,64,256]{3,2,1,0:T(8,128)S(1)} %get-tuple-element.35.g_own.refs_1_), channel_id=1, source_target_pairs={{0,1},{1,0},{2,3},{3,2},{4,5},{5,4},{6,7},{7,6},{8,9},{9,8},{10,11... | collective-permute-start | bytes 786440 | tf_op jit(solution)/shard_map/ppermute | solution.py:234
  30.7 6.4 %collective-permute-start.11 = (f32[2,2,64,256]{3,2,1,0:T(8,128)S(1)}, f32[2,2,64,256]{3,2,1,0:T(8,128)S(1)}, u32[]{:S(2)}, u32[]{:S(2)}) collective-permute-start(f32[2,2,64,256]{3,2,1,0:T(8,128)S(1)} %collective-permute-done.9.refs_5_.refs_3_), channel_id=1, source_target_pairs={{0,1},{1,0},{2,3},{3,2},{4,5},{5,4},{6,7},{7,6},{8,9},{9,8},{10,11... | collective-permute-start | bytes 786440 | tf_op jit(solution)/shard_map/ppermute | solution.py:234
  31.3 11.2 %collective-permute-start.13 = (f32[3,2,32,256]{3,2,1,0:T(8,128)S(1)}, f32[3,2,32,256]{3,2,1,0:T(8,128)S(1)}, u32[]{:S(2)}, u32[]{:S(2)}) collective-permute-start(f32[3,2,32,256]{3,2,1,0:T(8,128)S(1)} %collective-permute-done.4.g_pair.refs_5_), channel_id=1, source_target_pairs={{0,1},{1,0},{2,3},{3,2},{4,5},{5,4},{6,7},{7,6},{8,9},{9,8},{10,11... | collective-permute-start | bytes 589832 | tf_op jit(solution)/shard_map/ppermute | solution.py:234
  31.9 8.5 %collective-permute-start.15 = (f32[27,8,128]{2,1,0:T(8,128)S(1)}, f32[27,8,128]{2,1,0:T(8,128)S(1)}, u32[]{:S(2)}, u32[]{:S(2)}) collective-permute-start(f32[27,8,128]{2,1,0:T(8,128)S(1)} %shard_map.61.refs_0_), channel_id=1, source_target_pairs={{0,8},{2,10},{4,12},{6,14},{8,0},{10,2},{12,4},{14,6},{1,9},{3,11}... | collective-permute-start | bytes 331784 | tf_op jit(solution)/shard_map/ppermute | solution.py:241
  33.7 7.4 %collective-permute-start.16 = (f32[27,8,128]{2,1,0:T(8,128)S(1)}, f32[27,8,128]{2,1,0:T(8,128)S(1)}, u32[]{:S(2)}, u32[]{:S(2)}) collective-permute-start(f32[27,8,128]{2,1,0:T(8,128)S(1)} %shard_map.61.refs_0_), channel_id=1, source_target_pairs={{0,12},{2,14},{4,0},{6,2},{8,4},{10,6},{12,8},{14,10},{1,13},{3,15... | collective-permute-start | bytes 331784 | tf_op jit(solution)/shard_map/ppermute | solution.py:241
  37.1 7.8 %collective-permute-start.10 = (f32[27,8,128]{2,1,0:T(8,128)S(1)}, f32[27,8,128]{2,1,0:T(8,128)S(1)}, u32[]{:S(2)}, u32[]{:S(2)}) collective-permute-start(f32[27,8,128]{2,1,0:T(8,128)S(1)} %shard_map.61.refs_0_), channel_id=1, source_target_pairs={{0,4},{2,6},{4,8},{6,10},{8,12},{10,14},{12,0},{14,2},{1,5},{3,7},... | collective-permute-start | bytes 331784 | tf_op jit(solution)/shard_map/ppermute | solution.py:241
  37.1 7.8 %collective-permute-start.14 = (f32[27,8,128]{2,1,0:T(8,128)S(1)}, f32[27,8,128]{2,1,0:T(8,128)S(1)}, u32[]{:S(2)}, u32[]{:S(2)}) collective-permute-start(f32[27,8,128]{2,1,0:T(8,128)S(1)} %shard_map.61.refs_0_), channel_id=1, source_target_pairs={{0,2},{2,0},{4,6},{6,4},{8,10},{10,8},{12,14},{14,12},{1,3},{3,1},... | collective-permute-start | bytes 331784 | tf_op jit(solution)/shard_map/ppermute | solution.py:237
  40.4 7.8 %collective-permute-start.18 = (f32[27,8,128]{2,1,0:T(8,128)S(1)}, f32[27,8,128]{2,1,0:T(8,128)S(1)}, u32[]{:S(2)}, u32[]{:S(2)}) collective-permute-start(f32[27,8,128]{2,1,0:T(8,128)S(1)} %collective-permute-done.15.refs_2_), channel_id=1, source_target_pairs={{0,2},{2,0},{4,6},{6,4},{8,10},{10,8},{12,14},{14,12},{1,3},{3,1},... | collective-permute-start | bytes 331784 | tf_op jit(solution)/shard_map/ppermute | solution.py:237
  41.1 7.1 %collective-permute-start.19 = (f32[27,8,128]{2,1,0:T(8,128)S(1)}, f32[27,8,128]{2,1,0:T(8,128)S(1)}, u32[]{:S(2)}, u32[]{:S(2)}) collective-permute-start(f32[27,8,128]{2,1,0:T(8,128)S(1)} %collective-permute-done.16.refs_3_), channel_id=1, source_target_pairs={{0,2},{2,0},{4,6},{6,4},{8,10},{10,8},{12,14},{14,12},{1,3},{3,1},... | collective-permute-start | bytes 331784 | tf_op jit(solution)/shard_map/ppermute | solution.py:237
  45.0 4.7 %collective-permute-start.17 = (f32[27,8,128]{2,1,0:T(8,128)S(1)}, f32[27,8,128]{2,1,0:T(8,128)S(1)}, u32[]{:S(2)}, u32[]{:S(2)}) collective-permute-start(f32[27,8,128]{2,1,0:T(8,128)S(1)} %collective-permute-done.10.refs_1_), channel_id=1, source_target_pairs={{0,2},{2,0},{4,6},{6,4},{8,10},{10,8},{12,14},{14,12},{1,3},{3,1},... | collective-permute-start | bytes 331784 | tf_op jit(solution)/shard_map/ppermute | solution.py:237
